TPU v7x, 32 devices: a whole 2x2x4 slice. The times are simulated.
32 devices in a mesh: gx: 4 (over y, core), gy: 8 (over z, x).
Axes of the slice: x: 2, y: 2, z: 4, core: 2. Of those that a mesh axis runs over, the one named last changes fastest.
Arguments:
- eps_field: bfloat16 [48, 256, 1024], P(None, 'gx', 'gy'), may hold values from 1 to 10
- charge: float32 [48, 256, 1024], P(None, 'gx', 'gy'), may hold values from -6 to 6
- potential_start: float32 [48, 256, 1024], P(None, 'gx', 'gy'), may hold values from -3 to 3
- colloid_vel: float32 [3, 1024], P(None, ('gx', 'gy')), may hold values from -0.3 to 0.3
- colloid_spin: float32 [3, 1024], P(None, ('gx', 'gy')), may hold values from -0.06 to 0.06
- link_dir: int32 [4, 8, 32768], P('gx', 'gy'), may hold values from 0 to 17
- link_colloid: int32 [4, 8, 32768], P('gx', 'gy'), may hold values from -1 to 1023, as said below
- link_site: int32 [4, 8, 32768], P('gx', 'gy'), may hold values from 0 to 8191
- link_depth: int32 [4, 8, 32768], P('gx', 'gy'), may hold values from 0 to 47
- link_pop: float32 [4, 8, 32768], P('gx', 'gy'), may hold values from -0.1 to 0.1
- link_rb: float32 [3, 4, 8, 32768], P(None, 'gx', 'gy'), may hold values from -9 to 9
Outputs:
- potential: float32 [48, 256, 1024], P(None, 'gx', 'gy')
- force_torque: float32 [6, 1024], P(None, ('gx', 'gy'))
- link_out: float32 [4, 8, 32768], P('gx', 'gy')
Inputs may be any that keep to these rules, and one draw needn't show every extreme that they name: `link_colloid`: an empty slot holds -1 and the live slots of a tile come first; at least 16384 slots of every tile are live and every slot of at least one tile. The tile with index i along gx and j along gy owns the colloids (i n + j) * 32 up to (i n + j + 1) * 32 - 1, where n is the number of tiles along gy; a live slot names a colloid owned by its own tile or by one of the eight tiles beside it, wrapping around.
All inputs are finite; a program needn't handle non-finite values.
Results may differ from a plain program's by a relative error of at most 0.0003.
Values may be sent and summed in bfloat16 or wider, within the bound.
No kernel may reach another device: no remote copies, remote signals or barrier semaphores. Data moves between devices by JAX's collectives and lax.ppermute only.
A program may use at most 128 MiB of HBM per device.

v0:
```python
import math

import jax
import jax.numpy as jnp
import numpy as np
from jax import lax
from jax.sharding import PartitionSpec as P

SWEEPS = 6
RADIUS = 8


velocity_table = np.array(
    [
        [1, 0, 0],
        [-1, 0, 0],
        [0, 1, 0],
        [0, -1, 0],
        [0, 0, 1],
        [0, 0, -1],
        [1, 1, 0],
        [1, -1, 0],
        [-1, 1, 0],
        [-1, -1, 0],
        [1, 0, 1],
        [1, 0, -1],
        [-1, 0, 1],
        [-1, 0, -1],
        [0, 1, 1],
        [0, 1, -1],
        [0, -1, 1],
        [0, -1, -1],
    ],
    dtype=np.float32,
).T
weight_table = np.array([1.0 / 18.0] * 6 + [1.0 / 36.0] * 12, dtype=np.float32)
OVER_RELAX = 1.6
BLOCK_LINKS = 8192


def padded_2(block, sides, width):
    for axis, dim in sides:
        count = lax.axis_size(axis)
        forward = [(i, i + 1) for i in range(count - 1)]
        forward.append((count - 1, 0))
        backward = [(target, source) for source, target in forward]
        low = lax.ppermute(
            lax.slice_in_dim(block, block.shape[dim] - width, None, axis=dim), axis, forward
        )
        high = lax.ppermute(lax.slice_in_dim(block, 0, width, axis=dim), axis, backward)
        block = jnp.concatenate([low, block, high], axis=dim)
    return block


def lattice_lookup(directions):
    onehot = (directions[None, :] == jnp.arange(18, dtype=jnp.int32)[:, None]).astype(jnp.float32)
    velocity = jnp.dot(
        jnp.asarray(velocity_table).astype(jnp.float32), onehot, precision=lax.Precision.HIGHEST
    )
    weight = jnp.dot(
        jnp.asarray(weight_table).astype(jnp.float32)[None, :],
        onehot,
        precision=lax.Precision.HIGHEST,
    )[0]
    return (velocity, weight)


def cross_product(first, second):
    return jnp.stack(
        [
            first[1] * second[2] - first[2] * second[1],
            first[2] * second[0] - first[0] * second[2],
            first[0] * second[1] - first[1] * second[0],
        ]
    )


def link_terms(pops, velocity, weight, valid, offsets, at_links, pressure):
    boundary = at_links[0:3] + cross_product(at_links[3:6], offsets)
    along = jnp.sum(velocity * boundary, axis=0)
    transfer = (2.0 * pops - 6.0 * weight * along + weight * pressure) * valid
    force = velocity * transfer[None, :]
    torque = cross_product(offsets, force)
    return jnp.concatenate([force, torque], axis=0)


def reflected(pops, velocity, weight, valid, offsets, at_links):
    boundary = at_links[0:3] + cross_product(at_links[3:6], offsets)
    along = jnp.sum(velocity * boundary, axis=0)
    return pops - 6.0 * weight * along * valid


def owner_update(motion, sums):
    mass = 4.0 / 3.0 * math.pi * RADIUS**3
    inertia = 0.4 * mass * RADIUS**2
    new_motion = jnp.concatenate(
        [motion[0:3] + sums[0:3] / mass, motion[3:6] + sums[3:6] / inertia], axis=0
    )
    report = jnp.concatenate([sums[0:3], sums[3:6] / RADIUS], axis=0)
    return (new_motion, report)


def relax_colour(phi_pad, eps_pad, charge, colour_mask):
    eps_slab = jnp.pad(eps_pad, ((1, 1), (0, 0), (0, 0)), mode="edge")
    padded = jnp.pad(phi_pad, ((1, 1), (0, 0), (0, 0)))
    eps_centre = eps_slab[1:-1, 1:-1, 1:-1]
    centre = padded[1:-1, 1:-1, 1:-1]
    eps_sides = [
        eps_slab[:-2, 1:-1, 1:-1],
        eps_slab[2:, 1:-1, 1:-1],
        eps_slab[1:-1, :-2, 1:-1],
        eps_slab[1:-1, 2:, 1:-1],
        eps_slab[1:-1, 1:-1, :-2],
        eps_slab[1:-1, 1:-1, 2:],
    ]
    phi_sides = [
        padded[:-2, 1:-1, 1:-1],
        padded[2:, 1:-1, 1:-1],
        padded[1:-1, :-2, 1:-1],
        padded[1:-1, 2:, 1:-1],
        padded[1:-1, 1:-1, :-2],
        padded[1:-1, 1:-1, 2:],
    ]
    numerator = charge
    denominator = jnp.zeros_like(charge)
    for eps_side, phi_side in zip(eps_sides, phi_sides):
        face = 0.5 * (eps_centre + eps_side)
        numerator = numerator + face * phi_side
        denominator = denominator + face
    target = numerator / denominator
    return jnp.where(colour_mask, centre + OVER_RELAX * (target - centre), centre)


def parity_of(shape):
    return (
        lax.broadcasted_iota(jnp.int32, shape, 0)
        + lax.broadcasted_iota(jnp.int32, shape, 1)
        + lax.broadcasted_iota(jnp.int32, shape, 2)
    ) % 2


def slot_table(slots, width):
    return (slots[None, :] == jnp.arange(width, dtype=jnp.int32)[:, None]).astype(jnp.float32)


def into_blocks(values, block_size):
    lead = values.shape[0]
    count = values.shape[1] // block_size
    return values.reshape(lead, count, block_size).transpose(1, 0, 2)


def near_sums(table_rows, slots, pops, velocity, weight, valid, offsets, pressure, block_size):
    width = table_rows.shape[0]
    table_cols = table_rows.T

    def add_block(total, inputs):
        slot_b, pops_b, vel_b, weight_b, valid_b, off_b, press_b = inputs
        onehot = slot_table(slot_b, width)
        at_links = jnp.dot(table_cols, onehot, precision=lax.Precision.HIGHEST)
        terms = link_terms(pops_b, vel_b, weight_b, valid_b, off_b, at_links, press_b)
        partial_value = lax.dot_general(
            terms, onehot, (((1,), (1,)), ((), ())), precision=lax.Precision.HIGHEST
        )
        return (total + partial_value, jnp.zeros((), jnp.float32))

    inputs = (
        slots.reshape(-1, block_size),
        pops.reshape(-1, block_size),
        into_blocks(velocity, block_size),
        weight.reshape(-1, block_size),
        valid.reshape(-1, block_size),
        into_blocks(offsets, block_size),
        pressure.reshape(-1, block_size),
    )
    total = lax.scan(add_block, jnp.zeros((6, width), jnp.float32), inputs)[0]
    return total.T


def near_reflect(table_rows, slots, pops, velocity, weight, valid, offsets, block_size):
    width = table_rows.shape[0]
    table_cols = table_rows.T

    def one_block(inputs):
        slot_b, pops_b, vel_b, weight_b, valid_b, off_b = inputs
        onehot = slot_table(slot_b, width)
        at_links = jnp.dot(table_cols, onehot, precision=lax.Precision.HIGHEST)
        return reflected(pops_b, vel_b, weight_b, valid_b, off_b, at_links)

    inputs = (
        slots.reshape(-1, block_size),
        pops.reshape(-1, block_size),
        into_blocks(velocity, block_size),
        weight.reshape(-1, block_size),
        valid.reshape(-1, block_size),
        into_blocks(offsets, block_size),
    )
    return lax.map(one_block, inputs).reshape(-1)


def shards(
    eps_field,
    charge,
    potential_start,
    colloid_vel,
    colloid_spin,
    link_dir,
    link_colloid,
    link_site,
    link_depth,
    link_pop,
    link_rb,
):
    potential = potential_start
    parity = parity_of(charge.shape)
    eps_wide = padded_2(eps_field, (("gx", 1), ("gy", 2)), 2).astype(jnp.float32)
    charge_wide = padded_2(charge, (("gx", 1), ("gy", 2)), 1)
    parity_wide = parity_of(charge_wide.shape)
    eps_inner = eps_wide[:, 1:-1, 1:-1]
    for sweep_index in range(SWEEPS):
        phi_wide = padded_2(potential, (("gx", 1), ("gy", 2)), 2)
        first_pass = relax_colour(phi_wide, eps_wide, charge_wide, parity_wide == 0)
        potential = relax_colour(first_pass, eps_inner, charge, parity == 1)
    per_tile = colloid_vel.shape[1]
    lateral = charge.shape[1] * charge.shape[2]
    motion = jnp.concatenate([colloid_vel, colloid_spin], axis=0)
    motion_rows = motion.T
    directions = link_dir.reshape(-1)
    colloid_ids = link_colloid.reshape(-1)
    sites = link_depth.reshape(-1) * lateral + link_site.reshape(-1)
    pops = link_pop.reshape(-1)
    offsets = link_rb.reshape(3, -1)
    link_count = pops.shape[0]
    block_size = min(link_count, BLOCK_LINKS)
    velocity, weight = lattice_lookup(directions)
    valid_mask = colloid_ids >= 0
    valid = valid_mask.astype(jnp.float32)
    phi_here = jnp.take(potential.reshape(-1), sites)
    pressure = (
        0.5 * jnp.take(eps_field.reshape(-1), sites).astype(jnp.float32) * phi_here * phi_here
    )
    count_x = lax.axis_size("gx")
    count_y = lax.axis_size("gy")
    home_x = lax.axis_index("gx")
    home_y = lax.axis_index("gy")
    owner_tile = colloid_ids // per_tile
    near_x = (owner_tile // count_y - home_x + 1) % count_x
    near_y = (owner_tile % count_y - home_y + 1) % count_y
    slots = jnp.where(valid_mask, (near_x * 3 + near_y) * per_tile + colloid_ids % per_tile, -1)
    beside_all = padded_2(motion_rows.reshape(1, 1, per_tile, 6), (("gx", 0), ("gy", 1)), 1)
    partial_value = near_sums(
        beside_all.reshape(9 * per_tile, 6),
        slots,
        pops,
        velocity,
        weight,
        valid,
        offsets,
        pressure,
        block_size,
    )
    blocks = partial_value.reshape(3, 3, per_tile, 6)
    framed = padded_2(blocks, (("gx", 0), ("gy", 1)), 1)
    sums_rows = (
        blocks[1, 1]
        + framed[0, 0]
        + framed[0, 2]
        + framed[0, 4]
        + framed[2, 0]
        + framed[2, 4]
        + framed[4, 0]
        + framed[4, 2]
        + framed[4, 4]
    )
    new_motion, report = owner_update(motion, sums_rows.T)
    around_new = padded_2(new_motion.T.reshape(1, 1, per_tile, 6), (("gx", 0), ("gy", 1)), 1)
    table_new = around_new.reshape(9 * per_tile, 6)
    link_out = near_reflect(
        table_new, slots, pops, velocity, weight, valid, offsets, block_size
    ).reshape(link_pop.shape)
    return (potential, report, link_out)


def solution(mesh):
    placed = (
        P(None, "gx", "gy"),
        P(None, "gx", "gy"),
        P(None, "gx", "gy"),
        P(None, ("gx", "gy")),
        P(None, ("gx", "gy")),
        P("gx", "gy", None),
        P("gx", "gy", None),
        P("gx", "gy", None),
        P("gx", "gy", None),
        P("gx", "gy", None),
        P(None, "gx", "gy", None),
    )
    return jax.shard_map(
        shards,
        mesh=mesh,
        in_specs=placed,
        out_specs=(P(None, "gx", "gy"), P(None, ("gx", "gy")), P("gx", "gy", None)),
        check_vma=False,
    )
```

profile of v0, /device:TPU:1, one launch (start us, length us, event | category | flops | bytes accessed | tf_op | source)
XLA Modules:
  0.0 813.7 jit_solution(3490610900580527088)
XLA Ops:
  56.0 4.7 slice.912
  69.1 23.4 %add_select_fusion.5 = (f32[48,66,130]{2,1,0:T(8,128)}, f32[48,66,130]{2,1,0:T(8,128)}, f32[48,66,130]{2,1,0:T(8,128)}, f32[48,66,130]{2,1,0:T(8,128)}, f32[48,6...) fusion(f32[48,68,2]{2,1,0:T(8,128)S(1)} %copy-done.32, ...), kind=kLoop, calls=%fused_computation.52 | loop fusion | flops 24710400 | bytes 55573248 | tf_op jit(solution)/shard_map/jit(_where)/select_n | solution.py:131
  92.5 27.9 %add_select_fusion.12 = (f32[48,64,128]{2,1,0:T(8,128)}, f32[48,64,128]{2,1,0:T(8,128)}, f32[48,64,128]{2,1,0:T(8,128)}, f32[48,64,128]{2,1,0:T(8,128)}, f32[48,...) fusion(f32[48,66,130]{2,1,0:T(8,128)} %get-tuple-element.242, f32[48,64,128]{2,1,0:T(8,128)S(1)} %copy-done.14, ...), kind=kLoop, calls=%fused_computation.232 | loop fusion | flops 19660800 | bytes 35458080 | tf_op jit(solution)/shard_map/jit(_where)/select_n | solution.py:131
  135.5 4.4 collective-permute-start.15
  150.2 12.4 %add_select_fusion.4 = f32[48,66,130]{2,1,0:T(8,128)S(1)} fusion(f32[48,66,130]{2,1,0:T(8,128)} %get-tuple-element.249, f32[48,66,130]{2,1,0:T(8,128)} %get-tuple-element.248, f32[48,68,2]{2,1,0:T(8,128)} %copy.65, f32[48,2,128]{2,1,0:T(2,128)S(1)} %collective-permute-done.13, f32[48,64,128]{2,1,0:T(8,128)} %get-tuple-element.235, ...), kind=kLoop, calls=%fused_computation.51 | loop fusion | flops 17297280 | bytes 32841216 | tf_op jit(solution)/shard_map/jit(_where)/select_n | solution.py:131
  162.6 5.7 add_select_fusion.11
  181.8 4.6 collective-permute-start.19
  196.2 12.4 %add_select_fusion.3 = f32[48,66,130]{2,1,0:T(8,128)S(1)} fusion(f32[48,66,130]{2,1,0:T(8,128)} %get-tuple-element.249, f32[48,66,130]{2,1,0:T(8,128)} %get-tuple-element.248, f32[48,68,2]{2,1,0:T(8,128)} %copy.71, f32[48,2,128]{2,1,0:T(2,128)S(1)} %collective-permute-done.17, f32[48,64,128]{2,1,0:T(8,128)} %copy-done.29, ...), kind=kLoop, calls=%fused_computation.50 | loop fusion | flops 17297280 | bytes 32841216 | tf_op jit(solution)/shard_map/jit(_where)/select_n | solution.py:131
  208.7 5.7 add_select_fusion.10
  225.5 4.4 collective-permute-start.23
  240.2 12.4 %add_select_fusion.2 = f32[48,66,130]{2,1,0:T(8,128)S(1)} fusion(f32[48,66,130]{2,1,0:T(8,128)} %get-tuple-element.249, f32[48,66,130]{2,1,0:T(8,128)} %get-tuple-element.248, f32[48,68,2]{2,1,0:T(8,128)} %copy.77, f32[48,2,128]{2,1,0:T(2,128)S(1)} %collective-permute-done.21, f32[48,64,128]{2,1,0:T(8,128)} %copy-done.30, ...), kind=kLoop, calls=%fused_computation.49 | loop fusion | flops 17297280 | bytes 32841216 | tf_op jit(solution)/shard_map/jit(_where)/select_n | solution.py:131
  252.6 5.7 add_select_fusion.9
  267.9 4.4 collective-permute-start.27
  272.7 201.3 %gather_fusion = bf16[32768]{0:T(1024)(128)(2,1)S(1)} fusion(bf16[393216]{0:T(1024)(128)(2,1)S(1)} %bitcast.143, s32[32768]{0:T(1024)S(1)} %broadcast_clamp_fusion), kind=kCustom, calls=%fused_computation | custom fusion | bytes 262144 | tf_op jit(solution)/shard_map/jit(_take)/gather | solution.py:239
  484.7 4.3 pad_maximum_fusion.43
  489.3 12.7 %add_select_fusion.1 = f32[48,66,130]{2,1,0:T(8,128)S(1)} fusion(f32[48,66,130]{2,1,0:T(8,128)} %get-tuple-element.249, f32[48,66,130]{2,1,0:T(8,128)} %get-tuple-element.248, f32[48,68,2]{2,1,0:T(8,128)} %copy.83, f32[48,2,128]{2,1,0:T(2,128)S(1)} %copy-done.52, f32[48,64,128]{2,1,0:T(8,128)} %copy-done.28, f32[48,2,128]{2,1,0:T(2,128)S(1)} %copy-done.50, ...), kind=kLoop, calls=%fused_computation.48 | loop fusion | flops 17297280 | bytes 32841216 | tf_op jit(solution)/shard_map/jit(_where)/select_n | solution.py:131
  502.0 5.5 add_select_fusion.8
  535.0 4.3 pad_maximum_fusion.44
  539.7 12.0 %add_select_fusion = f32[48,66,130]{2,1,0:T(8,128)S(1)} fusion(f32[48,66,130]{2,1,0:T(8,128)} %get-tuple-element.249, f32[48,66,130]{2,1,0:T(8,128)} %get-tuple-element.248, f32[48,68,2]{2,1,0:T(8,128)} %copy.89, f32[48,2,128]{2,1,0:T(2,128)S(1)} %copy-done.48, f32[48,64,128]{2,1,0:T(8,128)} %copy-done.27, f32[48,2,128]{2,1,0:T(2,128)S(1)} %copy-done.46, ...), kind=kLoop, calls=%fused_computation.47 | loop fusion | flops 17297280 | bytes 34732800 | tf_op jit(solution)/shard_map/jit(_where)/select_n | solution.py:131
  551.7 5.9 add_select_fusion.7
  557.8 180.5 %gather_fusion.1 = f32[32768]{0:T(1024)S(1)} fusion(f32[393216]{0:T(1024)S(1)} %bitcast.142, s32[32768]{0:T(1024)S(1)} %copy-done.41), kind=kCustom, calls=%fused_computation.1 | custom fusion | bytes 393216 | tf_op jit(solution)/shard_map/jit(_take)/gather | solution.py:237
  739.4 35.2 %while.22 = (s32[]{:T(128)}, f32[6,288]{1,0:T(8,128)S(1)}, f32[4,3,8192]{2,1,0:T(4,128)S(1)}, f32[4,8192]{1,0:T(4,128)S(1)}, f32[4,8192]{1,0:T(4,128)S(1)}, /*in...) while((s32[]{:T(128)}, f32[6,288]{1,0:T(8,128)S(1)}, ...), condition=%wide.region_2.3_spmd.clone, body=%wide.region_0.2_spmd.clone.sunk | while | flops 344952192 | bytes 1888719 | solution.py:175
  790.7 4.5 collective-permute-start.43
  796.3 16.3 %while.21 = (s32[]{:T(128)}, f32[4,8192]{1,0:T(4,128)S(1)}, f32[4,8192]{1,0:T(4,128)S(1)}, f32[4,8192]{1,0:T(4,128)S(1)}, f32[4,3,8192]{2,1,0:T(4,128)S(1)}, /*i...) while((s32[]{:T(128)}, f32[4,8192]{1,0:T(4,128)S(1)}, ...), condition=%wide.region_5.6_spmd, body=%wide.region_3.5_spmd.sunk | while | flops 172449792 | bytes 1153969 | solution.py:197
  (374 shorter events, 251.9 us)
Async XLA Ops:
  5.4 12.6 %collective-permute-start.4 = (f32[48,1,128]{2,1,0:T(1,128)S(1)}, f32[48,1,128]{2,1,0:T(1,128)S(1)}, u32[]{:S(2)}, u32[]{:S(2)}) collective-permute-start(f32[48,1,128]{2,1,0:T(1,128)S(1)} %get-tuple-element.287), channel_id=1, source_target_pairs={{0,8},{8,16},{16,24},{24,0},{1,9},{9,17},{17,25},{25,1},{2,10},{10... | collective-permute-start | bytes 73736 | tf_op jit(solution)/shard_map/ppermute | solution.py:47
  7.2 10.8 %collective-permute-start.5 = (f32[48,1,128]{2,1,0:T(1,128)S(1)}, f32[48,1,128]{2,1,0:T(1,128)S(1)}, u32[]{:S(2)}, u32[]{:S(2)}) collective-permute-start(f32[48,1,128]{2,1,0:T(1,128)S(1)} %get-tuple-element.288), channel_id=1, source_target_pairs={{8,0},{16,8},{24,16},{0,24},{9,1},{17,9},{25,17},{1,25},{10,2},{18... | collective-permute-start | bytes 73736 | tf_op jit(solution)/shard_map/ppermute | solution.py:50
  12.6 23.5 %collective-permute-start.10 = (bf16[48,68,2]{1,0,2:T(8,128)(2,1)}, bf16[48,68,2]{1,0,2:T(8,128)(2,1)}, u32[]{:S(2)}, u32[]{:S(2)}) collective-permute-start(bf16[48,68,2]{1,0,2:T(8,128)(2,1)} %copy.56), channel_id=1, source_target_pairs={{0,1},{1,2},{2,3},{3,4},{4,5},{5,6},{6,7},{7,0},{8,9},{9,10},{10,1... | collective-permute-start | bytes 39176 | tf_op jit(solution)/shard_map/ppermute | solution.py:47
  14.9 22.5 %collective-permute-start.11 = (bf16[48,68,2]{1,0,2:T(8,128)(2,1)}, bf16[48,68,2]{1,0,2:T(8,128)(2,1)}, u32[]{:S(2)}, u32[]{:S(2)}) collective-permute-start(bf16[48,68,2]{1,0,2:T(8,128)(2,1)} %copy.57), channel_id=1, source_target_pairs={{1,0},{2,1},{3,2},{4,3},{5,4},{6,5},{7,6},{0,7},{9,8},{10,9},{11,1... | collective-permute-start | bytes 39176 | tf_op jit(solution)/shard_map/ppermute | solution.py:50
  22.6 9.8 %collective-permute-start.6 = (f32[48,66,1]{1,0,2:T(8,128)S(1)}, f32[48,66,1]{1,0,2:T(8,128)S(1)}, u32[]{:S(2)}, u32[]{:S(2)}) collective-permute-start(f32[48,66,1]{1,0,2:T(8,128)S(1)} %copy.52), channel_id=1, source_target_pairs={{0,1},{1,2},{2,3},{3,4},{4,5},{5,6},{6,7},{7,0},{8,9},{9,10},{10,1... | collective-permute-start | bytes 38024 | tf_op jit(solution)/shard_map/ppermute | solution.py:47
  24.8 9.5 %collective-permute-start.7 = (f32[48,66,1]{1,0,2:T(8,128)S(1)}, f32[48,66,1]{1,0,2:T(8,128)S(1)}, u32[]{:S(2)}, u32[]{:S(2)}) collective-permute-start(f32[48,66,1]{1,0,2:T(8,128)S(1)} %copy.53), channel_id=1, source_target_pairs={{1,0},{2,1},{3,2},{4,3},{5,4},{6,5},{7,6},{0,7},{9,8},{10,9},{11,1... | collective-permute-start | bytes 38024 | tf_op jit(solution)/shard_map/ppermute | solution.py:50
  30.0 14.0 %collective-permute-start = (f32[48,2,128]{2,1,0:T(2,128)S(1)}, f32[48,2,128]{2,1,0:T(2,128)S(1)}, u32[]{:S(2)}, u32[]{:S(2)}) collective-permute-start(f32[48,2,128]{2,1,0:T(2,128)S(1)} %get-tuple-element.289), channel_id=1, source_target_pairs={{0,8},{8,16},{16,24},{24,0},{1,9},{9,17},{17,25},{25,1},{2,10},{10... | collective-permute-start | bytes 147464 | tf_op jit(solution)/shard_map/ppermute | solution.py:47
  32.4 11.7 %collective-permute-start.1 = (f32[48,2,128]{2,1,0:T(2,128)S(1)}, f32[48,2,128]{2,1,0:T(2,128)S(1)}, u32[]{:S(2)}, u32[]{:S(2)}) collective-permute-start(f32[48,2,128]{2,1,0:T(2,128)S(1)} %get-tuple-element.290), channel_id=1, source_target_pairs={{8,0},{16,8},{24,16},{0,24},{9,1},{17,9},{25,17},{1,25},{10,2},{18... | collective-permute-start | bytes 147464 | tf_op jit(solution)/shard_map/ppermute | solution.py:50
  48.7 12.1 %collective-permute-start.2 = (f32[48,68,2]{1,0,2:T(8,128)S(1)}, f32[48,68,2]{1,0,2:T(8,128)S(1)}, u32[]{:S(2)}, u32[]{:S(2)}) collective-permute-start(f32[48,68,2]{1,0,2:T(8,128)S(1)} %copy.48), channel_id=1, source_target_pairs={{0,1},{1,2},{2,3},{3,4},{4,5},{5,6},{6,7},{7,0},{8,9},{9,10},{10,1... | collective-permute-start | bytes 78344 | tf_op jit(solution)/shard_map/ppermute | solution.py:47
  50.8 11.8 %collective-permute-start.3 = (f32[48,68,2]{1,0,2:T(8,128)S(1)}, f32[48,68,2]{1,0,2:T(8,128)S(1)}, u32[]{:S(2)}, u32[]{:S(2)}) collective-permute-start(f32[48,68,2]{1,0,2:T(8,128)S(1)} %copy.49), channel_id=1, source_target_pairs={{1,0},{2,1},{3,2},{4,3},{5,4},{6,5},{7,6},{0,7},{9,8},{10,9},{11,1... | collective-permute-start | bytes 78344 | tf_op jit(solution)/shard_map/ppermute | solution.py:50
  123.8 385.0 %collective-permute-start.32 = (f32[1,1,32,6]{2,3,1,0:T(8,128)S(1)}, f32[1,1,32,6]{2,3,1,0:T(8,128)}, u32[]{:S(2)}, u32[]{:S(2)}) collective-permute-start(f32[1,1,32,6]{2,3,1,0:T(8,128)S(1)} %maximum_bitcast_fusion), channel_id=1, source_target_pairs={{0,8},{8,16},{16,24},{24,0},{1,9},{9,17},{17,25},{25,1},{2,10},{10... | collective-permute-start | bytes 2312 | tf_op jit(solution)/shard_map/ppermute | solution.py:47
  125.6 383.2 %collective-permute-start.33 = (f32[1,1,32,6]{2,3,1,0:T(8,128)S(1)}, f32[1,1,32,6]{2,3,1,0:T(8,128)}, u32[]{:S(2)}, u32[]{:S(2)}) collective-permute-start(f32[1,1,32,6]{2,3,1,0:T(8,128)S(1)} %maximum_bitcast_fusion), channel_id=1, source_target_pairs={{8,0},{16,8},{24,16},{0,24},{9,1},{17,9},{25,17},{1,25},{10,2},{18... | collective-permute-start | bytes 2312 | tf_op jit(solution)/shard_map/ppermute | solution.py:50
  133.4 8.3 %collective-permute-start.14 = (f32[48,68,2]{1,0,2:T(8,128)S(1)}, f32[48,68,2]{1,0,2:T(8,128)S(1)}, u32[]{:S(2)}, u32[]{:S(2)}) collective-permute-start(f32[48,68,2]{1,0,2:T(8,128)S(1)} %copy.62), channel_id=1, source_target_pairs={{0,1},{1,2},{2,3},{3,4},{4,5},{5,6},{6,7},{7,0},{8,9},{9,10},{10,1... | collective-permute-start | bytes 78344 | tf_op jit(solution)/shard_map/ppermute | solution.py:47
  135.5 8.1 %collective-permute-start.15 = (f32[48,68,2]{1,0,2:T(8,128)S(1)}, f32[48,68,2]{1,0,2:T(8,128)S(1)}, u32[]{:S(2)}, u32[]{:S(2)}) collective-permute-start(f32[48,68,2]{1,0,2:T(8,128)S(1)} %copy.63), channel_id=1, source_target_pairs={{1,0},{2,1},{3,2},{4,3},{5,4},{6,5},{7,6},{0,7},{9,8},{10,9},{11,1... | collective-permute-start | bytes 78344 | tf_op jit(solution)/shard_map/ppermute | solution.py:50
  179.7 8.1 collective-permute-start.18
  181.8 7.9 collective-permute-start.19
  223.3 8.3 %collective-permute-start.22 = (f32[48,68,2]{1,0,2:T(8,128)S(1)}, f32[48,68,2]{1,0,2:T(8,128)S(1)}, u32[]{:S(2)}, u32[]{:S(2)}) collective-permute-start(f32[48,68,2]{1,0,2:T(8,128)S(1)} %copy.74), channel_id=1, source_target_pairs={{0,1},{1,2},{2,3},{3,4},{4,5},{5,6},{6,7},{7,0},{8,9},{9,10},{10,1... | collective-permute-start | bytes 78344 | tf_op jit(solution)/shard_map/ppermute | solution.py:47
  225.5 8.2 %collective-permute-start.23 = (f32[48,68,2]{1,0,2:T(8,128)S(1)}, f32[48,68,2]{1,0,2:T(8,128)S(1)}, u32[]{:S(2)}, u32[]{:S(2)}) collective-permute-start(f32[48,68,2]{1,0,2:T(8,128)S(1)} %copy.75), channel_id=1, source_target_pairs={{1,0},{2,1},{3,2},{4,3},{5,4},{6,5},{7,6},{0,7},{9,8},{10,9},{11,1... | collective-permute-start | bytes 78344 | tf_op jit(solution)/shard_map/ppermute | solution.py:50
  267.2 213.6 %collective-permute-start.26 = (f32[48,68,2]{1,0,2:T(8,128)S(1)}, f32[48,68,2]{1,0,2:T(8,128)S(1)}, u32[]{:S(2)}, u32[]{:S(2)}) collective-permute-start(f32[48,68,2]{1,0,2:T(8,128)S(1)} %copy.80), channel_id=1, source_target_pairs={{0,1},{1,2},{2,3},{3,4},{4,5},{5,6},{6,7},{7,0},{8,9},{9,10},{10,1... | collective-permute-start | bytes 78344 | tf_op jit(solution)/shard_map/ppermute | solution.py:47
  267.9 214.9 %collective-permute-start.27 = (f32[48,68,2]{1,0,2:T(8,128)S(1)}, f32[48,68,2]{1,0,2:T(8,128)S(1)}, u32[]{:S(2)}, u32[]{:S(2)}) collective-permute-start(f32[48,68,2]{1,0,2:T(8,128)S(1)} %copy.81), channel_id=1, source_target_pairs={{1,0},{2,1},{3,2},{4,3},{5,4},{6,5},{7,6},{0,7},{9,8},{10,9},{11,1... | collective-permute-start | bytes 78344 | tf_op jit(solution)/shard_map/ppermute | solution.py:50
  510.1 16.7 %collective-permute-start.34 = (f32[3,1,32,6]{2,3,1,0:T(8,128)}, f32[3,1,32,6]{2,3,1,0:T(8,128)}, u32[]{:S(2)}, u32[]{:S(2)}) collective-permute-start(f32[3,1,32,6]{2,3,1,0:T(8,128)} %pad_maximum_fusion.57), channel_id=1, source_target_pairs={{0,1},{1,2},{2,3},{3,4},{4,5},{5,6},{6,7},{7,0},{8,9},{9,10},{10,1... | collective-permute-start | bytes 6920 | tf_op jit(solution)/shard_map/ppermute | solution.py:47
  510.1 16.7 %collective-permute-start.35 = (f32[3,1,32,6]{2,3,1,0:T(8,128)}, f32[3,1,32,6]{2,3,1,0:T(8,128)}, u32[]{:S(2)}, u32[]{:S(2)}) collective-permute-start(f32[3,1,32,6]{2,3,1,0:T(8,128)} %pad_maximum_fusion.57), channel_id=1, source_target_pairs={{1,0},{2,1},{3,2},{4,3},{5,4},{6,5},{7,6},{0,7},{9,8},{10,9},{11,1... | collective-permute-start | bytes 6920 | tf_op jit(solution)/shard_map/ppermute | solution.py:50
  519.5 10.1 %collective-permute-start.30 = (f32[48,68,2]{1,0,2:T(8,128)}, f32[48,68,2]{1,0,2:T(8,128)}, u32[]{:S(2)}, u32[]{:S(2)}) collective-permute-start(f32[48,68,2]{1,0,2:T(8,128)} %copy.86), channel_id=1, source_target_pairs={{0,1},{1,2},{2,3},{3,4},{4,5},{5,6},{6,7},{7,0},{8,9},{9,10},{10,1... | collective-permute-start | bytes 78344 | tf_op jit(solution)/shard_map/ppermute | solution.py:47
  522.6 9.6 %collective-permute-start.31 = (f32[48,68,2]{1,0,2:T(8,128)}, f32[48,68,2]{1,0,2:T(8,128)}, u32[]{:S(2)}, u32[]{:S(2)}) collective-permute-start(f32[48,68,2]{1,0,2:T(8,128)} %copy.87), channel_id=1, source_target_pairs={{1,0},{2,1},{3,2},{4,3},{5,4},{6,5},{7,6},{0,7},{9,8},{10,9},{11,1... | collective-permute-start | bytes 78344 | tf_op jit(solution)/shard_map/ppermute | solution.py:50
  (83 other events, 2501.6 us)
where the time goes:
time: 823 us; the launch traced here: 814 us
  local copies, waits for them, and re-layouts  490 us (60%)
  other arithmetic  190 us (23%)
  starting transfers between devices  66.2 us (8%)
  matrix products  46.9 us (6%)
  waiting for transfers between devices  18.4 us (2%)
    gather x2, local copies, waits for them, and re-layouts, shards(): jnp.take(eps_field.reshape(-1), sites).astype(jnp.float32)  202 us
    gather x2, local copies, waits for them, and re-layouts, shards(): phi_here = jnp.take(potential.reshape(-1), sites)  181 us
    select_n x12, other arithmetic, relax_colour(): jnp.where(colour_mask, centre + OVER_RELAX * (target - centre), centre)  142 us
    ppermute x22, starting transfers between devices, padded_2(): lax.ppermute(lax.slice_in_dim(block, 0, width, axis=dim), axis, backward)  46.1 us
    slice x26, local copies, waits for them, and re-layouts, padded_2(): lax.slice_in_dim(block, block.shape[dim] - width, None, axis=dim)  39 us
    concatenate x18, other arithmetic, padded_2(): block = jnp.concatenate([low, block, high], axis=dim)  33.7 us
    ppermute x22, starting transfers between devices, padded_2(): lax.ppermute(lax.slice_in_dim(block, block.shape[dim] - width, None, axis...  20.1 us
    dot_general x4, matrix products, add_block(): lax.dot_general(terms, onehot, (((1,), (1,)), ((), ())), precision=lax.Pr...  17.1 us
  transfers between devices with their start and end apart: 44, of which 13 were waited for; matrix products, arithmetic and copies ran while one was open for 49% of the time, Pallas kernels for 0%

commit v1 on v0

v1 whole, which is shorter than its diff:
```python
import functools
import math

import jax
import jax.numpy as jnp
import numpy as np
from jax import lax
from jax.experimental import pallas as pl
from jax.experimental.pallas import tpu as pltpu
from jax.sharding import PartitionSpec as P

SWEEPS = 6
RADIUS = 8
OVER_RELAX = 1.6
HALO = 2 * SWEEPS
FIRST = 16
MARGIN = 8
GROUPS = 5
SLOT = 2 * HALO
KEY_BITS = 13
F32 = jnp.float32

VELOCITY = np.array(
    [
        [1, 0, 0], [-1, 0, 0], [0, 1, 0], [0, -1, 0], [0, 0, 1], [0, 0, -1],
        [1, 1, 0], [1, -1, 0], [-1, 1, 0], [-1, -1, 0], [1, 0, 1], [1, 0, -1],
        [-1, 0, 1], [-1, 0, -1], [0, 1, 1], [0, 1, -1], [0, -1, 1], [0, -1, -1],
    ],
    dtype=np.float32,
)
WEIGHT = np.array([1.0 / 18.0] * 6 + [1.0 / 36.0] * 12, dtype=np.float32)


def direction_table():
    table = np.zeros((4, 8, 128), np.float32)
    table[:3, :, :18] = VELOCITY.T[:, None, :]
    table[3, :, :18] = WEIGHT[None, :]
    return jnp.asarray(table)


PAIRS = [(a, b) for a in range(6) for b in range(a, 6)]


def lane_pick(table, index):
    return jnp.take_along_axis(table, index, axis=1, mode="promise_in_bounds")


def roll(value, shift):
    return pltpu.roll(value, shift % 128, 1)


def lanes_of(shape):
    return lax.broadcasted_iota(jnp.int32, shape, 1)


def parity_of(shape):
    rows = lax.broadcasted_iota(jnp.int32, shape, 0)
    return (rows + lanes_of(shape)) % 2 == 0


def pack_kernel(pot, charge, eps, low, high, split, to_right, to_left):
    depth, wide, _ = pot.shape
    layers = depth // 2
    last = FIRST + wide

    def build(k, carry):
        for f, field in enumerate((pot, charge, eps)):
            fill = 1.0 if f == 2 else 0.0
            parts = (
                (FIRST, field[2 * k].astype(F32), field[2 * k + 1].astype(F32)),
                (FIRST - HALO, low[f, 2 * k], low[f, 2 * k + 1]),
                (last, high[f, 2 * k], high[f, 2 * k + 1]),
            )
            for start, even, odd in parts:
                flat = parity_of(even.shape)
                count = even.shape[0]
                split[2 * f, k, start:start + count, :] = jnp.where(flat, even, odd)
                split[2 * f + 1, k, start:start + count, :] = jnp.where(flat, odd, even)
            spare = FIRST - HALO
            edge = jnp.full((spare, 128), fill, F32)
            for c in range(2):
                split[2 * f + c, k, 0:spare, :] = edge
                split[2 * f + c, k, last + HALO:last + HALO + spare, :] = edge
        return carry

    lax.fori_loop(0, layers, build, 0)
    for f in range(3):
        for c in range(2):
            split[2 * f + c, layers] = jnp.full(
                (split.shape[2], 128), 1.0 if f == 2 else 0.0, F32
            )

    rows = slice(FIRST - HALO, last + HALO)
    lane = lanes_of((wide + 2 * HALO, 128))

    def strips(n, carry):
        f = n // GROUPS
        i = n % GROUPS
        right = jnp.zeros((wide + 2 * HALO, 128), F32)
        left = jnp.zeros((wide + 2 * HALO, 128), F32)
        for g in range(GROUPS):
            red = split[2 * f, i + GROUPS * g, rows, :]
            black = split[2 * f + 1, i + GROUPS * g, rows, :]
            base = SLOT * g
            in_red = (lane >= base) & (lane < base + HALO)
            in_black = (lane >= base + HALO) & (lane < base + SLOT)
            right = jnp.where(in_red, roll(red, base + HALO), right)
            right = jnp.where(in_black, roll(black, base + SLOT), right)
            left = jnp.where(in_red, roll(red, base), left)
            left = jnp.where(in_black, roll(black, base + HALO), left)
        to_right[f, i] = right
        to_left[f, i] = left
        return carry

    lax.fori_loop(0, 3 * GROUPS, strips, 0)


def relax_kernel(split, from_left, from_right, pot_out, press_out, pa, ea, wa, pb, eb, cb, wb):
    layers = split.shape[1] - 1
    depth, wide, _ = pot_out.shape
    rows = split.shape[2]
    tiles = rows // 8
    top = MARGIN
    lane = lanes_of((8, 128))
    flat = parity_of((8, 128))
    at_0 = lane == 0
    at_127 = lane == 127
    in_slot = lane % SLOT
    in_left = in_slot < HALO
    slot_left = in_slot == HALO - 1
    slot_right = in_slot == HALO
    pick = [(lane == SLOT * g + HALO - 1) | (lane == SLOT * g + HALO) for g in range(GROUPS)]

    zero = jnp.zeros((rows + 2 * MARGIN, 128), F32)
    one = jnp.ones((rows + 2 * MARGIN, 128), F32)
    margin0 = jnp.zeros((MARGIN, 128), F32)
    margin1 = jnp.ones((MARGIN, 128), F32)
    for c in range(2):
        pa[c, 0] = zero
        ea[c, 0] = one
        ea[c, layers + 1] = one

    def load_core(k, carry):
        for c in range(2):
            pa[c, k + 1, 0:top, :] = margin0
            pa[c, k + 1, top:top + rows, :] = split[c, k]
            pa[c, k + 1, top + rows:, :] = margin0
            ea[c, k + 1, 0:top, :] = margin1
            ea[c, k + 1, top:top + rows, :] = split[4 + c, k]
            ea[c, k + 1, top + rows:, :] = margin1
        return carry

    lax.fori_loop(0, layers + 1, load_core, 0)
    for c in range(2):
        ea[c, 0, top:top + rows, :] = split[5 - c, 0]
        ea[c, layers + 1, top:top + rows, :] = split[5 - c, layers - 1]
        pa[c, layers + 2] = zero
        ea[c, layers + 2] = one

    first = FIRST - HALO
    high = wide + 2 * HALO
    wide_lane = lanes_of((high, 128))
    wide_left = wide_lane % SLOT < HALO
    wide_used = wide_lane < SLOT * GROUPS
    for c in range(2):
        for i in range(GROUPS + 2):
            pb[c, i] = zero
            eb[c, i] = one
        for i in range(GROUPS):
            cb[c, i] = jnp.zeros((rows, 128), F32)

    for f, target in enumerate((pb, cb, eb)):
        for i in range(GROUPS):
            west = from_left[f, i]
            east = from_right[f, i]
            red = jnp.where(wide_left, west, roll(east, HALO))
            black = jnp.where(wide_left, roll(west, -HALO), east)
            fill = 1.0 if f == 2 else 0.0
            red = jnp.where(wide_used, red, fill)
            black = jnp.where(wide_used, black, fill)
            if f == 1:
                target[0, i, first:first + high, :] = red
                target[1, i, first:first + high, :] = black
            else:
                target[0, i + 1, top + first:top + first + high, :] = red
                target[1, i + 1, top + first:top + first + high, :] = black

    all_lane = lanes_of((rows + 2 * MARGIN, 128))
    lead = all_lane < SLOT
    tail = all_lane >= SLOT * (GROUPS - 1)
    spare_slot = SLOT * (layers // GROUPS)
    in_spare = (all_lane >= spare_slot) & (all_lane < spare_slot + SLOT)

    def wrap_pot(c):
        pb[c, 0] = jnp.where(lead, 0.0, roll(pb[c, GROUPS], SLOT))
        pb[c, GROUPS + 1] = jnp.where(tail, 0.0, roll(pb[c, 1], -SLOT))

    spare_row = layers % GROUPS + 1
    for c in range(2):
        wrap_pot(c)
        eb[c, spare_row] = jnp.where(in_spare, eb[1 - c, spare_row - 1], eb[c, spare_row])
    for c in range(2):
        eb[c, 0] = jnp.where(lead, eb[1 - c, 1], roll(eb[c, GROUPS], SLOT))
        eb[c, GROUPS + 1] = jnp.where(tail, 1.0, roll(eb[c, 1], -SLOT))

    def around(src_a, src_b, other, color, i, t, body_a, body_b):
        r0 = top + 8 * t
        rs = slice(r0, r0 + 8)
        rm = slice(r0 - 1, r0 + 7)
        rp = slice(r0 + 1, r0 + 9)
        up = ~flat if color == 0 else flat
        side = src_b[other, i + 1, rs, :]
        edge = side
        for g in range(GROUPS):
            k = i + GROUPS * g
            here = src_a[other, k + 1, rs, :]
            halo = roll(side, -(SLOT * g + HALO))
            body_a(k, (
                here,
                jnp.where(up, src_a[other, k + 2, rs, :], src_a[other, k, rs, :]),
                src_a[other, k + 1, rm, :],
                src_a[other, k + 1, rp, :],
                roll(jnp.where(at_127, halo, here), 1),
                roll(jnp.where(at_0, halo, here), -1),
            ))
            if body_b is not None:
                edge = jnp.where(pick[g], roll(here, SLOT * g + HALO), edge)
        if body_b is not None:
            body_b((
                side,
                jnp.where(up, src_b[other, i + 2, rs, :], src_b[other, i, rs, :]),
                src_b[other, i + 1, rm, :],
                src_b[other, i + 1, rp, :],
                roll(jnp.where(slot_left, edge, side), 1),
                roll(jnp.where(slot_right, edge, side), -1),
            ))

    def coefficients(own, charge, sides):
        faces = [0.5 * (own + side) for side in sides]
        total = faces[0] + faces[1] + faces[2] + faces[3] + faces[4] + faces[5]
        scale = OVER_RELAX / total
        return [face * scale for face in faces] + [charge * scale]

    for c in range(2):
        def set_up(i, carry, c=c):
            for t in range(tiles):
                ts = slice(8 * t, 8 * t + 8)
                ps = slice(top + 8 * t, top + 8 * t + 8)

                def body_a(k, sides):
                    values = coefficients(ea[c, k + 1, ps, :], split[2 + c, k, ts, :], sides)
                    for n, value in enumerate(values):
                        wa[c, n, k, ts, :] = value

                def body_b(sides):
                    values = coefficients(eb[c, i + 1, ps, :], cb[c, i, ts, :], sides)
                    live = in_spare[0:8] & (i + 1 == spare_row)
                    for n, value in enumerate(values):
                        wb[c, n, i, ts, :] = jnp.where(live, 0.0, value)

                around(ea, eb, 1 - c, c, i, t, body_a, body_b)
            return carry

        lax.fori_loop(0, GROUPS, set_up, 0)
        for n in range(7):
            wa[c, n, layers] = jnp.zeros((rows, 128), F32)

    def combine(own, w, sides):
        left = w[0] * sides[0] + w[1] * sides[1]
        mid = w[2] * sides[2] + w[3] * sides[3]
        right = w[4] * sides[4] + w[5] * sides[5]
        return (w[6] - (OVER_RELAX - 1.0) * own) + (left + (mid + right))

    for step in range(2 * SWEEPS):
        c = step % 2
        reach = HALO - 1 - step
        t_low = (FIRST - reach) // 8
        t_high = -(-(FIRST + wide + reach) // 8)

        def half(i, carry, c=c, reach=reach, t_low=t_low, t_high=t_high):
            for t in range(t_low, t_high):
                ts = slice(8 * t, 8 * t + 8)
                ps = slice(top + 8 * t, top + 8 * t + 8)

                def body_a(k, sides):
                    w = [wa[c, n, k, ts, :] for n in range(7)]
                    pa[c, k + 1, ps, :] = combine(pa[c, k + 1, ps, :], w, sides)

                def body_b(sides):
                    w = [wb[c, n, i, ts, :] for n in range(7)]
                    pb[c, i + 1, ps, :] = combine(pb[c, i + 1, ps, :], w, sides)

                around(pa, pb, 1 - c, c, i, t, body_a, body_b if reach else None)
            return carry

        lax.fori_loop(0, GROUPS, half, 0)
        if reach:
            wrap_pot(c)

    core = slice(top + FIRST, top + FIRST + wide)
    core_flat = parity_of((wide, 128))

    def finish(k, carry):
        red, black = pa[0, k + 1, core, :], pa[1, k + 1, core, :]
        e_red, e_black = ea[0, k + 1, core, :], ea[1, k + 1, core, :]
        q_red = 0.5 * e_red * red * red
        q_black = 0.5 * e_black * black * black
        pot_out[2 * k] = jnp.where(core_flat, red, black)
        pot_out[2 * k + 1] = jnp.where(core_flat, black, red)
        press_out[2 * k] = jnp.where(core_flat, q_red, q_black)
        press_out[2 * k + 1] = jnp.where(core_flat, q_black, q_red)
        return carry

    lax.fori_loop(0, layers, finish, 0)


def geometry(direction, offsets, table):
    c0, c1, c2, w = [lane_pick(table[n], direction) for n in range(4)]
    r0, r1, r2 = offsets
    arms = [c0, c1, c2, r1 * c2 - r2 * c1, r2 * c0 - r0 * c2, r0 * c1 - r1 * c0]
    return arms, w


def store_split(stage, total, n, value):
    coarse = value.astype(jnp.bfloat16).astype(F32)
    stage[n] = coarse
    stage[total + n] = value - coarse


def add_by_slot(stage, slot, width):
    slots = lax.broadcasted_iota(jnp.int32, (width, 128), 0)
    hot, terms = [], []
    for s in range(8):
        row = jnp.broadcast_to(slot[s:s + 1, :], (width, 128))
        hot.append((row == slots).astype(F32).astype(jnp.bfloat16))
        terms.append(stage[:, s, :].astype(jnp.bfloat16))
    return lax.dot_general(
        jnp.concatenate(hot, axis=1),
        jnp.concatenate(terms, axis=1),
        (((1,), (1,)), ((), ())),
        preferred_element_type=F32,
    )


def fixed_kernel(slots, dirs, pops, rb, table, out, stage, acc, *, width):
    acc[...] = jnp.zeros_like(acc)
    total = stage.shape[0] // 2
    for n in range(6 + len(PAIRS), total):
        stage[n] = jnp.zeros((8, 128), F32)
        stage[total + n] = jnp.zeros((8, 128), F32)

    def block(b, carry):
        rs = pl.ds(pl.multiple_of(8 * b, 8), 8)
        arms, w = geometry(dirs[rs, :], [rb[n, rs, :] for n in range(3)], table)
        twice = 2.0 * pops[rs, :]
        weighted = [w * arm for arm in arms]
        for n in range(6):
            store_split(stage, total, n, twice * arms[n])
        for n, (a, d) in enumerate(PAIRS):
            store_split(stage, total, 6 + n, weighted[a] * arms[d])
        acc[...] += add_by_slot(stage, slots[rs, :], width)
        return carry

    lax.fori_loop(0, slots.shape[0] // 8, block, 0)
    out[...] = acc[:, 0:total] + acc[:, total:]


def press_kernel(low, high, keys, rb, table, press, out, stage, acc, *, width):
    acc[...] = jnp.zeros_like(acc)
    total = stage.shape[0] // 2
    for n in range(6, total):
        stage[n] = jnp.zeros((8, 128), F32)
        stage[total + n] = jnp.zeros((8, 128), F32)

    def block(b, carry):
        rs = pl.ds(pl.multiple_of(8 * b, 8), 8)
        key = keys[rs, :]
        place = (key >> KEY_BITS) + (1 << 18)
        code = key & ((1 << KEY_BITS) - 1)
        row = place >> 7
        column = place & 127
        slot = jnp.floor((code.astype(F32) + 0.5) * (1.0 / 18.0)).astype(jnp.int32)
        direction = code - 18 * slot

        def look(m, found):
            base = pl.multiple_of(8 * m, 8)
            ahead = row - base
            for s in range(8):
                line = jnp.broadcast_to(press[pl.ds(base + s, 1), :], (8, 128))
                found = jnp.where(ahead == s, lane_pick(line, column), found)
            return found

        q = lax.fori_loop(low[b], high[b] + 1, look, jnp.zeros((8, 128), F32))
        arms, w = geometry(direction, [rb[n][rs, :] for n in range(3)], table)
        wq = w * q
        for n in range(6):
            store_split(stage, total, n, wq * arms[n])
        acc[...] += add_by_slot(stage, slot, width)
        return carry

    lax.fori_loop(0, keys.shape[0] // 8, block, 0)
    out[...] = acc[:, 0:total] + acc[:, total:]


def press_entry(low, high, keys, rb0, rb1, rb2, table, press, out, stage, acc, *, width):
    press_kernel(low, high, keys, (rb0, rb1, rb2), table, press, out, stage, acc, width=width)


def reflect_kernel(slots, dirs, pops, rb, table, motion, out):
    def block(b, carry):
        rs = pl.ds(pl.multiple_of(8 * b, 8), 8)
        arms, w = geometry(dirs[rs, :], [rb[n, rs, :] for n in range(3)], table)
        slot = slots[rs, :]
        lane = slot & 127
        part = slot >> 7
        along = jnp.zeros((8, 128), F32)
        for n in range(6):
            value = jnp.zeros((8, 128), F32)
            for h in range(motion.shape[1]):
                line = jnp.broadcast_to(motion[n, h:h + 1, :], (8, 128))
                value = jnp.where(part == h, lane_pick(line, lane), value)
            along += arms[n] * value
        out[rs, :] = pops[rs, :] - jnp.where(slot >= 0, 6.0 * w * along, 0.0)
        return carry

    lax.fori_loop(0, slots.shape[0] // 8, block, 0)


def ring(axis):
    count = lax.axis_size(axis)
    forward = [(i, (i + 1) % count) for i in range(count)]
    return forward, [(b, a) for a, b in forward]


def vmem(n):
    return [pl.BlockSpec(memory_space=pltpu.VMEM)] * n


PARAMS = pltpu.CompilerParams(vmem_limit_bytes=60 * 1024 * 1024)


def shards(
    eps_field, charge, potential_start, colloid_vel, colloid_spin, link_dir, link_colloid,
    link_site, link_depth, link_pop, link_rb,
):
    depth, wide, long = charge.shape
    layers = depth // 2
    rows = wide + 2 * FIRST
    fx, bx = ring("gx")
    fy, by = ring("gy")

    def edge(part):
        return jnp.stack([potential_start[:, part], charge[:, part], eps_field[:, part].astype(F32)])

    low = lax.ppermute(edge(slice(wide - HALO, wide)), "gx", fx)
    high = lax.ppermute(edge(slice(0, HALO)), "gx", bx)

    per_tile = colloid_vel.shape[1]
    width = 9 * per_tile
    count = link_pop.shape[-1]
    lines = count // 128
    ids = link_colloid.reshape(lines, 128)
    dirs = link_dir.reshape(lines, 128)
    pops = link_pop.reshape(lines, 128)
    rb = link_rb.reshape(3, lines, 128)
    count_x, count_y = lax.axis_size("gx"), lax.axis_size("gy")
    owner = ids // per_tile
    near_x = (owner // count_y - lax.axis_index("gx") + 1) % count_x
    near_y = (owner % count_y - lax.axis_index("gy") + 1) % count_y
    live = ids >= 0
    slots = jnp.where(live, (near_x * 3 + near_y) * per_tile + ids % per_tile, -1)
    place = link_depth.reshape(lines, 128) * (wide * long) + link_site.reshape(lines, 128)
    key = jnp.where(
        live, (place - (1 << 18)) * (1 << KEY_BITS) + slots * 18 + dirs, np.int32(2**31 - 1)
    )
    keys, rb0, rb1, rb2 = lax.sort(
        (key.reshape(-1), rb[0].reshape(-1), rb[1].reshape(-1), rb[2].reshape(-1)),
        num_keys=1, is_stable=False,
    )
    keys = keys.reshape(lines, 128)
    table = direction_table()
    place_rows = (keys.reshape(-1, 1024)[:, ::1023] >> KEY_BITS) + (1 << 18)
    bounds = jnp.minimum(place_rows // 1024, depth * wide // 8 - 1)

    split, to_right, to_left = pl.pallas_call(
        pack_kernel,
        out_shape=(
            jax.ShapeDtypeStruct((6, layers + 1, rows, 128), F32),
            jax.ShapeDtypeStruct((3, GROUPS, wide + 2 * HALO, 128), F32),
            jax.ShapeDtypeStruct((3, GROUPS, wide + 2 * HALO, 128), F32),
        ),
        in_specs=vmem(5), out_specs=tuple(vmem(3)), compiler_params=PARAMS, name="pack",
    )(potential_start, charge, eps_field, low, high)
    from_left = lax.ppermute(to_right, "gy", fy)
    from_right = lax.ppermute(to_left, "gy", by)

    terms = 32
    fixed = pl.pallas_call(
        functools.partial(fixed_kernel, width=width),
        out_shape=jax.ShapeDtypeStruct((width, terms), F32),
        in_specs=vmem(5), out_specs=vmem(1)[0],
        scratch_shapes=[pltpu.VMEM((2 * terms, 8, 128), F32), pltpu.VMEM((width, 2 * terms), F32)],
        compiler_params=PARAMS, name="fixed",
        cost_estimate=pl.CostEstimate(flops=10**9, bytes_accessed=2 * 10**7, transcendentals=0),
    )(slots, dirs, pops, rb, table)

    tall = rows + 2 * MARGIN
    potential, press = pl.pallas_call(
        relax_kernel,
        out_shape=(jax.ShapeDtypeStruct(charge.shape, F32),) * 2,
        in_specs=vmem(3), out_specs=tuple(vmem(2)),
        scratch_shapes=[
            pltpu.VMEM((2, layers + 3, tall, 128), F32),
            pltpu.VMEM((2, layers + 3, tall, 128), F32),
            pltpu.VMEM((2, 7, layers + 1, rows, 128), F32),
            pltpu.VMEM((2, GROUPS + 2, tall, 128), F32),
            pltpu.VMEM((2, GROUPS + 2, tall, 128), F32),
            pltpu.VMEM((2, GROUPS, rows, 128), F32),
            pltpu.VMEM((2, 7, GROUPS, rows, 128), F32),
        ],
        compiler_params=PARAMS, name="relax",
    )(split, from_left, from_right)

    smem = pl.BlockSpec(memory_space=pltpu.SMEM)
    pressed = pl.pallas_call(
        functools.partial(press_entry, width=width),
        out_shape=jax.ShapeDtypeStruct((width, 8), F32),
        in_specs=[smem, smem] + vmem(6), out_specs=vmem(1)[0],
        scratch_shapes=[pltpu.VMEM((16, 8, 128), F32), pltpu.VMEM((width, 16), F32)],
        compiler_params=PARAMS, name="press",
    )(
        bounds[:, 0], bounds[:, 1], keys, rb0.reshape(lines, 128), rb1.reshape(lines, 128),
        rb2.reshape(lines, 128), table, press.reshape(depth * wide, 128),
    )

    sums = jnp.concatenate([fixed[:, 0:6] + pressed[:, 0:6], fixed[:, 6:27]], axis=1).T
    sums = sums.reshape(27, 3, 3, per_tile)
    mid = (
        sums[:, 1]
        + lax.ppermute(sums[:, 0], "gx", bx)
        + lax.ppermute(sums[:, 2], "gx", fx)
    )
    mine = mid[:, 1] + lax.ppermute(mid[:, 0], "gy", by) + lax.ppermute(mid[:, 2], "gy", fy)
    motion = jnp.concatenate([colloid_vel, colloid_spin], axis=0)
    drag = []
    for a in range(6):
        line = jnp.zeros_like(motion[0])
        for d in range(6):
            n = PAIRS.index((min(a, d), max(a, d)))
            line = line + mine[6 + n] * motion[d]
        drag.append(line)
    totals = mine[0:6] - 6.0 * jnp.stack(drag)
    mass = 4.0 / 3.0 * math.pi * RADIUS**3
    inertia = 0.4 * mass * RADIUS**2
    new_motion = jnp.concatenate(
        [motion[0:3] + totals[0:3] / mass, motion[3:6] + totals[3:6] / inertia], axis=0
    )
    report = jnp.concatenate([totals[0:3], totals[3:6] / RADIUS], axis=0)

    column = jnp.stack(
        [lax.ppermute(new_motion, "gy", fy), new_motion, lax.ppermute(new_motion, "gy", by)], axis=1
    )
    around = jnp.stack(
        [lax.ppermute(column, "gx", fx), column, lax.ppermute(column, "gx", bx)], axis=1
    ).reshape(6, width)
    groups = -(-width // 128)
    around = jnp.pad(around, ((0, 0), (0, groups * 128 - width))).reshape(6, groups, 128)
    link_out = pl.pallas_call(
        reflect_kernel,
        out_shape=jax.ShapeDtypeStruct((lines, 128), F32),
        in_specs=vmem(6), out_specs=vmem(1)[0], compiler_params=PARAMS, name="reflect",
    )(slots, dirs, pops, rb, table, around)
    return potential, report, link_out.reshape(link_pop.shape)


def solution(mesh):
    placed = (
        P(None, "gx", "gy"),
        P(None, "gx", "gy"),
        P(None, "gx", "gy"),
        P(None, ("gx", "gy")),
        P(None, ("gx", "gy")),
        P("gx", "gy", None),
        P("gx", "gy", None),
        P("gx", "gy", None),
        P("gx", "gy", None),
        P("gx", "gy", None),
        P(None, "gx", "gy", None),
    )
    return jax.shard_map(
        shards,
        mesh=mesh,
        in_specs=placed,
        out_specs=(P(None, "gx", "gy"), P(None, ("gx", "gy")), P("gx", "gy", None)),
        check_vma=False,
    )
```

time: 823 us -> 311 us (0.38); the launches traced: 814 us -> 311 us
  local copies, waits for them, and re-layouts: 490 us -> 10.2 us
  Pallas kernels: 0 us -> 231 us
  other arithmetic: 190 us -> 20.5 us
  matrix products: 46.9 us -> 0 us
  starting transfers between devices: 66.2 us -> 19.7 us
  waiting for transfers between devices: 18.4 us -> 28.8 us
    gather x4 -> x0, local copies, waits for them, and re-layouts: 383 us -> none  [the longest x2 202 us: shards(): jnp.take(eps_field.reshape(-1), sites).astype(jnp.float32)]
    pallas_call x0 -> x5, Pallas kernels: none -> 231 us  [the longest x1 143 us: shards(): pl.pallas_call(relax_kernel, out_shape=(jax.ShapeDtypeStruct(charge.shape...]
    select_n x14 -> x2, other arithmetic: 143 us -> 1.39 us  [the longest x1 1.01 us: shards(): jnp.where(live, (near_x * 3 + near_y) * per_tile + ids % per_tile, -1)]
    slice x39 -> x9, local copies, waits for them, and re-layouts: 59.7 us -> 3.48 us  [the longest x1 1.33 us: edge(): potential_start[:, part]]
    dot_general x14 -> x0, matrix products: 46.9 us -> none  [the longest x4 17.1 us: add_block(): lax.dot_general(terms, onehot, (((1,), (1,)), ((), ())), precision=lax.Pr...]
    ppermute x44 -> x12, starting transfers between devices: 66.2 us -> 19.7 us  [the longest x1 4.43 us: shards(): lax.ppermute(column, 'gx', fx)]
    concatenate x19 -> x1, other arithmetic: 34.3 us -> 0.6 us  [shards(): report = jnp.concatenate([totals[0:3], totals[3:6] / RADIUS], axis=0)]
    ppermute x16 -> x2, local copies, waits for them, and re-layouts: 31.6 us -> 3.8 us  [the longest x1 2.46 us: shards(): low = lax.ppermute(edge(slice(wide - HALO, wide)), 'gx', fx)]
  transfers between devices with their start and end apart: 44 -> 12, of which waited for: 13 -> 6; matrix products, arithmetic and copies ran while one was open for 49% -> 7% of each run, Pallas kernels for 0% -> 7%
where the time goes in v1:
time: 311 us
  Pallas kernels  231 us (74%)
  waiting for transfers between devices  28.8 us (9%)
  other arithmetic  20.5 us (7%)
  starting transfers between devices  19.7 us (6%)
  local copies, waits for them, and re-layouts  10.2 us (3%)
    pallas_call x1, Pallas kernels, shards(): pl.pallas_call(relax_kernel, out_shape=(jax.ShapeDtypeStruct(charge.shape...  143 us
    pallas_call x1, Pallas kernels, shards(): pl.pallas_call(functools.partial(press_entry, width=width), out_shape=jax...  48.9 us
    pallas_call x1, Pallas kernels, shards(): pl.pallas_call(functools.partial(fixed_kernel, width=width), out_shape=ja...  22.5 us
    ppermute x1, waiting for transfers between devices, shards(): high = lax.ppermute(edge(slice(0, HALO)), 'gx', bx)  18.6 us
    sort x1, other arithmetic, shards(): lax.sort((key.reshape(-1), rb[0].reshape(-1), rb[1].reshape(-1), rb[2].re...  16.9 us
    pallas_call x1, Pallas kernels, shards(): pl.pallas_call(pack_kernel, out_shape=(jax.ShapeDtypeStruct((6, layers +...  11.1 us
  transfers between devices with their start and end apart: 12, of which 6 were waited for; matrix products, arithmetic and copies ran while one was open for 7% of the time, Pallas kernels for 7%

profile of v1, /device:TPU:1, one launch (start us, length us, event | category | flops | bytes accessed | tf_op | source)
XLA Modules:
  0.0 310.6 jit_solution(472150519264429884)
XLA Ops:
  0.7 1.3 fusion.52
  3.3 2.7 collective-permute-start
  6.2 18.6 %collective-permute-done.1 = f32[3,48,12,128]{3,1,2,0:T(8,128)S(1)} collective-permute-done((f32[3,48,12,128]{3,1,2,0:T(8,128)S(1)}, f32[3,48,12,128]{3,1,2,0:T(8,128)S(1)}, u32[]{:S(2)}, u32[]{:S(2)}) %collective-permute-start.1) | collective-permute-done | bytes 884768 | tf_op jit(solution)/shard_map/ppermute | solution.py:456
  24.9 1.3 copy.47.high
  26.2 2.5 copy.46.low
  28.7 11.1 %pack.1 = (f32[6,25,96,128]{3,2,1,0:T(8,128)}, f32[3,5,88,128]{3,2,1,0:T(8,128)}, f32[3,5,88,128]{3,2,1,0:T(8,128)}) custom-call(f32[48,64,128]{2,1,0:T(8,128)} %pot.1, f32[48,64,128]{2,1,0:T(8,128)} %charge.1, bf16[48,64,128]{2,1,0:T(8,128)(2,1)} %eps.1, f32[3,48,12,128]{3,2,1,0:T(8,128)} %copy.46.low, f32[3,48,12,128]{3,2,1,0:T(8,128)} %copy.47.high), custom_call_target="tpu_custom_call" | custom-call | tf_op jit(solution)/shard_map/pack/pallas_call | solution.py:485
  39.8 1.2 collective-permute-start.2
  41.0 3.0 collective-permute-start.3
  44.5 16.9 %sort.27 = (s32[32768]{0:T(1024)S(1)}, f32[32768]{0:T(1024)}, f32[32768]{0:T(1024)}, f32[32768]{0:T(1024)}) sort(s32[32768]{0:T(1024)S(1)} %fusion.24, f32[32768]{0:T(1024)S(1)} %bitcast.78, f32[32768]{0:T(1024)S(1)} %bitcast.79, f32[32768]{0:T(1024)S(1)} %bitcast.77), dimensions={0}, to_apply=%region_0.1 | sort | flops 491520 | bytes 1048576 | tf_op jit(solution)/shard_map/sort | solution.py:476
  61.5 1.0 fusion.9.slots
  62.5 22.5 %fixed.1 = f32[288,32]{1,0:T(8,128)} custom-call(s32[256,128]{1,0:T(8,128)} %fusion.9.slots, s32[256,128]{1,0:T(8,128)} %bitcast.80, f32[256,128]{1,0:T(8,128)} %bitcast.86, f32[3,256,128]{2,1,0:T(8,128)} %bitcast.71, f32[4,8,128]{2,1,0:T(8,128)} %constant.128.clone.table), custom_call_target="tpu_custom_call" | custom-call | flops 1000000000 | bytes 20000000 | tf_op jit(solution)/shard_map/fixed/pallas_call | solution.py:498
  85.0 1.0 slice.258
  88.0 142.8 %relax.1 = (f32[48,64,128]{2,1,0:T(8,128)}, f32[48,64,128]{2,1,0:T(8,128)}) custom-call(f32[6,25,96,128]{3,2,1,0:T(8,128)} %get-tuple-element.12.split, f32[3,5,88,128]{3,2,1,0:T(8,128)} %copy-done.3, f32[3,5,88,128]{3,2,1,0:T(8,128)} %copy-done.4), custom_call_target="tpu_custom_call" | custom-call | tf_op jit(solution)/shard_map/relax/pallas_call | solution.py:508
  230.8 48.9 %press.1 = f32[288,8]{1,0:T(8,128)} custom-call(s32[32]{0:T(128)} %get-tuple-element.22.low, s32[32]{0:T(128)} %get-tuple-element.21.high, s32[256,128]{1,0:T(8,128)} %bitcast.73, f32[256,128]{1,0:T(8,128)} %bitcast.83, f32[256,128]{1,0:T(8,128)} %bitcast.84, f32[256,128]{1,0:T(8,128)} %bitcast.85, f32[4,8,128]{2,1,0:T(8,128)} %constant.128.clone.table, ...), custom_call_target="tpu_custom_call" | custom-call | tf_op jit(solution)/shard_map/press/pallas_call | solution.py:525
  281.6 1.2 collective-permute-start.5
  282.9 1.8 collective-permute-done.4
  284.7 1.6 collective-permute-start.6
  286.3 1.0 collective-permute-done.6
  287.4 4.2 %collective-permute-done.7 = f32[27,32]{1,0:T(8,128)S(1)} collective-permute-done((f32[27,32]{1,0:T(8,128)S(1)}, f32[27,32]{1,0:T(8,128)S(1)}, u32[]{:S(2)}, u32[]{:S(2)}) %collective-permute-start.7) | collective-permute-done | bytes 3488 | tf_op jit(solution)/shard_map/ppermute | solution.py:543
  291.9 4.1 %collective-permute-start.9 = (f32[6,32]{1,0:T(8,128)S(1)}, f32[6,32]{1,0:T(8,128)S(1)}, u32[]{:S(2)}, u32[]{:S(2)}) collective-permute-start(f32[6,32]{1,0:T(8,128)S(1)} %get-tuple-element.40), channel_id=1, source_target_pairs={{1,0},{2,1},{3,2},{4,3},{5,4},{6,5},{7,6},{0,7},{9,8},{10,9},{11,1... | collective-permute-start | bytes 2312 | tf_op jit(solution)/shard_map/ppermute | solution.py:561
  296.0 1.0 collective-permute-done.8
  297.0 4.4 %collective-permute-start.10 = (f32[6,3,32]{2,0,1:T(8,128)S(1)}, f32[6,3,32]{2,0,1:T(8,128)S(1)}, u32[]{:S(2)}, u32[]{:S(2)}) collective-permute-start(f32[6,3,32]{2,0,1:T(8,128)S(1)} %get-tuple-element.38), channel_id=1, source_target_pairs={{0,8},{8,16},{16,24},{24,0},{1,9},{9,17},{17,25},{25,1},{2,10},{10... | collective-permute-start | bytes 6920 | tf_op jit(solution)/shard_map/ppermute | solution.py:564
  302.6 2.1 collective-permute-done.11
  305.4 5.3 %reflect.1 = f32[256,128]{1,0:T(8,128)} custom-call(s32[256,128]{1,0:T(8,128)} %fusion.9.slots, s32[256,128]{1,0:T(8,128)} %bitcast.81, f32[256,128]{1,0:T(8,128)} %bitcast.87, f32[3,256,128]{2,1,0:T(8,128)} %bitcast.72, f32[4,8,128]{2,1,0:T(8,128)} %constant.128.clone.table, f32[6,3,128]{2,1,0:T(4,128)} %reshape.82.motion), custom_call_target="tpu_custom_call" | custom-call | tf_op jit(solution)/shard_map/reflect/pallas_call | solution.py:568
  (80 shorter events, 8.0 us)
Async XLA Ops:
  0.6 1.7 copy-start
  0.6 1.8 copy-start.1
  2.9 22.0 %collective-permute-start.1 = (f32[3,48,12,128]{3,1,2,0:T(8,128)S(1)}, f32[3,48,12,128]{3,1,2,0:T(8,128)S(1)}, u32[]{:S(2)}, u32[]{:S(2)}) collective-permute-start(f32[3,48,12,128]{3,1,2,0:T(8,128)S(1)} %pad_maximum_fusion.1), channel_id=1, source_target_pairs={{8,0},{16,8},{24,16},{0,24},{9,1},{17,9},{25,17},{1,25},{10,2},{18... | collective-permute-start | bytes 2654216 | tf_op jit(solution)/shard_map/ppermute | solution.py:456
  3.0 3.0 copy-start.2
  3.2 2.8 copy-start.9
  3.2 2.8 copy-start.10
  3.3 22.9 %collective-permute-start = (f32[3,48,12,128]{3,1,2,0:T(8,128)S(1)}, f32[3,48,12,128]{3,1,2,0:T(8,128)}, u32[]{:S(2)}, u32[]{:S(2)}) collective-permute-start(f32[3,48,12,128]{3,1,2,0:T(8,128)S(1)} %pad_maximum_fusion), channel_id=1, source_target_pairs={{0,8},{8,16},{16,24},{24,0},{1,9},{9,17},{17,25},{25,1},{2,10},{10... | collective-permute-start | bytes 2654216 | tf_op jit(solution)/shard_map/ppermute | solution.py:455
  28.7 15.4 %copy-start.7 = (s32[1,1,32768]{2,1,0:T(1,128)S(1)}, s32[1,1,32768]{2,1,0:T(1,128)}, u32[]{:S(2)}) copy-start(s32[1,1,32768]{2,1,0:T(1,128)} %param.18) | copy-start | bytes 393220
  28.7 15.4 %copy-start.8 = (s32[1,1,32768]{2,1,0:T(1,128)S(1)}, s32[1,1,32768]{2,1,0:T(1,128)}, u32[]{:S(2)}) copy-start(s32[1,1,32768]{2,1,0:T(1,128)} %param.17) | copy-start | bytes 393220
  39.8 47.1 %collective-permute-start.2 = (f32[3,5,88,128]{3,2,1,0:T(8,128)}, f32[3,5,88,128]{3,2,1,0:T(8,128)S(1)}, u32[]{:S(2)}, u32[]{:S(2)}) collective-permute-start(f32[3,5,88,128]{3,2,1,0:T(8,128)} %get-tuple-element.13), channel_id=1, source_target_pairs={{0,1},{1,2},{2,3},{3,4},{4,5},{5,6},{6,7},{7,0},{8,9},{9,10},{10,1... | collective-permute-start | bytes 2027528 | tf_op jit(solution)/shard_map/ppermute | solution.py:494
  41.0 45.9 %collective-permute-start.3 = (f32[3,5,88,128]{3,2,1,0:T(8,128)}, f32[3,5,88,128]{3,2,1,0:T(8,128)S(1)}, u32[]{:S(2)}, u32[]{:S(2)}) collective-permute-start(f32[3,5,88,128]{3,2,1,0:T(8,128)} %get-tuple-element.14), channel_id=1, source_target_pairs={{1,0},{2,1},{3,2},{4,3},{5,4},{6,5},{7,6},{0,7},{9,8},{10,9},{11,1... | collective-permute-start | bytes 2027528 | tf_op jit(solution)/shard_map/ppermute | solution.py:495
  61.4 23.6 %copy-start.6 = (s32[32768]{0:T(1024)}, s32[32768]{0:T(1024)S(1)}, u32[]{:S(2)}) copy-start(s32[32768]{0:T(1024)S(1)} %get-tuple-element.16) | copy-start | bytes 393220
  86.9 1.1 copy-start.4
  230.8 48.9 %copy-start.5 = (f32[288,32]{1,0:T(8,128)S(1)}, f32[288,32]{1,0:T(8,128)}, u32[]{:S(2)}) copy-start(f32[288,32]{1,0:T(8,128)} %fixed.1) | copy-start | bytes 110596
  230.8 60.8 %copy-start.11 = (f32[3,32]{1,0:T(4,128)S(1)}, f32[3,32]{1,0:T(4,128)}, u32[]{:S(2)}) copy-start(f32[3,32]{1,0:T(4,128)} %param.15) | copy-start | bytes 1156
  230.8 60.8 %copy-start.12 = (f32[3,32]{1,0:T(4,128)S(1)}, f32[3,32]{1,0:T(4,128)}, u32[]{:S(2)}) copy-start(f32[3,32]{1,0:T(4,128)} %param.16) | copy-start | bytes 1156
  280.9 3.8 %collective-permute-start.4 = (f32[27,3,32]{2,1,0:T(4,128)S(1)}, f32[27,3,32]{2,1,0:T(4,128)S(1)}, u32[]{:S(2)}, u32[]{:S(2)}) collective-permute-start(f32[27,3,32]{2,1,0:T(4,128)S(1)} %get-tuple-element.32), channel_id=1, source_target_pairs={{8,0},{16,8},{24,16},{0,24},{9,1},{17,9},{25,17},{1,25},{10,2},{18... | collective-permute-start | bytes 31112 | tf_op jit(solution)/shard_map/ppermute | solution.py:540
  281.6 3.0 collective-permute-start.5
  284.7 2.6 collective-permute-start.6
  286.3 5.3 %collective-permute-start.7 = (f32[27,32]{1,0:T(8,128)S(1)}, f32[27,32]{1,0:T(8,128)S(1)}, u32[]{:S(2)}, u32[]{:S(2)}) collective-permute-start(f32[27,32]{1,0:T(8,128)S(1)} %bitcast.90), channel_id=1, source_target_pairs={{0,1},{1,2},{2,3},{3,4},{4,5},{5,6},{6,7},{7,0},{8,9},{9,10},{10,1... | collective-permute-start | bytes 10376 | tf_op jit(solution)/shard_map/ppermute | solution.py:543
  291.8 5.2 %collective-permute-start.8 = (f32[6,32]{1,0:T(8,128)S(1)}, f32[6,32]{1,0:T(8,128)S(1)}, u32[]{:S(2)}, u32[]{:S(2)}) collective-permute-start(f32[6,32]{1,0:T(8,128)S(1)} %get-tuple-element.40), channel_id=1, source_target_pairs={{0,1},{1,2},{2,3},{3,4},{4,5},{5,6},{6,7},{7,0},{8,9},{9,10},{10,1... | collective-permute-start | bytes 2312 | tf_op jit(solution)/shard_map/ppermute | solution.py:561
  291.9 5.1 %collective-permute-start.9 = (f32[6,32]{1,0:T(8,128)S(1)}, f32[6,32]{1,0:T(8,128)S(1)}, u32[]{:S(2)}, u32[]{:S(2)}) collective-permute-start(f32[6,32]{1,0:T(8,128)S(1)} %get-tuple-element.40), channel_id=1, source_target_pairs={{1,0},{2,1},{3,2},{4,3},{5,4},{6,5},{7,6},{0,7},{9,8},{10,9},{11,1... | collective-permute-start | bytes 2312 | tf_op jit(solution)/shard_map/ppermute | solution.py:561
  297.0 5.5 %collective-permute-start.10 = (f32[6,3,32]{2,0,1:T(8,128)S(1)}, f32[6,3,32]{2,0,1:T(8,128)S(1)}, u32[]{:S(2)}, u32[]{:S(2)}) collective-permute-start(f32[6,3,32]{2,0,1:T(8,128)S(1)} %get-tuple-element.38), channel_id=1, source_target_pairs={{0,8},{8,16},{16,24},{24,0},{1,9},{9,17},{17,25},{25,1},{2,10},{10... | collective-permute-start | bytes 6920 | tf_op jit(solution)/shard_map/ppermute | solution.py:564
  301.5 3.2 %collective-permute-start.11 = (f32[6,3,32]{2,0,1:T(8,128)S(1)}, f32[6,3,32]{2,0,1:T(8,128)S(1)}, u32[]{:S(2)}, u32[]{:S(2)}) collective-permute-start(f32[6,3,32]{2,0,1:T(8,128)S(1)} %get-tuple-element.38), channel_id=1, source_target_pairs={{8,0},{16,8},{24,16},{0,24},{9,1},{17,9},{25,17},{1,25},{10,2},{18... | collective-permute-start | bytes 6920 | tf_op jit(solution)/shard_map/ppermute | solution.py:564
  (1 other events, 0.8 us)

commit v2 on v1

--- a/solution.py
+++ b/solution.py
@@ -58,7 +58,7 @@
     return (rows + lanes_of(shape)) % 2 == 0
 
 
-def pack_kernel(pot, charge, eps, low, high, split, to_right, to_left):
+def pack_kernel(pot, charge, eps, low, high, split, to_right, to_left, edges):
     depth, wide, _ = pot.shape
     layers = depth // 2
     last = FIRST + wide
@@ -92,24 +92,31 @@
 
     rows = slice(FIRST - HALO, last + HALO)
     lane = lanes_of((wide + 2 * HALO, 128))
+    early = lane % SLOT < HALO
+    slot_of = [(lane >= SLOT * g) & (lane < SLOT * (g + 1)) for g in range(GROUPS)]
+
+    def gather_edges(n, carry):
+        f = n // GROUPS
+        i = n % GROUPS
+        for c in range(2):
+            value = jnp.zeros((wide + 2 * HALO, 128), F32)
+            for g in range(GROUPS):
+                field = split[2 * f + c, i + GROUPS * g, rows, :]
+                value = jnp.where(slot_of[g], roll(field, SLOT * g + HALO), value)
+            edges[c, n] = value
+        return carry
+
+    lax.fori_loop(0, 3 * GROUPS, gather_edges, 0)
+
+    middle = lane - 2 * (lane % SLOT) + SLOT - 1
+    near, same, far = [jnp.clip(middle + n * HALO, 0, 127) for n in (-1, 0, 1)]
 
     def strips(n, carry):
         f = n // GROUPS
         i = n % GROUPS
-        right = jnp.zeros((wide + 2 * HALO, 128), F32)
-        left = jnp.zeros((wide + 2 * HALO, 128), F32)
-        for g in range(GROUPS):
-            red = split[2 * f, i + GROUPS * g, rows, :]
-            black = split[2 * f + 1, i + GROUPS * g, rows, :]
-            base = SLOT * g
-            in_red = (lane >= base) & (lane < base + HALO)
-            in_black = (lane >= base + HALO) & (lane < base + SLOT)
-            right = jnp.where(in_red, roll(red, base + HALO), right)
-            right = jnp.where(in_black, roll(black, base + SLOT), right)
-            left = jnp.where(in_red, roll(red, base), left)
-            left = jnp.where(in_black, roll(black, base + HALO), left)
-        to_right[f, i] = right
-        to_left[f, i] = left
+        red, black = edges[0, n], edges[1, n]
+        to_right[f, i] = jnp.where(early, lane_pick(red, near), lane_pick(black, same))
+        to_left[f, i] = jnp.where(early, lane_pick(red, same), lane_pick(black, far))
         return carry
 
     lax.fori_loop(0, 3 * GROUPS, strips, 0)
@@ -126,9 +133,8 @@
     at_0 = lane == 0
     at_127 = lane == 127
     in_slot = lane % SLOT
-    in_left = in_slot < HALO
-    slot_left = in_slot == HALO - 1
-    slot_right = in_slot == HALO
+    slot_east = in_slot == HALO - 1
+    slot_west = in_slot == HALO
     pick = [(lane == SLOT * g + HALO - 1) | (lane == SLOT * g + HALO) for g in range(GROUPS)]
 
     zero = jnp.zeros((rows + 2 * MARGIN, 128), F32)
@@ -160,7 +166,7 @@
     first = FIRST - HALO
     high = wide + 2 * HALO
     wide_lane = lanes_of((high, 128))
-    wide_left = wide_lane % SLOT < HALO
+    wide_first = wide_lane % SLOT < HALO
     wide_used = wide_lane < SLOT * GROUPS
     for c in range(2):
         for i in range(GROUPS + 2):
@@ -173,8 +179,8 @@
         for i in range(GROUPS):
             west = from_left[f, i]
             east = from_right[f, i]
-            red = jnp.where(wide_left, west, roll(east, HALO))
-            black = jnp.where(wide_left, roll(west, -HALO), east)
+            red = jnp.where(wide_first, east, roll(west, HALO))
+            black = jnp.where(wide_first, roll(east, -HALO), west)
             fill = 1.0 if f == 2 else 0.0
             red = jnp.where(wide_used, red, fill)
             black = jnp.where(wide_used, black, fill)
@@ -220,19 +226,19 @@
                 jnp.where(up, src_a[other, k + 2, rs, :], src_a[other, k, rs, :]),
                 src_a[other, k + 1, rm, :],
                 src_a[other, k + 1, rp, :],
-                roll(jnp.where(at_127, halo, here), 1),
-                roll(jnp.where(at_0, halo, here), -1),
+                jnp.where(at_0, halo, roll(here, 1)),
+                jnp.where(at_127, halo, roll(here, -1)),
             ))
             if body_b is not None:
                 edge = jnp.where(pick[g], roll(here, SLOT * g + HALO), edge)
         if body_b is not None:
             body_b((
                 side,
-                jnp.where(up, src_b[other, i + 2, rs, :], src_b[other, i, rs, :]),
+                jnp.where(up, src_b[other, i, rs, :], src_b[other, i + 2, rs, :]),
                 src_b[other, i + 1, rm, :],
                 src_b[other, i + 1, rp, :],
-                roll(jnp.where(slot_left, edge, side), 1),
-                roll(jnp.where(slot_right, edge, side), -1),
+                jnp.where(slot_east, edge, roll(side, -1)),
+                jnp.where(slot_west, edge, roll(side, 1)),
             ))
 
     def coefficients(own, charge, sides):
@@ -321,19 +327,29 @@
     return arms, w
 
 
-def store_split(stage, total, n, value):
-    coarse = value.astype(jnp.bfloat16).astype(F32)
-    stage[n] = coarse
-    stage[total + n] = value - coarse
+def store_term(stage, n, value):
+    stage[8 * n:8 * n + 8, :] = value
 
 
 def add_by_slot(stage, slot, width):
-    slots = lax.broadcasted_iota(jnp.int32, (width, 128), 0)
+    total = stage.shape[0] // 8
+    fine = slot & 15
+    coarse = slot >> 4
+    small = lax.broadcasted_iota(jnp.int32, (16, 128), 0)
     hot, terms = [], []
     for s in range(8):
-        row = jnp.broadcast_to(slot[s:s + 1, :], (width, 128))
-        hot.append((row == slots).astype(F32).astype(jnp.bfloat16))
-        terms.append(stage[:, s, :].astype(jnp.bfloat16))
+        match = (jnp.broadcast_to(fine[s:s + 1, :], (16, 128)) == small).astype(F32)
+        match = match.astype(jnp.bfloat16)
+        part = jnp.broadcast_to(coarse[s:s + 1, :].astype(F32), (16, 128)).astype(jnp.bfloat16)
+        none = jnp.zeros((16, 128), jnp.bfloat16)
+        hot.append(jnp.concatenate(
+            [jnp.where(part == m, match, none) for m in range(width // 16)], axis=0
+        ))
+        value = stage[pl.ds(s, total, stride=8), :]
+        head = value.astype(jnp.bfloat16)
+        terms.append(jnp.concatenate(
+            [head.astype(F32), value - head.astype(F32)], axis=0
+        ).astype(jnp.bfloat16))
     return lax.dot_general(
         jnp.concatenate(hot, axis=1),
         jnp.concatenate(terms, axis=1),
@@ -344,10 +360,9 @@
 
 def fixed_kernel(slots, dirs, pops, rb, table, out, stage, acc, *, width):
     acc[...] = jnp.zeros_like(acc)
-    total = stage.shape[0] // 2
+    total = stage.shape[0] // 8
     for n in range(6 + len(PAIRS), total):
-        stage[n] = jnp.zeros((8, 128), F32)
-        stage[total + n] = jnp.zeros((8, 128), F32)
+        store_term(stage, n, jnp.zeros((8, 128), F32))
 
     def block(b, carry):
         rs = pl.ds(pl.multiple_of(8 * b, 8), 8)
@@ -355,9 +370,9 @@
         twice = 2.0 * pops[rs, :]
         weighted = [w * arm for arm in arms]
         for n in range(6):
-            store_split(stage, total, n, twice * arms[n])
+            store_term(stage, n, twice * arms[n])
         for n, (a, d) in enumerate(PAIRS):
-            store_split(stage, total, 6 + n, weighted[a] * arms[d])
+            store_term(stage, 6 + n, weighted[a] * arms[d])
         acc[...] += add_by_slot(stage, slots[rs, :], width)
         return carry
 
@@ -365,45 +380,61 @@
     out[...] = acc[:, 0:total] + acc[:, total:]
 
 
-def press_kernel(low, high, keys, rb, table, press, out, stage, acc, *, width):
+BATCH = 4
+AHEAD = 4
+
+
+def press_kernel(low, passes, keys, rb0, rb1, rb2, table, press, out, stage, acc, *, width):
     acc[...] = jnp.zeros_like(acc)
-    total = stage.shape[0] // 2
-    for n in range(6, total):
-        stage[n] = jnp.zeros((8, 128), F32)
-        stage[total + n] = jnp.zeros((8, 128), F32)
-
-    def block(b, carry):
-        rs = pl.ds(pl.multiple_of(8 * b, 8), 8)
-        key = keys[rs, :]
-        place = (key >> KEY_BITS) + (1 << 18)
-        code = key & ((1 << KEY_BITS) - 1)
-        row = place >> 7
-        column = place & 127
-        slot = jnp.floor((code.astype(F32) + 0.5) * (1.0 / 18.0)).astype(jnp.int32)
-        direction = code - 18 * slot
+    for n in range(6, stage.shape[0] // 8):
+        store_term(stage, n, jnp.zeros((8, 128), F32))
+    limit = press.shape[0] - 1
+    line = lax.broadcasted_iota(jnp.int32, (8, 128), 0)
+
+    def batch(b, carry):
+        spots = [pl.ds(pl.multiple_of(8 * (BATCH * b + j), 8), 8) for j in range(BATCH)]
+        columns, offsets, starts = [], [], []
+        for j in range(BATCH):
+            place = (keys[spots[j], :] >> KEY_BITS) + (1 << 18)
+            start = [low[8 * (BATCH * b + j) + s] for s in range(8)]
+            first = jnp.zeros((8, 128), jnp.int32)
+            for s in range(8):
+                first = jnp.where(line == s, start[s], first)
+            columns.append(place & 127)
+            offsets.append((place >> 7) - first)
+            starts.append(start)
 
         def look(m, found):
-            base = pl.multiple_of(8 * m, 8)
-            ahead = row - base
-            for s in range(8):
-                line = jnp.broadcast_to(press[pl.ds(base + s, 1), :], (8, 128))
-                found = jnp.where(ahead == s, lane_pick(line, column), found)
-            return found
-
-        q = lax.fori_loop(low[b], high[b] + 1, look, jnp.zeros((8, 128), F32))
-        arms, w = geometry(direction, [rb[n][rs, :] for n in range(3)], table)
-        wq = w * q
-        for n in range(6):
-            store_split(stage, total, n, wq * arms[n])
-        acc[...] += add_by_slot(stage, slot, width)
-        return carry
-
-    lax.fori_loop(0, keys.shape[0] // 8, block, 0)
+            found = list(found)
+            for j in range(BATCH):
+                for t in range(AHEAD):
+                    step = AHEAD * m + t
+                    window = jnp.zeros((8, 128), F32)
+                    for s in range(8):
+                        row = press[pl.ds(jnp.minimum(starts[j][s] + step, limit), 1), :]
+                        window = jnp.where(line == s, jnp.broadcast_to(row, (8, 128)), window)
+                    value = lane_pick(window, columns[j])
+                    found[j] = jnp.where(offsets[j] == step, value, found[j])
+            return tuple(found)
+
+        found = lax.fori_loop(
+            0, passes[b], look, tuple(jnp.zeros((8, 128), F32) for _ in range(BATCH))
+        )
+        for j in range(BATCH):
+            rs = spots[j]
+            code = keys[rs, :] & ((1 << KEY_BITS) - 1)
+            slot = jnp.floor((code.astype(F32) + 0.5) * (1.0 / 18.0)).astype(jnp.int32)
+            direction = code - 18 * slot
+            arms, w = geometry(direction, [rb0[rs, :], rb1[rs, :], rb2[rs, :]], table)
+            wq = w * found[j]
+            for n in range(6):
+                store_term(stage, n, wq * arms[n])
+            acc[...] += add_by_slot(stage, slot, width)
+        return carry
+
+    lax.fori_loop(0, keys.shape[0] // (8 * BATCH), batch, 0)
+    total = stage.shape[0] // 8
     out[...] = acc[:, 0:total] + acc[:, total:]
-
-
-def press_entry(low, high, keys, rb0, rb1, rb2, table, press, out, stage, acc, *, width):
-    press_kernel(low, high, keys, (rb0, rb1, rb2), table, press, out, stage, acc, width=width)
 
 
 def reflect_kernel(slots, dirs, pops, rb, table, motion, out):
@@ -477,10 +508,14 @@
         (key.reshape(-1), rb[0].reshape(-1), rb[1].reshape(-1), rb[2].reshape(-1)),
         num_keys=1, is_stable=False,
     )
+    keys, rb0, rb1, rb2, low, high = lax.optimization_barrier((keys, rb0, rb1, rb2, low, high))
     keys = keys.reshape(lines, 128)
     table = direction_table()
-    place_rows = (keys.reshape(-1, 1024)[:, ::1023] >> KEY_BITS) + (1 << 18)
-    bounds = jnp.minimum(place_rows // 1024, depth * wide // 8 - 1)
+    table_rows = ((keys >> KEY_BITS) + (1 << 18)) >> 7
+    row_low = jnp.minimum(table_rows[:, 0], depth * wide - 1)
+    row_high = jnp.max(jnp.where(table_rows < depth * wide, table_rows, 0), axis=1)
+    span = jnp.max((row_high - row_low + 1).reshape(-1, 8 * BATCH), axis=1)
+    passes = (jnp.maximum(span, 0) + AHEAD - 1) // AHEAD
 
     split, to_right, to_left = pl.pallas_call(
         pack_kernel,
@@ -490,6 +525,7 @@
             jax.ShapeDtypeStruct((3, GROUPS, wide + 2 * HALO, 128), F32),
         ),
         in_specs=vmem(5), out_specs=tuple(vmem(3)), compiler_params=PARAMS, name="pack",
+        scratch_shapes=[pltpu.VMEM((2, 3 * GROUPS, wide + 2 * HALO, 128), F32)],
     )(potential_start, charge, eps_field, low, high)
     from_left = lax.ppermute(to_right, "gy", fy)
     from_right = lax.ppermute(to_left, "gy", by)
@@ -499,7 +535,7 @@
         functools.partial(fixed_kernel, width=width),
         out_shape=jax.ShapeDtypeStruct((width, terms), F32),
         in_specs=vmem(5), out_specs=vmem(1)[0],
-        scratch_shapes=[pltpu.VMEM((2 * terms, 8, 128), F32), pltpu.VMEM((width, 2 * terms), F32)],
+        scratch_shapes=[pltpu.VMEM((8 * terms, 128), F32), pltpu.VMEM((width, 2 * terms), F32)],
         compiler_params=PARAMS, name="fixed",
         cost_estimate=pl.CostEstimate(flops=10**9, bytes_accessed=2 * 10**7, transcendentals=0),
     )(slots, dirs, pops, rb, table)
@@ -523,13 +559,13 @@
 
     smem = pl.BlockSpec(memory_space=pltpu.SMEM)
     pressed = pl.pallas_call(
-        functools.partial(press_entry, width=width),
+        functools.partial(press_kernel, width=width),
         out_shape=jax.ShapeDtypeStruct((width, 8), F32),
         in_specs=[smem, smem] + vmem(6), out_specs=vmem(1)[0],
-        scratch_shapes=[pltpu.VMEM((16, 8, 128), F32), pltpu.VMEM((width, 16), F32)],
+        scratch_shapes=[pltpu.VMEM((64, 128), F32), pltpu.VMEM((width, 16), F32)],
         compiler_params=PARAMS, name="press",
     )(
-        bounds[:, 0], bounds[:, 1], keys, rb0.reshape(lines, 128), rb1.reshape(lines, 128),
+        row_low, passes, keys, rb0.reshape(lines, 128), rb1.reshape(lines, 128),
         rb2.reshape(lines, 128), table, press.reshape(depth * wide, 128),
     )
 

time: 311 us -> 173 us (0.56)
  Pallas kernels: 231 us -> 80.4 us
  waiting for transfers between devices: 28.8 us -> 37.6 us
    pallas_call x1, Pallas kernels: 143 us -> 32.3 us  [shards(): pl.pallas_call(relax_kernel, out_shape=(jax.ShapeDtypeStruct(charge.shape...]
    pallas_call x1, Pallas kernels: 48.9 us -> 16.9 us  [shards(): pl.pallas_call(functools.partial(press_kernel, width=width), out_shape=ja...]
    ppermute x1, waiting for transfers between devices: 0.01 us -> 24.7 us  [shards(): from_left = lax.ppermute(to_right, 'gy', fy)]
    ppermute x1, waiting for transfers between devices: 18.6 us -> 0.01 us  [shards(): high = lax.ppermute(edge(slice(0, HALO)), 'gx', bx)]
    pallas_call x1, Pallas kernels: 22.5 us -> 14.4 us  [shards(): pl.pallas_call(functools.partial(fixed_kernel, width=width), out_shape=ja...]
    optimization_barrier x0 -> x2, local copies, waits for them, and re-layouts: none -> 3.82 us  [shards(): lax.optimization_barrier((keys, rb0, rb1, rb2, low, high))]
    ppermute x2 -> x0, local copies, waits for them, and re-layouts: 3.8 us -> none  [the longest x1 2.46 us: shards(): low = lax.ppermute(edge(slice(wide - HALO, wide)), 'gx', fx)]
  transfers between devices with their start and end apart: 12 -> 12, of which waited for: 6 -> 8; matrix products, arithmetic and copies ran while one was open for 7% -> 13% of each run, Pallas kernels for 7% -> 8%
where the time goes in v2:
time: 173 us
  Pallas kernels  80.4 us (46%)
  waiting for transfers between devices  37.6 us (22%)
  other arithmetic  22.2 us (13%)
  starting transfers between devices  21.8 us (13%)
  local copies, waits for them, and re-layouts  9.9 us (6%)
    pallas_call x1, Pallas kernels, shards(): pl.pallas_call(relax_kernel, out_shape=(jax.ShapeDtypeStruct(charge.shape...  32.3 us
    ppermute x1, waiting for transfers between devices, shards(): from_left = lax.ppermute(to_right, 'gy', fy)  24.7 us
    pallas_call x1, Pallas kernels, shards(): pl.pallas_call(functools.partial(press_kernel, width=width), out_shape=ja...  16.9 us
    sort x1, other arithmetic, shards(): lax.sort((key.reshape(-1), rb[0].reshape(-1), rb[1].reshape(-1), rb[2].re...  16.7 us
    pallas_call x1, Pallas kernels, shards(): pl.pallas_call(functools.partial(fixed_kernel, width=width), out_shape=ja...  14.4 us
    pallas_call x1, Pallas kernels, shards(): pl.pallas_call(pack_kernel, out_shape=(jax.ShapeDtypeStruct((6, layers +...  11.5 us
    pallas_call x1, Pallas kernels, shards(): pl.pallas_call(reflect_kernel, out_shape=jax.ShapeDtypeStruct((lines, 128...  5.27 us
    ppermute x1, waiting for transfers between devices, shards(): lax.ppermute(mid[:, 2], 'gy', fy)  4.42 us
  transfers between devices with their start and end apart: 12, of which 8 were waited for; matrix products, arithmetic and copies ran while one was open for 13% of the time, Pallas kernels for 8%

profile of v2, /device:TPU:1, one launch (start us, length us, event | category | flops | bytes accessed | tf_op | source)
XLA Modules:
  0.0 172.7 jit_solution(11357256263561648029)
XLA Ops:
  0.7 1.3 fusion.51
  3.3 2.7 %collective-permute-start = (f32[3,48,12,128]{3,1,2,0:T(8,128)S(1)}, f32[3,48,12,128]{3,1,2,0:T(8,128)}, u32[]{:S(2)}, u32[]{:S(2)}) collective-permute-start(f32[3,48,12,128]{3,1,2,0:T(8,128)S(1)} %pad_maximum_fusion), channel_id=1, source_target_pairs={{0,8},{8,16},{16,24},{24,0},{1,9},{9,17},{17,25},{25,1},{2,10},{10... | collective-permute-start | bytes 2654216 | tf_op jit(solution)/shard_map/ppermute | solution.py:486
  6.6 1.0 fusion.24.slots
  7.6 14.4 %fixed.1 = f32[288,32]{1,0:T(8,128)} custom-call(s32[256,128]{1,0:T(8,128)} %fusion.24.slots, s32[256,128]{1,0:T(8,128)} %bitcast.83, f32[256,128]{1,0:T(8,128)} %bitcast.89, f32[3,256,128]{2,1,0:T(8,128)} %bitcast.74, f32[4,8,128]{2,1,0:T(8,128)} %constant.136.clone.table), custom_call_target="tpu_custom_call" | custom-call | flops 1000000000 | bytes 20000000 | tf_op jit(solution)/shard_map/fixed/pallas_call | solution.py:534
  23.1 1.2 add_multiply_fusion
  24.8 16.7 %sort.27 = (s32[32768]{0:T(1024)S(1)}, f32[32768]{0:T(1024)}, f32[32768]{0:T(1024)}, f32[32768]{0:T(1024)}) sort(s32[32768]{0:T(1024)S(1)} %fusion.13, f32[32768]{0:T(1024)S(1)} %bitcast.82, f32[32768]{0:T(1024)S(1)} %bitcast.81, f32[32768]{0:T(1024)S(1)} %bitcast.80), dimensions={0}, to_apply=%region_0.1 | sort | flops 491520 | bytes 1048576 | tf_op jit(solution)/shard_map/sort | solution.py:507
  41.5 2.5 %copy.42.low = f32[3,48,12,128]{3,2,1,0:T(8,128)} copy(f32[3,48,12,128]{3,1,2,0:T(8,128)} %collective-permute-done) | data formatting | bytes 1769472 | tf_op jit(solution)/shard_map/optimization_barrier | solution.py:511
  44.0 1.3 copy.43.high
  45.3 11.5 %pack.1 = (f32[6,25,96,128]{3,2,1,0:T(8,128)}, f32[3,5,88,128]{3,2,1,0:T(8,128)}, f32[3,5,88,128]{3,2,1,0:T(8,128)}) custom-call(f32[48,64,128]{2,1,0:T(8,128)} %pot.1, f32[48,64,128]{2,1,0:T(8,128)} %charge.1, bf16[48,64,128]{2,1,0:T(8,128)(2,1)} %eps.1, f32[3,48,12,128]{3,2,1,0:T(8,128)} %copy.42.low, f32[3,48,12,128]{3,2,1,0:T(8,128)} %copy.43.high), custom_call_target="tpu_custom_call" | custom-call | tf_op jit(solution)/shard_map/pack/pallas_call | solution.py:520
  56.8 1.2 collective-permute-start.2
  58.0 3.0 %collective-permute-start.3 = (f32[3,5,88,128]{3,2,1,0:T(8,128)}, f32[3,5,88,128]{3,2,1,0:T(8,128)S(1)}, u32[]{:S(2)}, u32[]{:S(2)}) collective-permute-start(f32[3,5,88,128]{3,2,1,0:T(8,128)} %get-tuple-element.26), channel_id=1, source_target_pairs={{1,0},{2,1},{3,2},{4,3},{5,4},{6,5},{7,6},{0,7},{9,8},{10,9},{11,1... | collective-permute-start | bytes 2027528 | tf_op jit(solution)/shard_map/ppermute | solution.py:531
  62.2 24.7 %collective-permute-done.2.from_left = f32[3,5,88,128]{3,2,1,0:T(8,128)S(1)} collective-permute-done((f32[3,5,88,128]{3,2,1,0:T(8,128)}, f32[3,5,88,128]{3,2,1,0:T(8,128)S(1)}, u32[]{:S(2)}, u32[]{:S(2)}) %collective-permute-start.2) | collective-permute-done | bytes 675872 | tf_op jit(solution)/shard_map/ppermute | solution.py:530
  86.9 1.8 %collective-permute-done.3.from_right = f32[3,5,88,128]{3,2,1,0:T(8,128)S(1)} collective-permute-done((f32[3,5,88,128]{3,2,1,0:T(8,128)}, f32[3,5,88,128]{3,2,1,0:T(8,128)S(1)}, u32[]{:S(2)}, u32[]{:S(2)}) %collective-permute-start.3) | collective-permute-done | bytes 675872 | tf_op jit(solution)/shard_map/ppermute | solution.py:531
  89.5 32.3 %relax.1 = (f32[48,64,128]{2,1,0:T(8,128)}, f32[48,64,128]{2,1,0:T(8,128)}) custom-call(f32[6,25,96,128]{3,2,1,0:T(8,128)} %get-tuple-element.24.split, f32[3,5,88,128]{3,2,1,0:T(8,128)} %copy-done.3, f32[3,5,88,128]{3,2,1,0:T(8,128)} %copy-done.4), custom_call_target="tpu_custom_call" | custom-call | tf_op jit(solution)/shard_map/relax/pallas_call | solution.py:544
  121.9 16.9 %press.1 = f32[288,8]{1,0:T(8,128)} custom-call(s32[256]{0:T(256)} %copy-done.12, s32[8]{0:T(128)} %and_select_fusion.passes, s32[256,128]{1,0:T(8,128)} %bitcast.76, f32[256,128]{1,0:T(8,128)} %bitcast.86, f32[256,128]{1,0:T(8,128)} %bitcast.87, f32[256,128]{1,0:T(8,128)} %bitcast.88, f32[4,8,128]{2,1,0:T(8,128)} %constant.136.clone.table, f32[3072,128]{1,0:T(8,128)} %bitcast.73), custom_call_target="tpu_custom_call" | custom-call | tf_op jit(solution)/shard_map/press/pallas_call | solution.py:561
  140.0 1.7 collective-permute-start.4
  141.6 1.5 collective-permute-start.5
  143.2 2.3 %collective-permute-done.4 = f32[27,3,32]{2,1,0:T(4,128)S(1)} collective-permute-done((f32[27,3,32]{2,1,0:T(4,128)S(1)}, f32[27,3,32]{2,1,0:T(4,128)S(1)}, u32[]{:S(2)}, u32[]{:S(2)}) %collective-permute-start.4) | collective-permute-done | bytes 10400 | tf_op jit(solution)/shard_map/ppermute | solution.py:576
  145.5 3.2 %collective-permute-start.6 = (f32[27,32]{1,0:T(8,128)S(1)}, f32[27,32]{1,0:T(8,128)S(1)}, u32[]{:S(2)}, u32[]{:S(2)}) collective-permute-start(f32[27,32]{1,0:T(8,128)S(1)} %bitcast.92), channel_id=1, source_target_pairs={{1,0},{2,1},{3,2},{4,3},{5,4},{6,5},{7,6},{0,7},{9,8},{10,9},{11,1... | collective-permute-start | bytes 10376 | tf_op jit(solution)/shard_map/ppermute | solution.py:579
  149.6 4.4 %collective-permute-done.7 = f32[27,32]{1,0:T(8,128)S(1)} collective-permute-done((f32[27,32]{1,0:T(8,128)S(1)}, f32[27,32]{1,0:T(8,128)S(1)}, u32[]{:S(2)}, u32[]{:S(2)}) %collective-permute-start.7) | collective-permute-done | bytes 3488 | tf_op jit(solution)/shard_map/ppermute | solution.py:579
  154.3 4.1 %collective-permute-start.9 = (f32[6,32]{1,0:T(8,128)S(1)}, f32[6,32]{1,0:T(8,128)S(1)}, u32[]{:S(2)}, u32[]{:S(2)}) collective-permute-start(f32[6,32]{1,0:T(8,128)S(1)} %get-tuple-element.52), channel_id=1, source_target_pairs={{1,0},{2,1},{3,2},{4,3},{5,4},{6,5},{7,6},{0,7},{9,8},{10,9},{11,1... | collective-permute-start | bytes 2312 | tf_op jit(solution)/shard_map/ppermute | solution.py:597
  159.4 4.2 %collective-permute-start.10 = (f32[6,3,32]{2,0,1:T(8,128)S(1)}, f32[6,3,32]{2,0,1:T(8,128)S(1)}, u32[]{:S(2)}, u32[]{:S(2)}) collective-permute-start(f32[6,3,32]{2,0,1:T(8,128)S(1)} %get-tuple-element.50), channel_id=1, source_target_pairs={{0,8},{8,16},{16,24},{24,0},{1,9},{9,17},{17,25},{25,1},{2,10},{10... | collective-permute-start | bytes 6920 | tf_op jit(solution)/shard_map/ppermute | solution.py:600
  164.4 2.3 %collective-permute-done.11 = f32[6,3,32]{2,0,1:T(8,128)S(1)} collective-permute-done((f32[6,3,32]{2,0,1:T(8,128)S(1)}, f32[6,3,32]{2,0,1:T(8,128)S(1)}, u32[]{:S(2)}, u32[]{:S(2)}) %collective-permute-start.11) | collective-permute-done | bytes 2336 | tf_op jit(solution)/shard_map/ppermute | solution.py:600
  167.4 5.3 %reflect.1 = f32[256,128]{1,0:T(8,128)} custom-call(s32[256,128]{1,0:T(8,128)} %fusion.24.slots, s32[256,128]{1,0:T(8,128)} %bitcast.84, f32[256,128]{1,0:T(8,128)} %bitcast.90, f32[3,256,128]{2,1,0:T(8,128)} %bitcast.75, f32[4,8,128]{2,1,0:T(8,128)} %constant.136.clone.table, f32[6,3,128]{2,1,0:T(4,128)} %reshape.89.motion), custom_call_target="tpu_custom_call" | custom-call | tf_op jit(solution)/shard_map/reflect/pallas_call | solution.py:604
  (82 shorter events, 10.2 us)
Async XLA Ops:
  0.6 1.7 copy-start
  0.6 1.8 %copy-start.1 = (bf16[48,64,128]{2,1,0:T(8,128)(2,1)S(1)}, bf16[48,64,128]{2,1,0:T(8,128)(2,1)}, u32[]{:S(2)}) copy-start(bf16[48,64,128]{2,1,0:T(8,128)(2,1)} %eps.1) | copy-start | bytes 2359300
  2.9 38.6 %collective-permute-start.1 = (f32[3,48,12,128]{3,1,2,0:T(8,128)S(1)}, f32[3,48,12,128]{3,1,2,0:T(8,128)S(1)}, u32[]{:S(2)}, u32[]{:S(2)}) collective-permute-start(f32[3,48,12,128]{3,1,2,0:T(8,128)S(1)} %pad_maximum_fusion.1), channel_id=1, source_target_pairs={{8,0},{16,8},{24,16},{0,24},{9,1},{17,9},{25,17},{1,25},{10,2},{18... | collective-permute-start | bytes 2654216 | tf_op jit(solution)/shard_map/ppermute | solution.py:487
  3.0 3.0 %copy-start.2 = (f32[3,1,1,32768]{3,2,1,0:T(1,128)S(1)}, f32[3,1,1,32768]{3,2,1,0:T(1,128)}, u32[]{:S(2)}) copy-start(f32[3,1,1,32768]{3,2,1,0:T(1,128)} %param.22) | copy-start | bytes 1179652
  3.2 3.4 %copy-start.7 = (s32[1,1,32768]{2,1,0:T(1,128)S(1)}, s32[1,1,32768]{2,1,0:T(1,128)}, u32[]{:S(2)}) copy-start(s32[1,1,32768]{2,1,0:T(1,128)} %param.18) | copy-start | bytes 393220
  3.3 38.3 %collective-permute-start = (f32[3,48,12,128]{3,1,2,0:T(8,128)S(1)}, f32[3,48,12,128]{3,1,2,0:T(8,128)}, u32[]{:S(2)}, u32[]{:S(2)}) collective-permute-start(f32[3,48,12,128]{3,1,2,0:T(8,128)S(1)} %pad_maximum_fusion), channel_id=1, source_target_pairs={{0,8},{8,16},{16,24},{24,0},{1,9},{9,17},{17,25},{25,1},{2,10},{10... | collective-permute-start | bytes 2654216 | tf_op jit(solution)/shard_map/ppermute | solution.py:486
  7.6 16.7 %copy-start.9 = (s32[1,1,32768]{2,1,0:T(1,128)S(1)}, s32[1,1,32768]{2,1,0:T(1,128)}, u32[]{:S(2)}) copy-start(s32[1,1,32768]{2,1,0:T(1,128)} %param.17) | copy-start | bytes 393220
  7.6 17.1 %copy-start.8 = (f32[1,1,1,32768]{3,2,1,0:T(1,128)S(1)}, f32[1,1,1,32768]{3,2,1,0:T(1,128)}, u32[]{:S(2)}) copy-start(f32[1,1,1,32768]{3,2,1,0:T(1,128)} %get-tuple-element.41) | copy-start | bytes 393220
  41.5 19.6 %copy-start.6 = (s32[32768]{0:T(1024)}, s32[32768]{0:T(1024)S(1)}, u32[]{:S(2)}) copy-start(s32[32768]{0:T(1024)S(1)} %get-tuple-element.28) | copy-start | bytes 393220
  56.8 30.1 %collective-permute-start.2 = (f32[3,5,88,128]{3,2,1,0:T(8,128)}, f32[3,5,88,128]{3,2,1,0:T(8,128)S(1)}, u32[]{:S(2)}, u32[]{:S(2)}) collective-permute-start(f32[3,5,88,128]{3,2,1,0:T(8,128)} %get-tuple-element.25), channel_id=1, source_target_pairs={{0,1},{1,2},{2,3},{3,4},{4,5},{5,6},{6,7},{7,0},{8,9},{9,10},{10,1... | collective-permute-start | bytes 2027528 | tf_op jit(solution)/shard_map/ppermute | solution.py:530
  58.0 30.7 %collective-permute-start.3 = (f32[3,5,88,128]{3,2,1,0:T(8,128)}, f32[3,5,88,128]{3,2,1,0:T(8,128)S(1)}, u32[]{:S(2)}, u32[]{:S(2)}) collective-permute-start(f32[3,5,88,128]{3,2,1,0:T(8,128)} %get-tuple-element.26), channel_id=1, source_target_pairs={{1,0},{2,1},{3,2},{4,3},{5,4},{6,5},{7,6},{0,7},{9,8},{10,9},{11,1... | collective-permute-start | bytes 2027528 | tf_op jit(solution)/shard_map/ppermute | solution.py:531
  61.3 60.6 %copy-start.12 = (s32[256]{0:T(256)}, s32[256]{0:T(256)S(1)}, u32[]{:S(2)}) copy-start(s32[256]{0:T(256)S(1)} %fusion.29.low) | copy-start | bytes 3076
  86.9 1.8 %copy-start.3 = (f32[3,5,88,128]{3,2,1,0:T(8,128)}, f32[3,5,88,128]{3,2,1,0:T(8,128)S(1)}, u32[]{:S(2)}) copy-start(f32[3,5,88,128]{3,2,1,0:T(8,128)S(1)} %collective-permute-done.2.from_left) | copy-start | bytes 2027524
  121.9 16.9 %copy-start.5 = (f32[288,32]{1,0:T(8,128)S(1)}, f32[288,32]{1,0:T(8,128)}, u32[]{:S(2)}) copy-start(f32[288,32]{1,0:T(8,128)} %fixed.1) | copy-start | bytes 110596
  121.9 32.2 %copy-start.10 = (f32[3,32]{1,0:T(4,128)S(1)}, f32[3,32]{1,0:T(4,128)}, u32[]{:S(2)}) copy-start(f32[3,32]{1,0:T(4,128)} %param.15) | copy-start | bytes 1156
  121.9 32.2 %copy-start.11 = (f32[3,32]{1,0:T(4,128)S(1)}, f32[3,32]{1,0:T(4,128)}, u32[]{:S(2)}) copy-start(f32[3,32]{1,0:T(4,128)} %param.16) | copy-start | bytes 1156
  140.0 5.4 %collective-permute-start.4 = (f32[27,3,32]{2,1,0:T(4,128)S(1)}, f32[27,3,32]{2,1,0:T(4,128)S(1)}, u32[]{:S(2)}, u32[]{:S(2)}) collective-permute-start(f32[27,3,32]{2,1,0:T(4,128)S(1)} %get-tuple-element.42), channel_id=1, source_target_pairs={{8,0},{16,8},{24,16},{0,24},{9,1},{17,9},{25,17},{1,25},{10,2},{18... | collective-permute-start | bytes 31112 | tf_op jit(solution)/shard_map/ppermute | solution.py:576
  141.6 3.8 %collective-permute-start.5 = (f32[27,3,32]{2,1,0:T(4,128)S(1)}, f32[27,3,32]{2,1,0:T(4,128)S(1)}, u32[]{:S(2)}, u32[]{:S(2)}) collective-permute-start(f32[27,3,32]{2,1,0:T(4,128)S(1)} %get-tuple-element.43), channel_id=1, source_target_pairs={{0,8},{8,16},{16,24},{24,0},{1,9},{9,17},{17,25},{25,1},{2,10},{10... | collective-permute-start | bytes 31112 | tf_op jit(solution)/shard_map/ppermute | solution.py:577
  145.5 4.1 %collective-permute-start.6 = (f32[27,32]{1,0:T(8,128)S(1)}, f32[27,32]{1,0:T(8,128)S(1)}, u32[]{:S(2)}, u32[]{:S(2)}) collective-permute-start(f32[27,32]{1,0:T(8,128)S(1)} %bitcast.92), channel_id=1, source_target_pairs={{1,0},{2,1},{3,2},{4,3},{5,4},{6,5},{7,6},{0,7},{9,8},{10,9},{11,1... | collective-permute-start | bytes 10376 | tf_op jit(solution)/shard_map/ppermute | solution.py:579
  148.7 5.3 %collective-permute-start.7 = (f32[27,32]{1,0:T(8,128)S(1)}, f32[27,32]{1,0:T(8,128)S(1)}, u32[]{:S(2)}, u32[]{:S(2)}) collective-permute-start(f32[27,32]{1,0:T(8,128)S(1)} %bitcast.93), channel_id=1, source_target_pairs={{0,1},{1,2},{2,3},{3,4},{4,5},{5,6},{6,7},{7,0},{8,9},{9,10},{10,1... | collective-permute-start | bytes 10376 | tf_op jit(solution)/shard_map/ppermute | solution.py:579
  154.2 5.2 %collective-permute-start.8 = (f32[6,32]{1,0:T(8,128)S(1)}, f32[6,32]{1,0:T(8,128)S(1)}, u32[]{:S(2)}, u32[]{:S(2)}) collective-permute-start(f32[6,32]{1,0:T(8,128)S(1)} %get-tuple-element.52), channel_id=1, source_target_pairs={{0,1},{1,2},{2,3},{3,4},{4,5},{5,6},{6,7},{7,0},{8,9},{9,10},{10,1... | collective-permute-start | bytes 2312 | tf_op jit(solution)/shard_map/ppermute | solution.py:597
  154.3 5.1 %collective-permute-start.9 = (f32[6,32]{1,0:T(8,128)S(1)}, f32[6,32]{1,0:T(8,128)S(1)}, u32[]{:S(2)}, u32[]{:S(2)}) collective-permute-start(f32[6,32]{1,0:T(8,128)S(1)} %get-tuple-element.52), channel_id=1, source_target_pairs={{1,0},{2,1},{3,2},{4,3},{5,4},{6,5},{7,6},{0,7},{9,8},{10,9},{11,1... | collective-permute-start | bytes 2312 | tf_op jit(solution)/shard_map/ppermute | solution.py:597
  159.4 5.0 %collective-permute-start.10 = (f32[6,3,32]{2,0,1:T(8,128)S(1)}, f32[6,3,32]{2,0,1:T(8,128)S(1)}, u32[]{:S(2)}, u32[]{:S(2)}) collective-permute-start(f32[6,3,32]{2,0,1:T(8,128)S(1)} %get-tuple-element.50), channel_id=1, source_target_pairs={{0,8},{8,16},{16,24},{24,0},{1,9},{9,17},{17,25},{25,1},{2,10},{10... | collective-permute-start | bytes 6920 | tf_op jit(solution)/shard_map/ppermute | solution.py:600
  163.6 3.1 %collective-permute-start.11 = (f32[6,3,32]{2,0,1:T(8,128)S(1)}, f32[6,3,32]{2,0,1:T(8,128)S(1)}, u32[]{:S(2)}, u32[]{:S(2)}) collective-permute-start(f32[6,3,32]{2,0,1:T(8,128)S(1)} %get-tuple-element.50), channel_id=1, source_target_pairs={{8,0},{16,8},{24,16},{0,24},{9,1},{17,9},{25,17},{1,25},{10,2},{18... | collective-permute-start | bytes 6920 | tf_op jit(solution)/shard_map/ppermute | solution.py:600
  (1 other events, 0.8 us)

commit v3 on v2

--- a/solution.py
+++ b/solution.py
@@ -19,6 +19,9 @@
 SLOT = 2 * HALO
 KEY_BITS = 13
 F32 = jnp.float32
+HALF = jnp.float16
+POT_SCALE = 2.0**14
+CHARGE_SCALE = 2.0**13
 
 VELOCITY = np.array(
     [
@@ -63,13 +66,16 @@
     layers = depth // 2
     last = FIRST + wide
 
+    def strip(source, f, z):
+        return source[pl.ds(f * HALO * depth + z, HALO, stride=depth), :]
+
     def build(k, carry):
         for f, field in enumerate((pot, charge, eps)):
             fill = 1.0 if f == 2 else 0.0
             parts = (
                 (FIRST, field[2 * k].astype(F32), field[2 * k + 1].astype(F32)),
-                (FIRST - HALO, low[f, 2 * k], low[f, 2 * k + 1]),
-                (last, high[f, 2 * k], high[f, 2 * k + 1]),
+                (FIRST - HALO, *(strip(low, f, 2 * k + n) for n in range(2))),
+                (last, *(strip(high, f, 2 * k + n) for n in range(2))),
             )
             for start, even, odd in parts:
                 flat = parity_of(even.shape)
@@ -351,14 +357,14 @@
             [head.astype(F32), value - head.astype(F32)], axis=0
         ).astype(jnp.bfloat16))
     return lax.dot_general(
+        jnp.concatenate(terms, axis=1),
         jnp.concatenate(hot, axis=1),
-        jnp.concatenate(terms, axis=1),
         (((1,), (1,)), ((), ())),
         preferred_element_type=F32,
     )
 
 
-def fixed_kernel(slots, dirs, pops, rb, table, out, stage, acc, *, width):
+def fixed_kernel(slots, dirs, pops, rb, table, out, reach, stage, acc, *, width):
     acc[...] = jnp.zeros_like(acc)
     total = stage.shape[0] // 8
     for n in range(6 + len(PAIRS), total):
@@ -370,6 +376,8 @@
         twice = 2.0 * pops[rs, :]
         weighted = [w * arm for arm in arms]
         for n in range(6):
+            reach[n, rs, :] = jnp.where(slots[rs, :] >= 0, 6.0 * weighted[n], 0.0)
+        for n in range(6):
             store_term(stage, n, twice * arms[n])
         for n, (a, d) in enumerate(PAIRS):
             store_term(stage, 6 + n, weighted[a] * arms[d])
@@ -377,7 +385,7 @@
         return carry
 
     lax.fori_loop(0, slots.shape[0] // 8, block, 0)
-    out[...] = acc[:, 0:total] + acc[:, total:]
+    out[...] = acc[0:total, :] + acc[total:, :]
 
 
 BATCH = 4
@@ -434,13 +442,12 @@
 
     lax.fori_loop(0, keys.shape[0] // (8 * BATCH), batch, 0)
     total = stage.shape[0] // 8
-    out[...] = acc[:, 0:total] + acc[:, total:]
-
-
-def reflect_kernel(slots, dirs, pops, rb, table, motion, out):
+    out[...] = acc[0:total, :] + acc[total:, :]
+
+
+def reflect_kernel(slots, reach, pops, motion, out):
     def block(b, carry):
         rs = pl.ds(pl.multiple_of(8 * b, 8), 8)
-        arms, w = geometry(dirs[rs, :], [rb[n, rs, :] for n in range(3)], table)
         slot = slots[rs, :]
         lane = slot & 127
         part = slot >> 7
@@ -450,8 +457,8 @@
             for h in range(motion.shape[1]):
                 line = jnp.broadcast_to(motion[n, h:h + 1, :], (8, 128))
                 value = jnp.where(part == h, lane_pick(line, lane), value)
-            along += arms[n] * value
-        out[rs, :] = pops[rs, :] - jnp.where(slot >= 0, 6.0 * w * along, 0.0)
+            along += reach[n, rs, :] * value
+        out[rs, :] = pops[rs, :] - along
         return carry
 
     lax.fori_loop(0, slots.shape[0] // 8, block, 0)
@@ -461,6 +468,18 @@
     count = lax.axis_size(axis)
     forward = [(i, (i + 1) % count) for i in range(count)]
     return forward, [(b, a) for a, b in forward]
+
+
+def scales():
+    return jnp.array([POT_SCALE, CHARGE_SCALE, 1.0], F32).reshape(3, 1, 1, 1)
+
+
+def to_half(strips):
+    return (strips * scales()).astype(HALF)
+
+
+def from_half(strips):
+    return strips.astype(F32) * (1.0 / scales())
 
 
 def vmem(n):
@@ -481,7 +500,12 @@
     fy, by = ring("gy")
 
     def edge(part):
-        return jnp.stack([potential_start[:, part], charge[:, part], eps_field[:, part].astype(F32)])
+        strips = jnp.stack([
+            potential_start[:, part] * POT_SCALE,
+            charge[:, part] * CHARGE_SCALE,
+            eps_field[:, part].astype(F32),
+        ])
+        return strips.transpose(0, 2, 1, 3).astype(HALF)
 
     low = lax.ppermute(edge(slice(wide - HALO, wide)), "gx", fx)
     high = lax.ppermute(edge(slice(0, HALO)), "gx", bx)
@@ -526,19 +550,23 @@
         ),
         in_specs=vmem(5), out_specs=tuple(vmem(3)), compiler_params=PARAMS, name="pack",
         scratch_shapes=[pltpu.VMEM((2, 3 * GROUPS, wide + 2 * HALO, 128), F32)],
-    )(potential_start, charge, eps_field, low, high)
-    from_left = lax.ppermute(to_right, "gy", fy)
-    from_right = lax.ppermute(to_left, "gy", by)
+    )(potential_start, charge, eps_field,
+      from_half(low).reshape(-1, 128), from_half(high).reshape(-1, 128))
+    from_left = lax.ppermute(to_half(to_right), "gy", fy)
+    from_right = lax.ppermute(to_half(to_left), "gy", by)
 
     terms = 32
-    fixed = pl.pallas_call(
+    dirs_late, split = lax.optimization_barrier((dirs, split))
+    fixed, reach = pl.pallas_call(
         functools.partial(fixed_kernel, width=width),
-        out_shape=jax.ShapeDtypeStruct((width, terms), F32),
-        in_specs=vmem(5), out_specs=vmem(1)[0],
-        scratch_shapes=[pltpu.VMEM((8 * terms, 128), F32), pltpu.VMEM((width, 2 * terms), F32)],
+        out_shape=(
+            jax.ShapeDtypeStruct((terms, width), F32), jax.ShapeDtypeStruct((6, lines, 128), F32),
+        ),
+        in_specs=vmem(5), out_specs=tuple(vmem(2)),
+        scratch_shapes=[pltpu.VMEM((8 * terms, 128), F32), pltpu.VMEM((2 * terms, width), F32)],
         compiler_params=PARAMS, name="fixed",
         cost_estimate=pl.CostEstimate(flops=10**9, bytes_accessed=2 * 10**7, transcendentals=0),
-    )(slots, dirs, pops, rb, table)
+    )(slots, dirs_late, pops, rb, table)
 
     tall = rows + 2 * MARGIN
     potential, press = pl.pallas_call(
@@ -555,21 +583,21 @@
             pltpu.VMEM((2, 7, GROUPS, rows, 128), F32),
         ],
         compiler_params=PARAMS, name="relax",
-    )(split, from_left, from_right)
+    )(split, from_half(from_left), from_half(from_right))
 
     smem = pl.BlockSpec(memory_space=pltpu.SMEM)
     pressed = pl.pallas_call(
         functools.partial(press_kernel, width=width),
-        out_shape=jax.ShapeDtypeStruct((width, 8), F32),
+        out_shape=jax.ShapeDtypeStruct((8, width), F32),
         in_specs=[smem, smem] + vmem(6), out_specs=vmem(1)[0],
-        scratch_shapes=[pltpu.VMEM((64, 128), F32), pltpu.VMEM((width, 16), F32)],
+        scratch_shapes=[pltpu.VMEM((64, 128), F32), pltpu.VMEM((16, width), F32)],
         compiler_params=PARAMS, name="press",
     )(
         row_low, passes, keys, rb0.reshape(lines, 128), rb1.reshape(lines, 128),
         rb2.reshape(lines, 128), table, press.reshape(depth * wide, 128),
     )
 
-    sums = jnp.concatenate([fixed[:, 0:6] + pressed[:, 0:6], fixed[:, 6:27]], axis=1).T
+    sums = jnp.concatenate([fixed[0:6] + pressed[0:6], fixed[6:27]], axis=0)
     sums = sums.reshape(27, 3, 3, per_tile)
     mid = (
         sums[:, 1]
@@ -604,8 +632,8 @@
     link_out = pl.pallas_call(
         reflect_kernel,
         out_shape=jax.ShapeDtypeStruct((lines, 128), F32),
-        in_specs=vmem(6), out_specs=vmem(1)[0], compiler_params=PARAMS, name="reflect",
-    )(slots, dirs, pops, rb, table, around)
+        in_specs=vmem(4), out_specs=vmem(1)[0], compiler_params=PARAMS, name="reflect",
+    )(slots, reach, pops, around)
     return potential, report, link_out.reshape(link_pop.shape)
 
 

time: 173 us -> 140 us (0.81)
  waiting for transfers between devices: 37.6 us -> 10.6 us
  local copies, waits for them, and re-layouts: 9.9 us -> 3.86 us
  other arithmetic: 22.2 us -> 25.8 us
  Pallas kernels: 80.4 us -> 77.9 us
    ppermute x2, waiting for transfers between devices: 26.5 us -> 0.01 us  [the longest x1 0.01 us: shards(): from_left = lax.ppermute(to_half(to_right), 'gy', fy)]
    optimization_barrier x2 -> x0, local copies, waits for them, and re-layouts: 3.82 us -> none  [shards(): lax.optimization_barrier((keys, rb0, rb1, rb2, low, high))]
    mul x0 -> x2, other arithmetic: none -> 2.77 us  [from_half(): return strips.astype(F32) * (1.0 / scales())]
    convert_element_type x0 -> x3, other arithmetic: none -> 1.79 us  [the longest x1 1.51 us: to_half(): return (strips * scales()).astype(HALF)]
  transfers between devices with their start and end apart: 12 -> 12, of which waited for: 8 -> 6; matrix products, arithmetic and copies ran while one was open for 13% -> 15% of each run, Pallas kernels for 8% -> 10%
where the time goes in v3:
time: 140 us
  Pallas kernels  77.9 us (56%)
  other arithmetic  25.8 us (18%)
  starting transfers between devices  20.8 us (15%)
  waiting for transfers between devices  10.6 us (8%)
  local copies, waits for them, and re-layouts  3.86 us (3%)
    pallas_call x1, Pallas kernels, shards(): pl.pallas_call(relax_kernel, out_shape=(jax.ShapeDtypeStruct(charge.shape...  32.2 us
    sort x1, other arithmetic, shards(): lax.sort((key.reshape(-1), rb[0].reshape(-1), rb[1].reshape(-1), rb[2].re...  16.7 us
    pallas_call x1, Pallas kernels, shards(): pl.pallas_call(functools.partial(press_kernel, width=width), out_shape=ja...  15.4 us
    pallas_call x1, Pallas kernels, shards(): pl.pallas_call(functools.partial(fixed_kernel, width=width), out_shape=(j...  13.7 us
    pallas_call x1, Pallas kernels, shards(): pl.pallas_call(pack_kernel, out_shape=(jax.ShapeDtypeStruct((6, layers +...  11.7 us
    ppermute x1, starting transfers between devices, shards(): lax.ppermute(column, 'gx', fx)  4.96 us
    pallas_call x1, Pallas kernels, shards(): pl.pallas_call(reflect_kernel, out_shape=jax.ShapeDtypeStruct((lines, 128...  4.89 us
    ppermute x1, waiting for transfers between devices, shards(): lax.ppermute(mid[:, 2], 'gy', fy)  4.42 us
  transfers between devices with their start and end apart: 12, of which 6 were waited for; matrix products, arithmetic and copies ran while one was open for 15% of the time, Pallas kernels for 10%

profile of v3, /device:TPU:1, one launch (start us, length us, event | category | flops | bytes accessed | tf_op | source)
XLA Modules:
  0.0 139.9 jit_solution(17910260255147387126)
XLA Ops:
  0.7 1.3 fusion.59
  3.5 2.7 %collective-permute-start = (f16[3,12,48,128]{3,2,1,0:T(8,128)(2,1)S(1)}, f16[3,12,48,128]{3,2,1,0:T(8,128)(2,1)S(1)}, u32[]{:S(2)}, u32[]{:S(2)}) collective-permute-start(f16[3,12,48,128]{3,2,1,0:T(8,128)(2,1)S(1)} %maximum_bitcast_fusion), channel_id=1, source_target_pairs={{0,8},{8,16},{16,24},{24,0},{1,9},{9,17},{17,25},{25,1},{2,10},{10... | collective-permute-start | bytes 1327112 | tf_op jit(solution)/shard_map/ppermute | solution.py:510
  6.9 16.7 %sort.27 = (s32[32768]{0:T(1024)S(1)}, f32[32768]{0:T(1024)}, f32[32768]{0:T(1024)}, f32[32768]{0:T(1024)}) sort(s32[32768]{0:T(1024)S(1)} %fusion.21, f32[32768]{0:T(1024)S(1)} %bitcast.80, f32[32768]{0:T(1024)S(1)} %bitcast.79, f32[32768]{0:T(1024)S(1)} %bitcast.78), dimensions={0}, to_apply=%region_0.1 | sort | flops 491520 | bytes 1048576 | tf_op jit(solution)/shard_map/sort | solution.py:531
  23.6 1.0 fusion.32.slots
  24.7 1.5 %convert_multiply_fusion = (f32[3,12,48,128]{3,2,1,0:T(8,128)}, f32[3,12,48,128]{3,2,1,0:T(8,128)}) fusion(f16[3,12,48,128]{3,2,1,0:T(8,128)(2,1)S(1)} %collective-permute-done.1, f32[3]{0:T(128)S(1)} %copy-done.11, f16[3,12,48,128]{3,2,1,0:T(8,128)(2,1)S(1)} %collective-permute-done), kind=kLoop, calls=%fused_computation | loop fusion | flops 884736 | bytes 2654220 | tf_op jit(solution)/shard_map/mul | solution.py:482
  26.2 11.7 %pack.1 = (f32[6,25,96,128]{3,2,1,0:T(8,128)}, f32[3,5,88,128]{3,2,1,0:T(8,128)}, f32[3,5,88,128]{3,2,1,0:T(8,128)}) custom-call(f32[48,64,128]{2,1,0:T(8,128)} %pot.1, f32[48,64,128]{2,1,0:T(8,128)} %charge.1, bf16[48,64,128]{2,1,0:T(8,128)(2,1)} %eps.1, f32[1728,128]{1,0:T(8,128)} %bitcast.72, f32[1728,128]{1,0:T(8,128)} %bitcast.71), custom_call_target="tpu_custom_call" | custom-call | tf_op jit(solution)/shard_map/pack/pallas_call | solution.py:544
  37.9 1.5 %multiply_convert_fusion = (f16[3,5,88,128]{3,2,1,0:T(8,128)(2,1)S(1)}, f16[3,5,88,128]{3,2,1,0:T(8,128)(2,1)S(1)}) fusion(f32[3,5,88,128]{3,2,1,0:T(8,128)} %get-tuple-element.31, f32[3]{0:T(128)S(1)} %copy-done.12, f32[3,5,88,128]{3,2,1,0:T(8,128)} %get-tuple-element.30), kind=kLoop, calls=%fused_computation.3 | loop fusion | flops 675840 | bytes 2027532 | tf_op jit(solution)/shard_map/convert_element_type | solution.py:478
  39.4 1.3 collective-permute-start.2
  40.7 3.3 %collective-permute-start.3 = (f16[3,5,88,128]{3,2,1,0:T(8,128)(2,1)S(1)}, f16[3,5,88,128]{3,2,1,0:T(8,128)(2,1)S(1)}, u32[]{:S(2)}, u32[]{:S(2)}) collective-permute-start(f16[3,5,88,128]{3,2,1,0:T(8,128)(2,1)S(1)} %get-tuple-element.67), channel_id=1, source_target_pairs={{1,0},{2,1},{3,2},{4,3},{5,4},{6,5},{7,6},{0,7},{9,8},{10,9},{11,1... | collective-permute-start | bytes 1013768 | tf_op jit(solution)/shard_map/ppermute | solution.py:556
  44.2 13.7 %fixed.1 = (f32[32,288]{1,0:T(8,128)}, f32[6,256,128]{2,1,0:T(8,128)}) custom-call(s32[256,128]{1,0:T(8,128)} %fusion.32.slots, s32[256,128]{1,0:T(8,128)} %bitcast.88, f32[256,128]{1,0:T(8,128)} %bitcast.82, f32[3,256,128]{2,1,0:T(8,128)} %bitcast.81, f32[4,8,128]{2,1,0:T(8,128)} %constant.144.clone.table), custom_call_target="tpu_custom_call" | custom-call | flops 1000000000 | bytes 20000000 | tf_op jit(solution)/shard_map/fixed/pallas_call | solution.py:560
  58.1 0.8 slice.209
  59.5 1.3 convert_multiply_fusion.2
  60.8 32.2 %relax.1 = (f32[48,64,128]{2,1,0:T(8,128)}, f32[48,64,128]{2,1,0:T(8,128)}) custom-call(f32[6,25,96,128]{3,2,1,0:T(8,128)} %get-tuple-element.29.split, f32[3,5,88,128]{3,2,1,0:T(8,128)} %get-tuple-element.66.from_left, f32[3,5,88,128]{3,2,1,0:T(8,128)} %get-tuple-element.65.from_right), custom_call_target="tpu_custom_call" | custom-call | tf_op jit(solution)/shard_map/relax/pallas_call | solution.py:572
  93.0 15.4 %press.1 = f32[8,288]{1,0:T(8,128)} custom-call(s32[256]{0:T(256)} %copy-done.10, s32[8]{0:T(128)} %and_select_fusion.passes, s32[256,128]{1,0:T(8,128)} %bitcast.74, f32[256,128]{1,0:T(8,128)} %bitcast.84, f32[256,128]{1,0:T(8,128)} %bitcast.85, f32[256,128]{1,0:T(8,128)} %bitcast.86, f32[4,8,128]{2,1,0:T(8,128)} %constant.144.clone.table, f32[3072,128]{1,0:T(8,128)} %bitcast.73), custom_call_target="tpu_custom_call" | custom-call | tf_op jit(solution)/shard_map/press/pallas_call | solution.py:589
  109.3 1.4 collective-permute-start.4
  111.5 1.8 %collective-permute-done.4 = f32[27,3,32]{2,1,0:T(4,128)S(1)} collective-permute-done((f32[27,3,32]{2,1,0:T(4,128)S(1)}, f32[27,3,32]{2,1,0:T(4,128)S(1)}, u32[]{:S(2)}, u32[]{:S(2)}) %collective-permute-start.4) | collective-permute-done | bytes 10400 | tf_op jit(solution)/shard_map/ppermute | solution.py:604
  113.3 2.2 %collective-permute-start.6 = (f32[27,32]{1,0:T(8,128)S(1)}, f32[27,32]{1,0:T(8,128)S(1)}, u32[]{:S(2)}, u32[]{:S(2)}) collective-permute-start(f32[27,32]{1,0:T(8,128)S(1)} %bitcast.90), channel_id=1, source_target_pairs={{1,0},{2,1},{3,2},{4,3},{5,4},{6,5},{7,6},{0,7},{9,8},{10,9},{11,1... | collective-permute-start | bytes 10376 | tf_op jit(solution)/shard_map/ppermute | solution.py:607
  115.5 0.9 collective-permute-done.6
  116.4 4.4 %collective-permute-done.7 = f32[27,32]{1,0:T(8,128)S(1)} collective-permute-done((f32[27,32]{1,0:T(8,128)S(1)}, f32[27,32]{1,0:T(8,128)S(1)}, u32[]{:S(2)}, u32[]{:S(2)}) %collective-permute-start.7) | collective-permute-done | bytes 3488 | tf_op jit(solution)/shard_map/ppermute | solution.py:607
  121.1 4.1 %collective-permute-start.9 = (f32[6,32]{1,0:T(8,128)S(1)}, f32[6,32]{1,0:T(8,128)S(1)}, u32[]{:S(2)}, u32[]{:S(2)}) collective-permute-start(f32[6,32]{1,0:T(8,128)S(1)} %get-tuple-element.60), channel_id=1, source_target_pairs={{1,0},{2,1},{3,2},{4,3},{5,4},{6,5},{7,6},{0,7},{9,8},{10,9},{11,1... | collective-permute-start | bytes 2312 | tf_op jit(solution)/shard_map/ppermute | solution.py:625
  125.2 1.0 collective-permute-done.8
  126.2 5.0 %collective-permute-start.10 = (f32[6,3,32]{2,0,1:T(8,128)S(1)}, f32[6,3,32]{2,0,1:T(8,128)S(1)}, u32[]{:S(2)}, u32[]{:S(2)}) collective-permute-start(f32[6,3,32]{2,0,1:T(8,128)S(1)} %get-tuple-element.58), channel_id=1, source_target_pairs={{0,8},{8,16},{16,24},{24,0},{1,9},{9,17},{17,25},{25,1},{2,10},{10... | collective-permute-start | bytes 6920 | tf_op jit(solution)/shard_map/ppermute | solution.py:628
  132.0 2.3 %collective-permute-done.11 = f32[6,3,32]{2,0,1:T(8,128)S(1)} collective-permute-done((f32[6,3,32]{2,0,1:T(8,128)S(1)}, f32[6,3,32]{2,0,1:T(8,128)S(1)}, u32[]{:S(2)}, u32[]{:S(2)}) %collective-permute-start.11) | collective-permute-done | bytes 2336 | tf_op jit(solution)/shard_map/ppermute | solution.py:628
  135.1 4.9 %reflect.1 = f32[256,128]{1,0:T(8,128)} custom-call(s32[256,128]{1,0:T(8,128)} %fusion.32.slots, f32[6,256,128]{2,1,0:T(8,128)} %get-tuple-element.40.reach, f32[256,128]{1,0:T(8,128)} %bitcast.83, f32[6,3,128]{2,1,0:T(4,128)} %reshape.113.motion), custom_call_target="tpu_custom_call" | custom-call | tf_op jit(solution)/shard_map/reflect/pallas_call | solution.py:632
  (81 shorter events, 6.6 us)
Async XLA Ops:
  0.6 1.8 %copy-start.1 = (bf16[48,64,128]{2,1,0:T(8,128)(2,1)S(1)}, bf16[48,64,128]{2,1,0:T(8,128)(2,1)}, u32[]{:S(2)}) copy-start(bf16[48,64,128]{2,1,0:T(8,128)(2,1)} %eps.1) | copy-start | bytes 2359300
  2.8 3.4 %copy-start.4 = (f32[3,1,1,32768]{3,2,1,0:T(1,128)S(1)}, f32[3,1,1,32768]{3,2,1,0:T(1,128)}, u32[]{:S(2)}) copy-start(f32[3,1,1,32768]{3,2,1,0:T(1,128)} %param.28) | copy-start | bytes 1179652
  3.0 3.2 %copy-start.5 = (s32[1,1,32768]{2,1,0:T(1,128)S(1)}, s32[1,1,32768]{2,1,0:T(1,128)}, u32[]{:S(2)}) copy-start(s32[1,1,32768]{2,1,0:T(1,128)} %param.25) | copy-start | bytes 393220
  3.0 3.2 %copy-start.6 = (s32[1,1,32768]{2,1,0:T(1,128)S(1)}, s32[1,1,32768]{2,1,0:T(1,128)}, u32[]{:S(2)}) copy-start(s32[1,1,32768]{2,1,0:T(1,128)} %param.26) | copy-start | bytes 393220
  3.0 21.6 %collective-permute-start.1 = (f16[3,12,48,128]{3,2,1,0:T(8,128)(2,1)S(1)}, f16[3,12,48,128]{3,2,1,0:T(8,128)(2,1)S(1)}, u32[]{:S(2)}, u32[]{:S(2)}) collective-permute-start(f16[3,12,48,128]{3,2,1,0:T(8,128)(2,1)S(1)} %maximum_bitcast_fusion.1), channel_id=1, source_target_pairs={{8,0},{16,8},{24,16},{0,24},{9,1},{17,9},{25,17},{1,25},{10,2},{18... | collective-permute-start | bytes 1327112 | tf_op jit(solution)/shard_map/ppermute | solution.py:511
  3.1 3.4 %copy-start.3 = (s32[1,1,32768]{2,1,0:T(1,128)S(1)}, s32[1,1,32768]{2,1,0:T(1,128)}, u32[]{:S(2)}) copy-start(s32[1,1,32768]{2,1,0:T(1,128)} %param.24) | copy-start | bytes 393220
  3.1 3.4 %copy-start.7 = (s32[1,1,32768]{2,1,0:T(1,128)S(1)}, s32[1,1,32768]{2,1,0:T(1,128)}, u32[]{:S(2)}) copy-start(s32[1,1,32768]{2,1,0:T(1,128)} %param.23) | copy-start | bytes 393220
  3.4 21.3 %copy-start.11 = (f32[3]{0:T(128)S(1)}, f32[3]{0:T(128)}, u32[]{:S(2)}) copy-start(f32[3]{0:T(128)} %constant.154) | copy-start | bytes 40
  3.5 21.1 %collective-permute-start = (f16[3,12,48,128]{3,2,1,0:T(8,128)(2,1)S(1)}, f16[3,12,48,128]{3,2,1,0:T(8,128)(2,1)S(1)}, u32[]{:S(2)}, u32[]{:S(2)}) collective-permute-start(f16[3,12,48,128]{3,2,1,0:T(8,128)(2,1)S(1)} %maximum_bitcast_fusion), channel_id=1, source_target_pairs={{0,8},{8,16},{16,24},{24,0},{1,9},{9,17},{17,25},{25,1},{2,10},{10... | collective-permute-start | bytes 1327112 | tf_op jit(solution)/shard_map/ppermute | solution.py:510
  23.6 20.3 %copy-start.2 = (s32[32768]{0:T(1024)}, s32[32768]{0:T(1024)S(1)}, u32[]{:S(2)}) copy-start(s32[32768]{0:T(1024)S(1)} %get-tuple-element.35) | copy-start | bytes 393220
  26.2 11.7 %copy-start.12 = (f32[3]{0:T(128)S(1)}, f32[3]{0:T(128)}, u32[]{:S(2)}) copy-start(f32[3]{0:T(128)} %constant.145.clone) | copy-start | bytes 40
  39.4 20.1 %collective-permute-start.2 = (f16[3,5,88,128]{3,2,1,0:T(8,128)(2,1)S(1)}, f16[3,5,88,128]{3,2,1,0:T(8,128)(2,1)S(1)}, u32[]{:S(2)}, u32[]{:S(2)}) collective-permute-start(f16[3,5,88,128]{3,2,1,0:T(8,128)(2,1)S(1)} %get-tuple-element.68), channel_id=1, source_target_pairs={{0,1},{1,2},{2,3},{3,4},{4,5},{5,6},{6,7},{7,0},{8,9},{9,10},{10,1... | collective-permute-start | bytes 1013768 | tf_op jit(solution)/shard_map/ppermute | solution.py:555
  40.7 18.9 %collective-permute-start.3 = (f16[3,5,88,128]{3,2,1,0:T(8,128)(2,1)S(1)}, f16[3,5,88,128]{3,2,1,0:T(8,128)(2,1)S(1)}, u32[]{:S(2)}, u32[]{:S(2)}) collective-permute-start(f16[3,5,88,128]{3,2,1,0:T(8,128)(2,1)S(1)} %get-tuple-element.67), channel_id=1, source_target_pairs={{1,0},{2,1},{3,2},{4,3},{5,4},{6,5},{7,6},{0,7},{9,8},{10,9},{11,1... | collective-permute-start | bytes 1013768 | tf_op jit(solution)/shard_map/ppermute | solution.py:556
  44.2 13.7 %copy-start.10 = (s32[256]{0:T(256)}, s32[256]{0:T(256)S(1)}, u32[]{:S(2)}) copy-start(s32[256]{0:T(256)S(1)} %fusion.37.low) | copy-start | bytes 3076
  93.0 27.8 %copy-start.8 = (f32[3,32]{1,0:T(4,128)S(1)}, f32[3,32]{1,0:T(4,128)}, u32[]{:S(2)}) copy-start(f32[3,32]{1,0:T(4,128)} %param.21) | copy-start | bytes 1156
  93.0 27.8 %copy-start.9 = (f32[3,32]{1,0:T(4,128)S(1)}, f32[3,32]{1,0:T(4,128)}, u32[]{:S(2)}) copy-start(f32[3,32]{1,0:T(4,128)} %param.22) | copy-start | bytes 1156
  109.3 3.9 %collective-permute-start.4 = (f32[27,3,32]{2,1,0:T(4,128)S(1)}, f32[27,3,32]{2,1,0:T(4,128)S(1)}, u32[]{:S(2)}, u32[]{:S(2)}) collective-permute-start(f32[27,3,32]{2,1,0:T(4,128)S(1)} %get-tuple-element.50), channel_id=1, source_target_pairs={{8,0},{16,8},{24,16},{0,24},{9,1},{17,9},{25,17},{1,25},{10,2},{18... | collective-permute-start | bytes 31112 | tf_op jit(solution)/shard_map/ppermute | solution.py:604
  110.7 2.5 %collective-permute-start.5 = (f32[27,3,32]{2,1,0:T(4,128)S(1)}, f32[27,3,32]{2,1,0:T(4,128)S(1)}, u32[]{:S(2)}, u32[]{:S(2)}) collective-permute-start(f32[27,3,32]{2,1,0:T(4,128)S(1)} %get-tuple-element.51), channel_id=1, source_target_pairs={{0,8},{8,16},{16,24},{24,0},{1,9},{9,17},{17,25},{25,1},{2,10},{10... | collective-permute-start | bytes 31112 | tf_op jit(solution)/shard_map/ppermute | solution.py:605
  113.3 3.1 %collective-permute-start.6 = (f32[27,32]{1,0:T(8,128)S(1)}, f32[27,32]{1,0:T(8,128)S(1)}, u32[]{:S(2)}, u32[]{:S(2)}) collective-permute-start(f32[27,32]{1,0:T(8,128)S(1)} %bitcast.90), channel_id=1, source_target_pairs={{1,0},{2,1},{3,2},{4,3},{5,4},{6,5},{7,6},{0,7},{9,8},{10,9},{11,1... | collective-permute-start | bytes 10376 | tf_op jit(solution)/shard_map/ppermute | solution.py:607
  115.5 5.3 %collective-permute-start.7 = (f32[27,32]{1,0:T(8,128)S(1)}, f32[27,32]{1,0:T(8,128)S(1)}, u32[]{:S(2)}, u32[]{:S(2)}) collective-permute-start(f32[27,32]{1,0:T(8,128)S(1)} %bitcast.91), channel_id=1, source_target_pairs={{0,1},{1,2},{2,3},{3,4},{4,5},{5,6},{6,7},{7,0},{8,9},{9,10},{10,1... | collective-permute-start | bytes 10376 | tf_op jit(solution)/shard_map/ppermute | solution.py:607
  121.0 5.2 %collective-permute-start.8 = (f32[6,32]{1,0:T(8,128)S(1)}, f32[6,32]{1,0:T(8,128)S(1)}, u32[]{:S(2)}, u32[]{:S(2)}) collective-permute-start(f32[6,32]{1,0:T(8,128)S(1)} %get-tuple-element.60), channel_id=1, source_target_pairs={{0,1},{1,2},{2,3},{3,4},{4,5},{5,6},{6,7},{7,0},{8,9},{9,10},{10,1... | collective-permute-start | bytes 2312 | tf_op jit(solution)/shard_map/ppermute | solution.py:625
  121.1 5.1 %collective-permute-start.9 = (f32[6,32]{1,0:T(8,128)S(1)}, f32[6,32]{1,0:T(8,128)S(1)}, u32[]{:S(2)}, u32[]{:S(2)}) collective-permute-start(f32[6,32]{1,0:T(8,128)S(1)} %get-tuple-element.60), channel_id=1, source_target_pairs={{1,0},{2,1},{3,2},{4,3},{5,4},{6,5},{7,6},{0,7},{9,8},{10,9},{11,1... | collective-permute-start | bytes 2312 | tf_op jit(solution)/shard_map/ppermute | solution.py:625
  126.2 5.8 %collective-permute-start.10 = (f32[6,3,32]{2,0,1:T(8,128)S(1)}, f32[6,3,32]{2,0,1:T(8,128)S(1)}, u32[]{:S(2)}, u32[]{:S(2)}) collective-permute-start(f32[6,3,32]{2,0,1:T(8,128)S(1)} %get-tuple-element.58), channel_id=1, source_target_pairs={{0,8},{8,16},{16,24},{24,0},{1,9},{9,17},{17,25},{25,1},{2,10},{10... | collective-permute-start | bytes 6920 | tf_op jit(solution)/shard_map/ppermute | solution.py:628
  131.2 3.1 %collective-permute-start.11 = (f32[6,3,32]{2,0,1:T(8,128)S(1)}, f32[6,3,32]{2,0,1:T(8,128)S(1)}, u32[]{:S(2)}, u32[]{:S(2)}) collective-permute-start(f32[6,3,32]{2,0,1:T(8,128)S(1)} %get-tuple-element.58), channel_id=1, source_target_pairs={{8,0},{16,8},{24,16},{0,24},{9,1},{17,9},{25,17},{1,25},{10,2},{18... | collective-permute-start | bytes 6920 | tf_op jit(solution)/shard_map/ppermute | solution.py:628
  (1 other events, 1.7 us)

commit v4 on v3

--- a/solution.py
+++ b/solution.py
@@ -309,6 +309,7 @@
         if reach:
             wrap_pot(c)
 
+    press_out[depth] = jnp.zeros((wide, 128), F32)
     core = slice(top + FIRST, top + FIRST + wide)
     core_flat = parity_of((wide, 128))
 
@@ -364,6 +365,39 @@
     )
 
 
+def add_by_tile(stage, slot, per_tile):
+    total = stage.shape[0] // 8
+    shift = per_tile.bit_length() - 1
+    tile = (slot >> shift).astype(F32)
+    fine = (slot & (per_tile - 1)).astype(F32)
+    small = lax.broadcasted_iota(jnp.int32, (per_tile, 128), 0).astype(F32).astype(jnp.bfloat16)
+    one = jnp.ones((per_tile, 128), jnp.bfloat16)
+    none = jnp.zeros((2 * total, 128), jnp.bfloat16)
+    hot, terms = [], []
+    for s in range(8):
+        place = jnp.broadcast_to(fine[s:s + 1, :], (per_tile, 128)).astype(jnp.bfloat16)
+        hot.append(jnp.where(place == small, one, jnp.zeros_like(one)))
+        owner = jnp.broadcast_to(tile[s:s + 1, :], (2 * total, 128)).astype(jnp.bfloat16)
+        value = stage[pl.ds(s, total, stride=8), :]
+        head = value.astype(jnp.bfloat16)
+        both = jnp.concatenate([head.astype(F32), value - head.astype(F32)], axis=0)
+        both = both.astype(jnp.bfloat16)
+        terms.append(jnp.concatenate([jnp.where(owner == t, both, none) for t in range(9)], axis=0))
+    return lax.dot_general(
+        jnp.concatenate(terms, axis=1),
+        jnp.concatenate(hot, axis=1),
+        (((1,), (1,)), ((), ())),
+        preferred_element_type=F32,
+    )
+
+
+def write_sums(acc, out):
+    total = out.shape[1]
+    for t in range(9):
+        base = 2 * total * t
+        out[t] = acc[base:base + total, :] + acc[base + total:base + 2 * total, :]
+
+
 def fixed_kernel(slots, dirs, pops, rb, table, out, reach, stage, acc, *, width):
     acc[...] = jnp.zeros_like(acc)
     total = stage.shape[0] // 8
@@ -388,15 +422,15 @@
     out[...] = acc[0:total, :] + acc[total:, :]
 
 
-BATCH = 4
+BATCH = 8
 AHEAD = 4
 
 
-def press_kernel(low, passes, keys, rb0, rb1, rb2, table, press, out, stage, acc, *, width):
+def press_kernel(low, passes, keys, rb0, rb1, rb2, table, press, out, stage, acc, *, per_tile):
     acc[...] = jnp.zeros_like(acc)
     for n in range(6, stage.shape[0] // 8):
         store_term(stage, n, jnp.zeros((8, 128), F32))
-    limit = press.shape[0] - 1
+    limit = press.shape[0] - AHEAD
     line = lax.broadcasted_iota(jnp.int32, (8, 128), 0)
 
     def batch(b, carry):
@@ -415,14 +449,14 @@
         def look(m, found):
             found = list(found)
             for j in range(BATCH):
+                bases = [jnp.minimum(starts[j][s] + AHEAD * m, limit) for s in range(8)]
                 for t in range(AHEAD):
-                    step = AHEAD * m + t
                     window = jnp.zeros((8, 128), F32)
                     for s in range(8):
-                        row = press[pl.ds(jnp.minimum(starts[j][s] + step, limit), 1), :]
+                        row = press[pl.ds(bases[s] + t, 1), :]
                         window = jnp.where(line == s, jnp.broadcast_to(row, (8, 128)), window)
                     value = lane_pick(window, columns[j])
-                    found[j] = jnp.where(offsets[j] == step, value, found[j])
+                    found[j] = jnp.where(offsets[j] == AHEAD * m + t, value, found[j])
             return tuple(found)
 
         found = lax.fori_loop(
@@ -437,31 +471,34 @@
             wq = w * found[j]
             for n in range(6):
                 store_term(stage, n, wq * arms[n])
-            acc[...] += add_by_slot(stage, slot, width)
+            acc[...] += add_by_tile(stage, slot, per_tile)
         return carry
 
     lax.fori_loop(0, keys.shape[0] // (8 * BATCH), batch, 0)
-    total = stage.shape[0] // 8
-    out[...] = acc[0:total, :] + acc[total:, :]
+    write_sums(acc, out)
+
+
+TOGETHER = 4
 
 
 def reflect_kernel(slots, reach, pops, motion, out):
-    def block(b, carry):
-        rs = pl.ds(pl.multiple_of(8 * b, 8), 8)
-        slot = slots[rs, :]
-        lane = slot & 127
-        part = slot >> 7
-        along = jnp.zeros((8, 128), F32)
-        for n in range(6):
-            value = jnp.zeros((8, 128), F32)
-            for h in range(motion.shape[1]):
-                line = jnp.broadcast_to(motion[n, h:h + 1, :], (8, 128))
-                value = jnp.where(part == h, lane_pick(line, lane), value)
-            along += reach[n, rs, :] * value
-        out[rs, :] = pops[rs, :] - along
-        return carry
-
-    lax.fori_loop(0, slots.shape[0] // 8, block, 0)
+    def batch(b, carry):
+        for j in range(TOGETHER):
+            rs = pl.ds(pl.multiple_of(8 * (TOGETHER * b + j), 8), 8)
+            slot = slots[rs, :]
+            lane = slot & 127
+            part = slot >> 7
+            along = jnp.zeros((8, 128), F32)
+            for n in range(6):
+                value = jnp.zeros((8, 128), F32)
+                for h in range(motion.shape[1]):
+                    line = jnp.broadcast_to(motion[n, h:h + 1, :], (8, 128))
+                    value = jnp.where(part == h, lane_pick(line, lane), value)
+                along += reach[n, rs, :] * value
+            out[rs, :] = pops[rs, :] - along
+        return carry
+
+    lax.fori_loop(0, slots.shape[0] // (8 * TOGETHER), batch, 0)
 
 
 def ring(axis):
@@ -486,7 +523,8 @@
     return [pl.BlockSpec(memory_space=pltpu.VMEM)] * n
 
 
-PARAMS = pltpu.CompilerParams(vmem_limit_bytes=60 * 1024 * 1024)
+def grant(mib):
+    return pltpu.CompilerParams(vmem_limit_bytes=mib * 1024 * 1024)
 
 
 def shards(
@@ -548,7 +586,7 @@
             jax.ShapeDtypeStruct((3, GROUPS, wide + 2 * HALO, 128), F32),
             jax.ShapeDtypeStruct((3, GROUPS, wide + 2 * HALO, 128), F32),
         ),
-        in_specs=vmem(5), out_specs=tuple(vmem(3)), compiler_params=PARAMS, name="pack",
+        in_specs=vmem(5), out_specs=tuple(vmem(3)), compiler_params=grant(24), name="pack",
         scratch_shapes=[pltpu.VMEM((2, 3 * GROUPS, wide + 2 * HALO, 128), F32)],
     )(potential_start, charge, eps_field,
       from_half(low).reshape(-1, 128), from_half(high).reshape(-1, 128))
@@ -564,14 +602,17 @@
         ),
         in_specs=vmem(5), out_specs=tuple(vmem(2)),
         scratch_shapes=[pltpu.VMEM((8 * terms, 128), F32), pltpu.VMEM((2 * terms, width), F32)],
-        compiler_params=PARAMS, name="fixed",
+        compiler_params=grant(8), name="fixed",
         cost_estimate=pl.CostEstimate(flops=10**9, bytes_accessed=2 * 10**7, transcendentals=0),
     )(slots, dirs_late, pops, rb, table)
 
     tall = rows + 2 * MARGIN
     potential, press = pl.pallas_call(
         relax_kernel,
-        out_shape=(jax.ShapeDtypeStruct(charge.shape, F32),) * 2,
+        out_shape=(
+            jax.ShapeDtypeStruct((depth, wide, 128), F32),
+            jax.ShapeDtypeStruct((depth + 1, wide, 128), F32),
+        ),
         in_specs=vmem(3), out_specs=tuple(vmem(2)),
         scratch_shapes=[
             pltpu.VMEM((2, layers + 3, tall, 128), F32),
@@ -582,29 +623,26 @@
             pltpu.VMEM((2, GROUPS, rows, 128), F32),
             pltpu.VMEM((2, 7, GROUPS, rows, 128), F32),
         ],
-        compiler_params=PARAMS, name="relax",
+        compiler_params=grant(44), name="relax",
     )(split, from_half(from_left), from_half(from_right))
 
     smem = pl.BlockSpec(memory_space=pltpu.SMEM)
     pressed = pl.pallas_call(
-        functools.partial(press_kernel, width=width),
-        out_shape=jax.ShapeDtypeStruct((8, width), F32),
+        functools.partial(press_kernel, per_tile=per_tile),
+        out_shape=jax.ShapeDtypeStruct((9, 8, per_tile), F32),
         in_specs=[smem, smem] + vmem(6), out_specs=vmem(1)[0],
-        scratch_shapes=[pltpu.VMEM((64, 128), F32), pltpu.VMEM((16, width), F32)],
-        compiler_params=PARAMS, name="press",
+        scratch_shapes=[pltpu.VMEM((64, 128), F32), pltpu.VMEM((9 * 16, per_tile), F32)],
+        compiler_params=grant(8), name="press",
     )(
         row_low, passes, keys, rb0.reshape(lines, 128), rb1.reshape(lines, 128),
-        rb2.reshape(lines, 128), table, press.reshape(depth * wide, 128),
-    )
-
-    sums = jnp.concatenate([fixed[0:6] + pressed[0:6], fixed[6:27]], axis=0)
-    sums = sums.reshape(27, 3, 3, per_tile)
-    mid = (
-        sums[:, 1]
-        + lax.ppermute(sums[:, 0], "gx", bx)
-        + lax.ppermute(sums[:, 2], "gx", fx)
-    )
-    mine = mid[:, 1] + lax.ppermute(mid[:, 0], "gy", by) + lax.ppermute(mid[:, 2], "gy", fy)
+        rb2.reshape(lines, 128), table, press.reshape(-1, 128),
+    )
+
+    fixed = fixed.reshape(terms, 9, per_tile).transpose(1, 0, 2)
+    sums = jnp.concatenate([fixed[:, 0:6] + pressed[:, 0:6], fixed[:, 6:27]], axis=1)
+    sums = sums.reshape(3, 3, 27, per_tile)
+    mid = sums[1] + lax.ppermute(sums[0], "gx", bx) + lax.ppermute(sums[2], "gx", fx)
+    mine = mid[1] + lax.ppermute(mid[0], "gy", by) + lax.ppermute(mid[2], "gy", fy)
     motion = jnp.concatenate([colloid_vel, colloid_spin], axis=0)
     drag = []
     for a in range(6):
@@ -632,7 +670,7 @@
     link_out = pl.pallas_call(
         reflect_kernel,
         out_shape=jax.ShapeDtypeStruct((lines, 128), F32),
-        in_specs=vmem(4), out_specs=vmem(1)[0], compiler_params=PARAMS, name="reflect",
+        in_specs=vmem(4), out_specs=vmem(1)[0], compiler_params=grant(6), name="reflect",
     )(slots, reach, pops, around)
     return potential, report, link_out.reshape(link_pop.shape)
 

time: 140 us -> 128 us (0.914)
  Pallas kernels: 77.9 us -> 55.7 us
  local copies, waits for them, and re-layouts: 3.86 us -> 9.97 us
  other arithmetic: 25.8 us -> 27.7 us
    pallas_call x2, Pallas kernels: 47.6 us -> 36.1 us  [the longest x1 28.3 us: shards(): pl.pallas_call(relax_kernel, out_shape=(jax.ShapeDtypeStruct((depth, wide...]
    unnamed x28 -> x32, local copies, waits for them, and re-layouts: 0.49 us -> 7.22 us
    pallas_call x1, Pallas kernels: 11.7 us -> 5.73 us  [shards(): pl.pallas_call(pack_kernel, out_shape=(jax.ShapeDtypeStruct((6, layers +...]
    pallas_call x1, Pallas kernels: 4.89 us -> 1.96 us  [shards(): pl.pallas_call(reflect_kernel, out_shape=jax.ShapeDtypeStruct((lines, 128...]
    ppermute x4, starting transfers between devices: 4.38 us -> 6.4 us  [the longest x1 4.6 us: shards(): lax.ppermute(mid[0], 'gy', by)]
    pallas_call x1, Pallas kernels: 13.7 us -> 11.9 us  [shards(): pl.pallas_call(functools.partial(fixed_kernel, width=width), out_shape=(j...]
    convert_element_type x2, other arithmetic: 0.28 us -> 1.84 us  [edge(): return strips.transpose(0, 2, 1, 3).astype(HALF)]
  transfers between devices with their start and end apart: 12 -> 12, of which waited for: 6 -> 7; matrix products, arithmetic and copies ran while one was open for 15% -> 19% of each run, Pallas kernels for 10% -> 9%
where the time goes in v4:
time: 128 us; the launch traced here: 127 us
  Pallas kernels  55.7 us (44%)
  other arithmetic  27.7 us (22%)
  starting transfers between devices  22.1 us (17%)
  waiting for transfers between devices  10.8 us (8%)
  local copies, waits for them, and re-layouts  9.97 us (8%)
    pallas_call x1, Pallas kernels, shards(): pl.pallas_call(relax_kernel, out_shape=(jax.ShapeDtypeStruct((depth, wide...  28.3 us
    sort x1, other arithmetic, shards(): lax.sort((key.reshape(-1), rb[0].reshape(-1), rb[1].reshape(-1), rb[2].re...  17.1 us
    pallas_call x1, Pallas kernels, shards(): pl.pallas_call(functools.partial(fixed_kernel, width=width), out_shape=(j...  11.9 us
    pallas_call x1, Pallas kernels, shards(): pl.pallas_call(functools.partial(press_kernel, per_tile=per_tile), out_sh...  7.82 us
    unnamed x32, local copies, waits for them, and re-layouts  7.22 us
    pallas_call x1, Pallas kernels, shards(): pl.pallas_call(pack_kernel, out_shape=(jax.ShapeDtypeStruct((6, layers +...  5.73 us
    ppermute x1, starting transfers between devices, shards(): lax.ppermute(column, 'gx', fx)  4.61 us
    ppermute x1, starting transfers between devices, shards(): lax.ppermute(mid[0], 'gy', by)  4.6 us
  transfers between devices with their start and end apart: 12, of which 7 were waited for; matrix products, arithmetic and copies ran while one was open for 19% of the time, Pallas kernels for 9%

profile of v4, /device:TPU:1, one launch (start us, length us, event | category | flops | bytes accessed | tf_op | source)
XLA Modules:
  0.0 127.3 jit_solution(11081577009684326326)
XLA Ops:
  0.6 1.3 %fusion.61 = (f32[48,12,128]{2,1,0:T(8,128)S(1)}, f32[48,12,128]{2,1,0:T(8,128)S(1)}) fusion(f32[48,64,128]{2,1,0:T(8,128)} %pot.1), kind=kLoop, calls=%fused_computation.147 | loop fusion | bytes 1179648 | tf_op jit(solution)/shard_map/slice | solution.py:542
  5.0 2.6 %collective-permute-start = (f16[3,12,48,128]{3,2,1,0:T(8,128)(2,1)}, f16[3,12,48,128]{3,2,1,0:T(8,128)(2,1)}, u32[]{:S(2)}, u32[]{:S(2)}) collective-permute-start(f16[3,12,48,128]{3,2,1,0:T(8,128)(2,1)} %maximum_bitcast_fusion), channel_id=1, source_target_pairs={{0,8},{8,16},{16,24},{24,0},{1,9},{9,17},{17,25},{25,1},{2,10},{10... | collective-permute-start | bytes 1327112 | tf_op jit(solution)/shard_map/ppermute | solution.py:548
  8.4 1.1 add_multiply_fusion
  9.5 1.0 fusion.21
  10.6 17.1 %sort.27 = (s32[32768]{0:T(1024)S(1)}, f32[32768]{0:T(1024)S(1)}, f32[32768]{0:T(1024)S(1)}, f32[32768]{0:T(1024)S(1)}) sort(s32[32768]{0:T(1024)} %fusion.21, f32[32768]{0:T(1024)} %bitcast.77, f32[32768]{0:T(1024)} %bitcast.76, f32[32768]{0:T(1024)} %bitcast.75), dimensions={0}, to_apply=%region_0.1 | sort | flops 491520 | bytes 1048576 | tf_op jit(solution)/shard_map/sort | solution.py:569
  27.6 1.4 %fusion.32.slots = s32[256,128]{1,0:T(8,128)S(1)} fusion(s32[256,128]{1,0:T(8,128)} %bitcast.73, s32[]{:T(128)S(6)} %axis_index.25, s32[]{:T(128)S(6)} %axis_index.23), kind=kLoop, calls=%fused_computation.83 | loop fusion | flops 2293760 | bytes 262152 | tf_op jit(solution)/shard_map/jit(_where)/select_n | solution.py:564
  29.1 1.4 %convert_multiply_fusion = (f32[3,12,48,128]{3,2,1,0:T(8,128)S(1)}, f32[3,12,48,128]{3,2,1,0:T(8,128)S(1)}) fusion(f16[3,12,48,128]{3,2,1,0:T(8,128)(2,1)} %collective-permute-done.1, f32[3]{0:T(128)S(1)} %copy-done.14, f16[3,12,48,128]{3,2,1,0:T(8,128)(2,1)} %collective-permute-done), kind=kLoop, calls=%fused_computation | loop fusion | flops 884736 | bytes 2654220 | tf_op jit(solution)/shard_map/mul | solution.py:519
  30.5 5.7 %pack.1 = (f32[6,25,96,128]{3,2,1,0:T(8,128)S(1)}, f32[3,5,88,128]{3,2,1,0:T(8,128)S(1)}, f32[3,5,88,128]{3,2,1,0:T(8,128)S(1)}) custom-call(f32[48,64,128]{2,1,0:T(8,128)S(1)} %copy-done.2, f32[48,64,128]{2,1,0:T(8,128)S(1)} %copy-done.3, bf16[48,64,128]{2,1,0:T(8,128)(2,1)S(1)} %copy-done.4, f32[1728,128]{1,0:T(8,128)S(1)} %bitcast.58, ...), custom_call_target="tpu_custom_call" | custom-call | tf_op jit(solution)/shard_map/pack/pallas_call | solution.py:582
  36.2 2.9 %copy-done = f32[6,25,96,128]{3,2,1,0:T(8,128)} copy-done((f32[6,25,96,128]{3,2,1,0:T(8,128)}, f32[6,25,96,128]{3,2,1,0:T(8,128)S(1)}, u32[]{:S(2)}) %copy-start) | copy-done | bytes 7372824
  40.1 1.2 collective-permute-start.2
  41.3 3.0 %collective-permute-start.3 = (f16[3,5,88,128]{3,2,1,0:T(8,128)(2,1)S(1)}, f16[3,5,88,128]{3,2,1,0:T(8,128)(2,1)}, u32[]{:S(2)}, u32[]{:S(2)}) collective-permute-start(f16[3,5,88,128]{3,2,1,0:T(8,128)(2,1)S(1)} %get-tuple-element.66), channel_id=1, source_target_pairs={{1,0},{2,1},{3,2},{4,3},{5,4},{6,5},{7,6},{0,7},{9,8},{10,9},{11,1... | collective-permute-start | bytes 1013768 | tf_op jit(solution)/shard_map/ppermute | solution.py:594
  44.6 11.9 %fixed.1 = (f32[32,288]{1,0:T(8,128)S(1)}, f32[6,256,128]{2,1,0:T(8,128)S(1)}) custom-call(s32[256,128]{1,0:T(8,128)S(1)} %fusion.32.slots, s32[256,128]{1,0:T(8,128)S(1)} %bitcast.68, f32[256,128]{1,0:T(8,128)S(1)} %bitcast.62, f32[3,256,128]{2,1,0:T(8,128)S(1)} %bitcast.61, f32[4,8,128]{2,1,0:T(8,128)S(1)} %copy-done.8), custom_call_target="tpu_custom_call" | custom-call | flops 1000000000 | bytes 20000000 | tf_op jit(solution)/shard_map/fixed/pallas_call | solution.py:598
  58.1 1.2 convert_multiply_fusion.2
  59.3 3.1 %copy-done.1 = f32[6,25,96,128]{3,2,1,0:T(8,128)S(1)} copy-done((f32[6,25,96,128]{3,2,1,0:T(8,128)S(1)}, f32[6,25,96,128]{3,2,1,0:T(8,128)}, u32[]{:S(2)}) %copy-start.1) | copy-done | bytes 7372824
  62.4 28.3 %relax.1 = (f32[48,64,128]{2,1,0:T(8,128)}, f32[49,64,128]{2,1,0:T(8,128)S(1)}) custom-call(f32[6,25,96,128]{3,2,1,0:T(8,128)S(1)} %copy-done.1, f32[3,5,88,128]{3,2,1,0:T(8,128)S(1)} %get-tuple-element.65.from_left, f32[3,5,88,128]{3,2,1,0:T(8,128)S(1)} %get-tuple-element.64.from_right), custom_call_target="tpu_custom_call" | custom-call | tf_op jit(solution)/shard_map/relax/pallas_call | solution.py:610
  90.7 7.8 %press.1 = f32[9,8,32]{2,1,0:T(8,128)S(1)} custom-call(s32[256]{0:T(256)S(1)} %fusion.37.low, s32[4]{0:T(128)S(1)} %and_select_fusion.passes, s32[256,128]{1,0:T(8,128)S(1)} %bitcast.60, f32[256,128]{1,0:T(8,128)S(1)} %bitcast.64, f32[256,128]{1,0:T(8,128)S(1)} %bitcast.65, f32[256,128]{1,0:T(8,128)S(1)} %bitcast.66, f32[4,8,128]{2,1,0:T(8,128)S(1)} %copy-done.8, ...), custom_call_target="tpu_custom_call" | custom-call | tf_op jit(solution)/shard_map/press/pallas_call | solution.py:630
  98.5 1.2 collective-permute-start.4
  100.3 1.8 %collective-permute-done.4 = f32[3,27,32]{2,1,0:T(8,128)S(1)} collective-permute-done((f32[3,27,32]{2,1,0:T(8,128)S(1)}, f32[3,27,32]{2,1,0:T(8,128)S(1)}, u32[]{:S(2)}, u32[]{:S(2)}) %collective-permute-start.4) | collective-permute-done | bytes 10400 | tf_op jit(solution)/shard_map/ppermute | solution.py:644
  102.1 4.6 %collective-permute-start.6 = (f32[27,32]{1,0:T(8,128)S(1)}, f32[27,32]{1,0:T(8,128)S(1)}, u32[]{:S(2)}, u32[]{:S(2)}) collective-permute-start(f32[27,32]{1,0:T(8,128)S(1)} %get-tuple-element.54), channel_id=1, source_target_pairs={{1,0},{2,1},{3,2},{4,3},{5,4},{6,5},{7,6},{0,7},{9,8},{10,9},{11,1... | collective-permute-start | bytes 10376 | tf_op jit(solution)/shard_map/ppermute | solution.py:645
  107.6 4.4 %collective-permute-done.7 = f32[27,32]{1,0:T(8,128)S(1)} collective-permute-done((f32[27,32]{1,0:T(8,128)S(1)}, f32[27,32]{1,0:T(8,128)S(1)}, u32[]{:S(2)}, u32[]{:S(2)}) %collective-permute-start.7) | collective-permute-done | bytes 3488 | tf_op jit(solution)/shard_map/ppermute | solution.py:645
  112.3 4.1 %collective-permute-start.9 = (f32[6,32]{1,0:T(8,128)S(1)}, f32[6,32]{1,0:T(8,128)S(1)}, u32[]{:S(2)}, u32[]{:S(2)}) collective-permute-start(f32[6,32]{1,0:T(8,128)S(1)} %get-tuple-element.59), channel_id=1, source_target_pairs={{1,0},{2,1},{3,2},{4,3},{5,4},{6,5},{7,6},{0,7},{9,8},{10,9},{11,1... | collective-permute-start | bytes 2312 | tf_op jit(solution)/shard_map/ppermute | solution.py:663
  117.4 4.6 %collective-permute-start.10 = (f32[6,3,32]{2,0,1:T(8,128)S(1)}, f32[6,3,32]{2,0,1:T(8,128)S(1)}, u32[]{:S(2)}, u32[]{:S(2)}) collective-permute-start(f32[6,3,32]{2,0,1:T(8,128)S(1)} %get-tuple-element.57), channel_id=1, source_target_pairs={{0,8},{8,16},{16,24},{24,0},{1,9},{9,17},{17,25},{25,1},{2,10},{10... | collective-permute-start | bytes 6920 | tf_op jit(solution)/shard_map/ppermute | solution.py:666
  122.9 2.3 %collective-permute-done.11 = f32[6,3,32]{2,0,1:T(8,128)S(1)} collective-permute-done((f32[6,3,32]{2,0,1:T(8,128)S(1)}, f32[6,3,32]{2,0,1:T(8,128)S(1)}, u32[]{:S(2)}, u32[]{:S(2)}) %collective-permute-start.11) | collective-permute-done | bytes 2336 | tf_op jit(solution)/shard_map/ppermute | solution.py:666
  125.3 2.0 %reflect.1 = f32[256,128]{1,0:T(8,128)} custom-call(s32[256,128]{1,0:T(8,128)S(1)} %fusion.32.slots, f32[6,256,128]{2,1,0:T(8,128)S(1)} %get-tuple-element.40.reach, f32[256,128]{1,0:T(8,128)S(1)} %bitcast.63, f32[6,3,128]{2,1,0:T(4,128)S(1)} %reshape.120.motion), custom_call_target="tpu_custom_call" | custom-call | tf_op jit(solution)/shard_map/reflect/pallas_call | solution.py:670
  (85 shorter events, 10.0 us)
Async XLA Ops:
  2.8 4.8 %copy-start.5 = (f32[3,1,1,32768]{3,2,1,0:T(1,128)S(1)}, f32[3,1,1,32768]{3,2,1,0:T(1,128)}, u32[]{:S(2)}) copy-start(f32[3,1,1,32768]{3,2,1,0:T(1,128)} %param.28) | copy-start | bytes 1179652
  3.7 4.6 %copy-start.11 = (s32[1,1,32768]{2,1,0:T(1,128)S(1)}, s32[1,1,32768]{2,1,0:T(1,128)}, u32[]{:S(2)}) copy-start(s32[1,1,32768]{2,1,0:T(1,128)} %param.25) | copy-start | bytes 393220
  3.7 25.3 %collective-permute-start.1 = (f16[3,12,48,128]{3,2,1,0:T(8,128)(2,1)}, f16[3,12,48,128]{3,2,1,0:T(8,128)(2,1)}, u32[]{:S(2)}, u32[]{:S(2)}) collective-permute-start(f16[3,12,48,128]{3,2,1,0:T(8,128)(2,1)} %maximum_bitcast_fusion.1), channel_id=1, source_target_pairs={{8,0},{16,8},{24,16},{0,24},{9,1},{17,9},{25,17},{1,25},{10,2},{18... | collective-permute-start | bytes 1327112 | tf_op jit(solution)/shard_map/ppermute | solution.py:549
  3.8 5.7 %copy-start.7 = (s32[1,1,32768]{2,1,0:T(1,128)S(1)}, s32[1,1,32768]{2,1,0:T(1,128)}, u32[]{:S(2)}) copy-start(s32[1,1,32768]{2,1,0:T(1,128)} %param.23) | copy-start | bytes 393220
  3.8 5.7 %copy-start.9 = (s32[1,1,32768]{2,1,0:T(1,128)S(1)}, s32[1,1,32768]{2,1,0:T(1,128)}, u32[]{:S(2)}) copy-start(s32[1,1,32768]{2,1,0:T(1,128)} %param.24) | copy-start | bytes 393220
  4.1 25.0 %copy-start.14 = (f32[3]{0:T(128)S(1)}, f32[3]{0:T(128)}, u32[]{:S(2)}) copy-start(f32[3]{0:T(128)} %constant.154) | copy-start | bytes 40
  5.0 24.0 %collective-permute-start = (f16[3,12,48,128]{3,2,1,0:T(8,128)(2,1)}, f16[3,12,48,128]{3,2,1,0:T(8,128)(2,1)}, u32[]{:S(2)}, u32[]{:S(2)}) collective-permute-start(f16[3,12,48,128]{3,2,1,0:T(8,128)(2,1)} %maximum_bitcast_fusion), channel_id=1, source_target_pairs={{0,8},{8,16},{16,24},{24,0},{1,9},{9,17},{17,25},{25,1},{2,10},{10... | collective-permute-start | bytes 1327112 | tf_op jit(solution)/shard_map/ppermute | solution.py:548
  30.5 8.7 %copy-start.15 = (f32[3]{0:T(128)S(1)}, f32[3]{0:T(128)}, u32[]{:S(2)}) copy-start(f32[3]{0:T(128)} %constant.145.clone) | copy-start | bytes 40
  36.2 2.9 %copy-start = (f32[6,25,96,128]{3,2,1,0:T(8,128)}, f32[6,25,96,128]{3,2,1,0:T(8,128)S(1)}, u32[]{:S(2)}) copy-start(f32[6,25,96,128]{3,2,1,0:T(8,128)S(1)} %get-tuple-element.29.split) | copy-start | bytes 22118404
  39.2 5.5 %copy-start.6 = (f32[1,1,32768]{2,1,0:T(1,128)S(1)}, f32[1,1,32768]{2,1,0:T(1,128)}, u32[]{:S(2)}) copy-start(f32[1,1,32768]{2,1,0:T(1,128)} %param.27) | copy-start | bytes 393220
  39.2 5.5 %copy-start.8 = (f32[4,8,128]{2,1,0:T(8,128)S(1)}, f32[4,8,128]{2,1,0:T(8,128)}, u32[]{:S(2)}) copy-start(f32[4,8,128]{2,1,0:T(8,128)} %constant.144.clone.table) | copy-start | bytes 49156
  40.1 17.0 %collective-permute-start.2 = (f16[3,5,88,128]{3,2,1,0:T(8,128)(2,1)}, f16[3,5,88,128]{3,2,1,0:T(8,128)(2,1)S(1)}, u32[]{:S(2)}, u32[]{:S(2)}) collective-permute-start(f16[3,5,88,128]{3,2,1,0:T(8,128)(2,1)} %get-tuple-element.67), channel_id=1, source_target_pairs={{0,1},{1,2},{2,3},{3,4},{4,5},{5,6},{6,7},{7,0},{8,9},{9,10},{10,1... | collective-permute-start | bytes 1013768 | tf_op jit(solution)/shard_map/ppermute | solution.py:593
  41.3 16.7 %collective-permute-start.3 = (f16[3,5,88,128]{3,2,1,0:T(8,128)(2,1)S(1)}, f16[3,5,88,128]{3,2,1,0:T(8,128)(2,1)}, u32[]{:S(2)}, u32[]{:S(2)}) collective-permute-start(f16[3,5,88,128]{3,2,1,0:T(8,128)(2,1)S(1)} %get-tuple-element.66), channel_id=1, source_target_pairs={{1,0},{2,1},{3,2},{4,3},{5,4},{6,5},{7,6},{0,7},{9,8},{10,9},{11,1... | collective-permute-start | bytes 1013768 | tf_op jit(solution)/shard_map/ppermute | solution.py:594
  59.3 3.1 %copy-start.1 = (f32[6,25,96,128]{3,2,1,0:T(8,128)S(1)}, f32[6,25,96,128]{3,2,1,0:T(8,128)}, u32[]{:S(2)}) copy-start(f32[6,25,96,128]{3,2,1,0:T(8,128)} %copy-done) | copy-start | bytes 22118404
  90.7 21.4 %copy-start.12 = (f32[3,32]{1,0:T(4,128)S(1)}, f32[3,32]{1,0:T(4,128)}, u32[]{:S(2)}) copy-start(f32[3,32]{1,0:T(4,128)} %param.21) | copy-start | bytes 1156
  90.7 21.4 %copy-start.13 = (f32[3,32]{1,0:T(4,128)S(1)}, f32[3,32]{1,0:T(4,128)}, u32[]{:S(2)}) copy-start(f32[3,32]{1,0:T(4,128)} %param.22) | copy-start | bytes 1156
  98.5 3.6 %collective-permute-start.4 = (f32[3,27,32]{2,1,0:T(8,128)S(1)}, f32[3,27,32]{2,1,0:T(8,128)S(1)}, u32[]{:S(2)}, u32[]{:S(2)}) collective-permute-start(f32[3,27,32]{2,1,0:T(8,128)S(1)} %get-tuple-element.50), channel_id=1, source_target_pairs={{8,0},{16,8},{24,16},{0,24},{9,1},{17,9},{25,17},{1,25},{10,2},{18... | collective-permute-start | bytes 31112 | tf_op jit(solution)/shard_map/ppermute | solution.py:644
  99.8 2.4 %collective-permute-start.5 = (f32[3,27,32]{2,1,0:T(8,128)S(1)}, f32[3,27,32]{2,1,0:T(8,128)S(1)}, u32[]{:S(2)}, u32[]{:S(2)}) collective-permute-start(f32[3,27,32]{2,1,0:T(8,128)S(1)} %get-tuple-element.51), channel_id=1, source_target_pairs={{0,8},{8,16},{16,24},{24,0},{1,9},{9,17},{17,25},{25,1},{2,10},{10... | collective-permute-start | bytes 31112 | tf_op jit(solution)/shard_map/ppermute | solution.py:644
  102.1 5.5 %collective-permute-start.6 = (f32[27,32]{1,0:T(8,128)S(1)}, f32[27,32]{1,0:T(8,128)S(1)}, u32[]{:S(2)}, u32[]{:S(2)}) collective-permute-start(f32[27,32]{1,0:T(8,128)S(1)} %get-tuple-element.54), channel_id=1, source_target_pairs={{1,0},{2,1},{3,2},{4,3},{5,4},{6,5},{7,6},{0,7},{9,8},{10,9},{11,1... | collective-permute-start | bytes 10376 | tf_op jit(solution)/shard_map/ppermute | solution.py:645
  106.7 5.3 %collective-permute-start.7 = (f32[27,32]{1,0:T(8,128)S(1)}, f32[27,32]{1,0:T(8,128)S(1)}, u32[]{:S(2)}, u32[]{:S(2)}) collective-permute-start(f32[27,32]{1,0:T(8,128)S(1)} %get-tuple-element.55), channel_id=1, source_target_pairs={{0,1},{1,2},{2,3},{3,4},{4,5},{5,6},{6,7},{7,0},{8,9},{9,10},{10,1... | collective-permute-start | bytes 10376 | tf_op jit(solution)/shard_map/ppermute | solution.py:645
  112.2 5.2 %collective-permute-start.8 = (f32[6,32]{1,0:T(8,128)S(1)}, f32[6,32]{1,0:T(8,128)S(1)}, u32[]{:S(2)}, u32[]{:S(2)}) collective-permute-start(f32[6,32]{1,0:T(8,128)S(1)} %get-tuple-element.59), channel_id=1, source_target_pairs={{0,1},{1,2},{2,3},{3,4},{4,5},{5,6},{6,7},{7,0},{8,9},{9,10},{10,1... | collective-permute-start | bytes 2312 | tf_op jit(solution)/shard_map/ppermute | solution.py:663
  112.3 5.1 %collective-permute-start.9 = (f32[6,32]{1,0:T(8,128)S(1)}, f32[6,32]{1,0:T(8,128)S(1)}, u32[]{:S(2)}, u32[]{:S(2)}) collective-permute-start(f32[6,32]{1,0:T(8,128)S(1)} %get-tuple-element.59), channel_id=1, source_target_pairs={{1,0},{2,1},{3,2},{4,3},{5,4},{6,5},{7,6},{0,7},{9,8},{10,9},{11,1... | collective-permute-start | bytes 2312 | tf_op jit(solution)/shard_map/ppermute | solution.py:663
  117.4 5.4 %collective-permute-start.10 = (f32[6,3,32]{2,0,1:T(8,128)S(1)}, f32[6,3,32]{2,0,1:T(8,128)S(1)}, u32[]{:S(2)}, u32[]{:S(2)}) collective-permute-start(f32[6,3,32]{2,0,1:T(8,128)S(1)} %get-tuple-element.57), channel_id=1, source_target_pairs={{0,8},{8,16},{16,24},{24,0},{1,9},{9,17},{17,25},{25,1},{2,10},{10... | collective-permute-start | bytes 6920 | tf_op jit(solution)/shard_map/ppermute | solution.py:666
  122.1 3.1 %collective-permute-start.11 = (f32[6,3,32]{2,0,1:T(8,128)S(1)}, f32[6,3,32]{2,0,1:T(8,128)S(1)}, u32[]{:S(2)}, u32[]{:S(2)}) collective-permute-start(f32[6,3,32]{2,0,1:T(8,128)S(1)} %get-tuple-element.57), channel_id=1, source_target_pairs={{8,0},{16,8},{24,16},{0,24},{9,1},{17,9},{25,17},{1,25},{10,2},{18... | collective-permute-start | bytes 6920 | tf_op jit(solution)/shard_map/ppermute | solution.py:666
  (4 other events, 7.1 us)

commit v5 on v4

--- a/solution.py
+++ b/solution.py
@@ -61,7 +61,7 @@
     return (rows + lanes_of(shape)) % 2 == 0
 
 
-def pack_kernel(pot, charge, eps, low, high, split, to_right, to_left, edges):
+def pack_kernel(pot, charge, eps, low, high, kept, to_right, to_left, split, edges, sem):
     depth, wide, _ = pot.shape
     layers = depth // 2
     last = FIRST + wide
@@ -96,6 +96,9 @@
                 (split.shape[2], 128), 1.0 if f == 2 else 0.0, F32
             )
 
+    keep = pltpu.make_async_copy(split, kept, sem)
+    keep.start()
+
     rows = slice(FIRST - HALO, last + HALO)
     lane = lanes_of((wide + 2 * HALO, 128))
     early = lane % SLOT < HALO
@@ -126,12 +129,15 @@
         return carry
 
     lax.fori_loop(0, 3 * GROUPS, strips, 0)
-
-
-def relax_kernel(split, from_left, from_right, pot_out, press_out, pa, ea, wa, pb, eb, cb, wb):
-    layers = split.shape[1] - 1
+    keep.wait()
+
+
+def relax_kernel(
+    kept, from_left, from_right, pot_out, press_out, pa, ea, ca, wa, pb, eb, cb, wb, sems
+):
+    layers = kept.shape[1] - 1
     depth, wide, _ = pot_out.shape
-    rows = split.shape[2]
+    rows = kept.shape[2]
     tiles = rows // 8
     top = MARGIN
     lane = lanes_of((8, 128))
@@ -147,26 +153,29 @@
     one = jnp.ones((rows + 2 * MARGIN, 128), F32)
     margin0 = jnp.zeros((MARGIN, 128), F32)
     margin1 = jnp.ones((MARGIN, 128), F32)
+    body = pl.ds(top, rows)
+    middle = pl.ds(1, layers + 1)
+    loads = []
+    for c in range(2):
+        loads.append(pltpu.make_async_copy(kept.at[4 + c], ea.at[c, middle, body], sems.at[c]))
+        loads.append(pltpu.make_async_copy(kept.at[2 + c], ca.at[c], sems.at[2 + c]))
+        loads.append(pltpu.make_async_copy(kept.at[c], pa.at[c, middle, body], sems.at[4 + c]))
+        for load in loads[-3:]:
+            load.start()
+
+    def set_margins(k, carry):
+        for c in range(2):
+            for start in (0, top + rows):
+                pa[c, k + 1, start:start + MARGIN, :] = margin0
+                ea[c, k + 1, start:start + MARGIN, :] = margin1
+        return carry
+
+    lax.fori_loop(0, layers + 1, set_margins, 0)
     for c in range(2):
         pa[c, 0] = zero
-        ea[c, 0] = one
-        ea[c, layers + 1] = one
-
-    def load_core(k, carry):
-        for c in range(2):
-            pa[c, k + 1, 0:top, :] = margin0
-            pa[c, k + 1, top:top + rows, :] = split[c, k]
-            pa[c, k + 1, top + rows:, :] = margin0
-            ea[c, k + 1, 0:top, :] = margin1
-            ea[c, k + 1, top:top + rows, :] = split[4 + c, k]
-            ea[c, k + 1, top + rows:, :] = margin1
-        return carry
-
-    lax.fori_loop(0, layers + 1, load_core, 0)
-    for c in range(2):
-        ea[c, 0, top:top + rows, :] = split[5 - c, 0]
-        ea[c, layers + 1, top:top + rows, :] = split[5 - c, layers - 1]
         pa[c, layers + 2] = zero
+        for start in (0, top + rows):
+            ea[c, 0, start:start + MARGIN, :] = margin1
         ea[c, layers + 2] = one
 
     first = FIRST - HALO
@@ -214,6 +223,12 @@
     for c in range(2):
         eb[c, 0] = jnp.where(lead, eb[1 - c, 1], roll(eb[c, GROUPS], SLOT))
         eb[c, GROUPS + 1] = jnp.where(tail, 1.0, roll(eb[c, 1], -SLOT))
+
+    for load in loads:
+        load.wait()
+    for c in range(2):
+        ea[c, 0, top:top + rows, :] = ea[1 - c, 1, top:top + rows, :]
+        ea[c, layers + 1, top:top + rows, :] = ea[1 - c, layers, top:top + rows, :]
 
     def around(src_a, src_b, other, color, i, t, body_a, body_b):
         r0 = top + 8 * t
@@ -260,7 +275,7 @@
                 ps = slice(top + 8 * t, top + 8 * t + 8)
 
                 def body_a(k, sides):
-                    values = coefficients(ea[c, k + 1, ps, :], split[2 + c, k, ts, :], sides)
+                    values = coefficients(ea[c, k + 1, ps, :], ca[c, k, ts, :], sides)
                     for n, value in enumerate(values):
                         wa[c, n, k, ts, :] = value
 
@@ -332,6 +347,27 @@
     r0, r1, r2 = offsets
     arms = [c0, c1, c2, r1 * c2 - r2 * c1, r2 * c0 - r0 * c2, r0 * c1 - r1 * c0]
     return arms, w
+
+
+ARM_REACH = 9.0
+ARM_BITS = 21
+ARM_STEP = 2.0 * ARM_REACH / (2**ARM_BITS - 1)
+SPARE_BITS = 32 - ARM_BITS
+
+
+def pack_arms(rb):
+    a, b, c = [jnp.round((rb[n] + ARM_REACH) * (1.0 / ARM_STEP)).astype(jnp.int32) for n in range(3)]
+    low = c & ((1 << SPARE_BITS) - 1)
+    return (a << SPARE_BITS) | low, (b << SPARE_BITS) | (c >> SPARE_BITS)
+
+
+def unpack_arms(first, second):
+    low = (1 << SPARE_BITS) - 1
+    whole = (1 << ARM_BITS) - 1
+    a = (first >> SPARE_BITS) & whole
+    b = (second >> SPARE_BITS) & whole
+    c = ((second & low) << SPARE_BITS) | (first & low)
+    return [part.astype(F32) * ARM_STEP - ARM_REACH for part in (a, b, c)]
 
 
 def store_term(stage, n, value):
@@ -426,7 +462,7 @@
 AHEAD = 4
 
 
-def press_kernel(low, passes, keys, rb0, rb1, rb2, table, press, out, stage, acc, *, per_tile):
+def press_kernel(low, passes, keys, arm0, arm1, table, press, out, stage, acc, *, per_tile):
     acc[...] = jnp.zeros_like(acc)
     for n in range(6, stage.shape[0] // 8):
         store_term(stage, n, jnp.zeros((8, 128), F32))
@@ -467,7 +503,7 @@
             code = keys[rs, :] & ((1 << KEY_BITS) - 1)
             slot = jnp.floor((code.astype(F32) + 0.5) * (1.0 / 18.0)).astype(jnp.int32)
             direction = code - 18 * slot
-            arms, w = geometry(direction, [rb0[rs, :], rb1[rs, :], rb2[rs, :]], table)
+            arms, w = geometry(direction, unpack_arms(arm0[rs, :], arm1[rs, :]), table)
             wq = w * found[j]
             for n in range(6):
                 store_term(stage, n, wq * arms[n])
@@ -566,11 +602,11 @@
     key = jnp.where(
         live, (place - (1 << 18)) * (1 << KEY_BITS) + slots * 18 + dirs, np.int32(2**31 - 1)
     )
-    keys, rb0, rb1, rb2 = lax.sort(
-        (key.reshape(-1), rb[0].reshape(-1), rb[1].reshape(-1), rb[2].reshape(-1)),
+    keys, arm0, arm1 = lax.sort(
+        (key.reshape(-1), *(part.reshape(-1) for part in pack_arms(rb))),
         num_keys=1, is_stable=False,
     )
-    keys, rb0, rb1, rb2, low, high = lax.optimization_barrier((keys, rb0, rb1, rb2, low, high))
+    keys, arm0, arm1, low, high = lax.optimization_barrier((keys, arm0, arm1, low, high))
     keys = keys.reshape(lines, 128)
     table = direction_table()
     table_rows = ((keys >> KEY_BITS) + (1 << 18)) >> 7
@@ -586,15 +622,20 @@
             jax.ShapeDtypeStruct((3, GROUPS, wide + 2 * HALO, 128), F32),
             jax.ShapeDtypeStruct((3, GROUPS, wide + 2 * HALO, 128), F32),
         ),
-        in_specs=vmem(5), out_specs=tuple(vmem(3)), compiler_params=grant(24), name="pack",
-        scratch_shapes=[pltpu.VMEM((2, 3 * GROUPS, wide + 2 * HALO, 128), F32)],
+        in_specs=vmem(5), out_specs=(pl.BlockSpec(memory_space=pltpu.HBM), *vmem(2)),
+        compiler_params=grant(52), name="pack",
+        scratch_shapes=[
+            pltpu.VMEM((6, layers + 1, rows, 128), F32),
+            pltpu.VMEM((2, 3 * GROUPS, wide + 2 * HALO, 128), F32),
+            pltpu.SemaphoreType.DMA,
+        ],
     )(potential_start, charge, eps_field,
       from_half(low).reshape(-1, 128), from_half(high).reshape(-1, 128))
-    from_left = lax.ppermute(to_half(to_right), "gy", fy)
+    to_right, dirs_late = lax.optimization_barrier((to_half(to_right), dirs))
+    from_left = lax.ppermute(to_right, "gy", fy)
     from_right = lax.ppermute(to_half(to_left), "gy", by)
 
     terms = 32
-    dirs_late, split = lax.optimization_barrier((dirs, split))
     fixed, reach = pl.pallas_call(
         functools.partial(fixed_kernel, width=width),
         out_shape=(
@@ -613,29 +654,31 @@
             jax.ShapeDtypeStruct((depth, wide, 128), F32),
             jax.ShapeDtypeStruct((depth + 1, wide, 128), F32),
         ),
-        in_specs=vmem(3), out_specs=tuple(vmem(2)),
+        in_specs=[pl.BlockSpec(memory_space=pltpu.HBM)] + vmem(2), out_specs=tuple(vmem(2)),
         scratch_shapes=[
             pltpu.VMEM((2, layers + 3, tall, 128), F32),
             pltpu.VMEM((2, layers + 3, tall, 128), F32),
+            pltpu.VMEM((2, layers + 1, rows, 128), F32),
             pltpu.VMEM((2, 7, layers + 1, rows, 128), F32),
             pltpu.VMEM((2, GROUPS + 2, tall, 128), F32),
             pltpu.VMEM((2, GROUPS + 2, tall, 128), F32),
             pltpu.VMEM((2, GROUPS, rows, 128), F32),
             pltpu.VMEM((2, 7, GROUPS, rows, 128), F32),
+            pltpu.SemaphoreType.DMA((6,)),
         ],
-        compiler_params=grant(44), name="relax",
+        compiler_params=grant(48), name="relax",
     )(split, from_half(from_left), from_half(from_right))
 
     smem = pl.BlockSpec(memory_space=pltpu.SMEM)
     pressed = pl.pallas_call(
         functools.partial(press_kernel, per_tile=per_tile),
         out_shape=jax.ShapeDtypeStruct((9, 8, per_tile), F32),
-        in_specs=[smem, smem] + vmem(6), out_specs=vmem(1)[0],
+        in_specs=[smem, smem] + vmem(5), out_specs=vmem(1)[0],
         scratch_shapes=[pltpu.VMEM((64, 128), F32), pltpu.VMEM((9 * 16, per_tile), F32)],
         compiler_params=grant(8), name="press",
     )(
-        row_low, passes, keys, rb0.reshape(lines, 128), rb1.reshape(lines, 128),
-        rb2.reshape(lines, 128), table, press.reshape(-1, 128),
+        row_low, passes, keys, arm0.reshape(lines, 128), arm1.reshape(lines, 128),
+        table, press.reshape(-1, 128),
     )
 
     fixed = fixed.reshape(terms, 9, per_tile).transpose(1, 0, 2)

time: 128 us -> 119 us (0.930)
  local copies, waits for them, and re-layouts: 9.97 us -> 2.49 us
  other arithmetic: 27.7 us -> 22.3 us
  Pallas kernels: 55.7 us -> 60.4 us
    unnamed x32 -> x26, local copies, waits for them, and re-layouts: 7.22 us -> 0.5 us
    pallas_call x1, Pallas kernels: 5.73 us -> 8.36 us  [shards(): pl.pallas_call(pack_kernel, out_shape=(jax.ShapeDtypeStruct((6, layers +...]
    pallas_call x1, Pallas kernels: 28.3 us -> 30.3 us  [shards(): pl.pallas_call(relax_kernel, out_shape=(jax.ShapeDtypeStruct((depth, wide...]
    convert_element_type x2, other arithmetic: 1.84 us -> 0.28 us  [edge(): return strips.transpose(0, 2, 1, 3).astype(HALF)]
  transfers between devices with their start and end apart: 12 -> 12, of which waited for: 7 -> 7; matrix products, arithmetic and copies ran while one was open for 19% -> 16% of each run, Pallas kernels for 9% -> 10%
where the time goes in v5:
time: 119 us
  Pallas kernels  60.4 us (51%)
  other arithmetic  22.3 us (19%)
  starting transfers between devices  21.7 us (18%)
  waiting for transfers between devices  11.3 us (9%)
  local copies, waits for them, and re-layouts  2.49 us (2%)
    pallas_call x1, Pallas kernels, shards(): pl.pallas_call(relax_kernel, out_shape=(jax.ShapeDtypeStruct((depth, wide...  30.3 us
    sort x1, other arithmetic, shards(): lax.sort((key.reshape(-1), *(part.reshape(-1) for part in pack_arms(rb)))...  15.9 us
    pallas_call x1, Pallas kernels, shards(): pl.pallas_call(functools.partial(fixed_kernel, width=width), out_shape=(j...  11.9 us
    pallas_call x1, Pallas kernels, shards(): pl.pallas_call(pack_kernel, out_shape=(jax.ShapeDtypeStruct((6, layers +...  8.36 us
    pallas_call x1, Pallas kernels, shards(): pl.pallas_call(functools.partial(press_kernel, per_tile=per_tile), out_sh...  7.82 us
    ppermute x1, waiting for transfers between devices, shards(): lax.ppermute(mid[2], 'gy', fy)  4.42 us
    ppermute x1, starting transfers between devices, shards(): lax.ppermute(new_motion, 'gy', by)  4.15 us
    ppermute x1, starting transfers between devices, shards(): lax.ppermute(mid[0], 'gy', by)  4.06 us
  transfers between devices with their start and end apart: 12, of which 7 were waited for; matrix products, arithmetic and copies ran while one was open for 16% of the time, Pallas kernels for 10%

profile of v5, /device:TPU:1, one launch (start us, length us, event | category | flops | bytes accessed | tf_op | source)
XLA Modules:
  0.0 119.3 jit_solution(14249533433498148279)
XLA Ops:
  0.7 1.3 %fusion.61 = (f32[48,12,128]{2,1,0:T(8,128)S(1)}, f32[48,12,128]{2,1,0:T(8,128)S(1)}) fusion(f32[48,64,128]{2,1,0:T(8,128)} %pot.1), kind=kLoop, calls=%fused_computation.150 | loop fusion | bytes 1179648 | tf_op jit(solution)/shard_map/slice | solution.py:578
  3.5 2.7 %collective-permute-start = (f16[3,12,48,128]{3,2,1,0:T(8,128)(2,1)S(1)}, f16[3,12,48,128]{3,2,1,0:T(8,128)(2,1)}, u32[]{:S(2)}, u32[]{:S(2)}) collective-permute-start(f16[3,12,48,128]{3,2,1,0:T(8,128)(2,1)S(1)} %maximum_bitcast_fusion), channel_id=1, source_target_pairs={{0,8},{8,16},{16,24},{24,0},{1,9},{9,17},{17,25},{25,1},{2,10},{10... | collective-permute-start | bytes 1327112 | tf_op jit(solution)/shard_map/ppermute | solution.py:584
  6.2 0.6 shift-right-arithmetic_or_fusion
  7.4 15.9 %sort.21 = (s32[32768]{0:T(1024)S(1)}, s32[32768]{0:T(1024)S(1)}, s32[32768]{0:T(1024)S(1)}) sort(s32[32768]{0:T(1024)S(1)} %fusion.21, s32[32768]{0:T(1024)S(1)} %bitcast.70, s32[32768]{0:T(1024)S(1)} %bitcast.69), dimensions={0}, to_apply=%region_0.1 | sort | flops 491520 | bytes 786432 | tf_op jit(solution)/shard_map/sort | solution.py:605
  23.7 2.5 %convert_multiply_fusion = (f32[3,12,48,128]{3,2,1,0:T(8,128)}, f32[3,12,48,128]{3,2,1,0:T(8,128)}) fusion(f16[3,12,48,128]{3,2,1,0:T(8,128)(2,1)S(1)} %collective-permute-done.1, f32[3]{0:T(128)S(1)} %copy-done.11, f16[3,12,48,128]{3,2,1,0:T(8,128)(2,1)} %collective-permute-done), kind=kLoop, calls=%fused_computation | loop fusion | flops 884736 | bytes 2654220 | tf_op jit(solution)/shard_map/mul | solution.py:555
  26.3 8.4 %pack.1 = (f32[6,25,96,128]{3,2,1,0:T(8,128)}, f32[3,5,88,128]{3,2,1,0:T(8,128)S(1)}, f32[3,5,88,128]{3,2,1,0:T(8,128)S(1)}) custom-call(f32[48,64,128]{2,1,0:T(8,128)} %pot.1, f32[48,64,128]{2,1,0:T(8,128)} %charge.1, bf16[48,64,128]{2,1,0:T(8,128)(2,1)} %eps.1, f32[1728,128]{1,0:T(8,128)} %bitcast.65, f32[1728,128]{1,0:T(8,128)} %bitcast.64), custom_call_target="tpu_custom_call" | custom-call | tf_op jit(solution)/shard_map/pack/pallas_call | solution.py:618
  34.9 1.3 %collective-permute-start.2 = (f16[3,5,88,128]{3,2,1,0:T(8,128)(2,1)S(1)}, f16[3,5,88,128]{3,2,1,0:T(8,128)(2,1)S(1)}, u32[]{:S(2)}, u32[]{:S(2)}) collective-permute-start(f16[3,5,88,128]{3,2,1,0:T(8,128)(2,1)S(1)} %get-tuple-element.27), channel_id=1, source_target_pairs={{0,1},{1,2},{2,3},{3,4},{4,5},{5,6},{6,7},{7,0},{8,9},{9,10},{10,1... | collective-permute-start | bytes 1013768 | tf_op jit(solution)/shard_map/ppermute | solution.py:635
  36.2 3.1 %collective-permute-start.3 = (f16[3,5,88,128]{3,2,1,0:T(8,128)(2,1)S(1)}, f16[3,5,88,128]{3,2,1,0:T(8,128)(2,1)S(1)}, u32[]{:S(2)}, u32[]{:S(2)}) collective-permute-start(f16[3,5,88,128]{3,2,1,0:T(8,128)(2,1)S(1)} %get-tuple-element.61), channel_id=1, source_target_pairs={{1,0},{2,1},{3,2},{4,3},{5,4},{6,5},{7,6},{0,7},{9,8},{10,9},{11,1... | collective-permute-start | bytes 1013768 | tf_op jit(solution)/shard_map/ppermute | solution.py:636
  39.5 11.9 %fixed.1 = (f32[32,288]{1,0:T(8,128)S(1)}, f32[6,256,128]{2,1,0:T(8,128)S(1)}) custom-call(s32[256,128]{1,0:T(8,128)S(1)} %fusion.32.slots, s32[256,128]{1,0:T(8,128)S(1)} %bitcast.63, f32[256,128]{1,0:T(8,128)S(1)} %bitcast.58, f32[3,256,128]{2,1,0:T(8,128)S(1)} %bitcast.57, f32[4,8,128]{2,1,0:T(8,128)S(1)} %copy-done.3), custom_call_target="tpu_custom_call" | custom-call | flops 1000000000 | bytes 20000000 | tf_op jit(solution)/shard_map/fixed/pallas_call | solution.py:639
  52.0 0.8 collective-permute-done.3
  53.0 30.3 %relax.1 = (f32[48,64,128]{2,1,0:T(8,128)}, f32[49,64,128]{2,1,0:T(8,128)S(1)}) custom-call(f32[6,25,96,128]{3,2,1,0:T(8,128)} %get-tuple-element.25.kept, f32[3,5,88,128]{3,2,1,0:T(8,128)S(1)} %get-tuple-element.60.from_left, f32[3,5,88,128]{3,2,1,0:T(8,128)S(1)} %get-tuple-element.59.from_right), custom_call_target="tpu_custom_call" | custom-call | tf_op jit(solution)/shard_map/relax/pallas_call | solution.py:651
  83.3 7.8 %press.1 = f32[9,8,32]{2,1,0:T(8,128)S(1)} custom-call(s32[256]{0:T(256)S(1)} %fusion.37.low, s32[4]{0:T(128)S(1)} %and_select_fusion.passes, s32[256,128]{1,0:T(8,128)S(1)} %bitcast.56, s32[256,128]{1,0:T(8,128)S(1)} %bitcast.60, s32[256,128]{1,0:T(8,128)S(1)} %bitcast.61, f32[4,8,128]{2,1,0:T(8,128)S(1)} %copy-done.3, f32[3136,128]{1,0:T(8,128)S(1)} %bitcast.55), custom_call_target="tpu_custom_call" | custom-call | tf_op jit(solution)/shard_map/press/pallas_call | solution.py:673
  91.2 1.1 collective-permute-start.4
  92.3 1.5 %collective-permute-start.5 = (f32[3,27,32]{2,1,0:T(8,128)S(1)}, f32[3,27,32]{2,1,0:T(8,128)S(1)}, u32[]{:S(2)}, u32[]{:S(2)}) collective-permute-start(f32[3,27,32]{2,1,0:T(8,128)S(1)} %get-tuple-element.46), channel_id=1, source_target_pairs={{0,8},{8,16},{16,24},{24,0},{1,9},{9,17},{17,25},{25,1},{2,10},{10... | collective-permute-start | bytes 31112 | tf_op jit(solution)/shard_map/ppermute | solution.py:687
  93.8 1.7 %collective-permute-done.4 = f32[3,27,32]{2,1,0:T(8,128)S(1)} collective-permute-done((f32[3,27,32]{2,1,0:T(8,128)S(1)}, f32[3,27,32]{2,1,0:T(8,128)S(1)}, u32[]{:S(2)}, u32[]{:S(2)}) %collective-permute-start.4) | collective-permute-done | bytes 10400 | tf_op jit(solution)/shard_map/ppermute | solution.py:687
  95.5 4.1 %collective-permute-start.6 = (f32[27,32]{1,0:T(8,128)S(1)}, f32[27,32]{1,0:T(8,128)S(1)}, u32[]{:S(2)}, u32[]{:S(2)}) collective-permute-start(f32[27,32]{1,0:T(8,128)S(1)} %get-tuple-element.49), channel_id=1, source_target_pairs={{1,0},{2,1},{3,2},{4,3},{5,4},{6,5},{7,6},{0,7},{9,8},{10,9},{11,1... | collective-permute-start | bytes 10376 | tf_op jit(solution)/shard_map/ppermute | solution.py:688
  99.6 0.9 collective-permute-done.6
  100.5 4.4 %collective-permute-done.7 = f32[27,32]{1,0:T(8,128)S(1)} collective-permute-done((f32[27,32]{1,0:T(8,128)S(1)}, f32[27,32]{1,0:T(8,128)S(1)}, u32[]{:S(2)}, u32[]{:S(2)}) %collective-permute-start.7) | collective-permute-done | bytes 3488 | tf_op jit(solution)/shard_map/ppermute | solution.py:688
  105.1 4.1 %collective-permute-start.9 = (f32[6,32]{1,0:T(8,128)S(1)}, f32[6,32]{1,0:T(8,128)S(1)}, u32[]{:S(2)}, u32[]{:S(2)}) collective-permute-start(f32[6,32]{1,0:T(8,128)S(1)} %get-tuple-element.54), channel_id=1, source_target_pairs={{1,0},{2,1},{3,2},{4,3},{5,4},{6,5},{7,6},{0,7},{9,8},{10,9},{11,1... | collective-permute-start | bytes 2312 | tf_op jit(solution)/shard_map/ppermute | solution.py:706
  109.3 1.0 collective-permute-done.8
  110.3 3.8 %collective-permute-start.10 = (f32[6,3,32]{2,0,1:T(8,128)S(1)}, f32[6,3,32]{2,0,1:T(8,128)S(1)}, u32[]{:S(2)}, u32[]{:S(2)}) collective-permute-start(f32[6,3,32]{2,0,1:T(8,128)S(1)} %get-tuple-element.52), channel_id=1, source_target_pairs={{0,8},{8,16},{16,24},{24,0},{1,9},{9,17},{17,25},{25,1},{2,10},{10... | collective-permute-start | bytes 6920 | tf_op jit(solution)/shard_map/ppermute | solution.py:709
  114.1 0.6 pad_maximum_fusion.3
  114.9 2.3 %collective-permute-done.11 = f32[6,3,32]{2,0,1:T(8,128)S(1)} collective-permute-done((f32[6,3,32]{2,0,1:T(8,128)S(1)}, f32[6,3,32]{2,0,1:T(8,128)S(1)}, u32[]{:S(2)}, u32[]{:S(2)}) %collective-permute-start.11) | collective-permute-done | bytes 2336 | tf_op jit(solution)/shard_map/ppermute | solution.py:709
  117.3 2.0 %reflect.1 = f32[256,128]{1,0:T(8,128)} custom-call(s32[256,128]{1,0:T(8,128)S(1)} %fusion.32.slots, f32[6,256,128]{2,1,0:T(8,128)S(1)} %get-tuple-element.36.reach, f32[256,128]{1,0:T(8,128)S(1)} %bitcast.59, f32[6,3,128]{2,1,0:T(4,128)S(1)} %reshape.140.motion), custom_call_target="tpu_custom_call" | custom-call | tf_op jit(solution)/shard_map/reflect/pallas_call | solution.py:713
  (79 shorter events, 4.2 us)
Async XLA Ops:
  0.6 1.8 %copy-start.5 = (bf16[48,64,128]{2,1,0:T(8,128)(2,1)S(1)}, bf16[48,64,128]{2,1,0:T(8,128)(2,1)}, u32[]{:S(2)}) copy-start(bf16[48,64,128]{2,1,0:T(8,128)(2,1)} %eps.1) | copy-start | bytes 2359300
  2.8 3.4 %copy-start = (f32[3,1,1,32768]{3,2,1,0:T(1,128)S(1)}, f32[3,1,1,32768]{3,2,1,0:T(1,128)}, u32[]{:S(2)}) copy-start(f32[3,1,1,32768]{3,2,1,0:T(1,128)} %param.28) | copy-start | bytes 1179652
  3.0 3.8 %copy-start.7 = (s32[1,1,32768]{2,1,0:T(1,128)S(1)}, s32[1,1,32768]{2,1,0:T(1,128)}, u32[]{:S(2)}) copy-start(s32[1,1,32768]{2,1,0:T(1,128)} %param.25) | copy-start | bytes 393220
  3.0 3.8 %copy-start.8 = (s32[1,1,32768]{2,1,0:T(1,128)S(1)}, s32[1,1,32768]{2,1,0:T(1,128)}, u32[]{:S(2)}) copy-start(s32[1,1,32768]{2,1,0:T(1,128)} %param.26) | copy-start | bytes 393220
  3.0 20.7 %collective-permute-start.1 = (f16[3,12,48,128]{3,2,1,0:T(8,128)(2,1)S(1)}, f16[3,12,48,128]{3,2,1,0:T(8,128)(2,1)S(1)}, u32[]{:S(2)}, u32[]{:S(2)}) collective-permute-start(f16[3,12,48,128]{3,2,1,0:T(8,128)(2,1)S(1)} %maximum_bitcast_fusion.1), channel_id=1, source_target_pairs={{8,0},{16,8},{24,16},{0,24},{9,1},{17,9},{25,17},{1,25},{10,2},{18... | collective-permute-start | bytes 1327112 | tf_op jit(solution)/shard_map/ppermute | solution.py:585
  3.1 3.9 %copy-start.2 = (s32[1,1,32768]{2,1,0:T(1,128)S(1)}, s32[1,1,32768]{2,1,0:T(1,128)}, u32[]{:S(2)}) copy-start(s32[1,1,32768]{2,1,0:T(1,128)} %param.23) | copy-start | bytes 393220
  3.1 3.9 %copy-start.6 = (s32[1,1,32768]{2,1,0:T(1,128)S(1)}, s32[1,1,32768]{2,1,0:T(1,128)}, u32[]{:S(2)}) copy-start(s32[1,1,32768]{2,1,0:T(1,128)} %param.24) | copy-start | bytes 393220
  3.4 20.3 %copy-start.11 = (f32[3]{0:T(128)S(1)}, f32[3]{0:T(128)}, u32[]{:S(2)}) copy-start(f32[3]{0:T(128)} %constant.162) | copy-start | bytes 40
  3.5 20.2 %collective-permute-start = (f16[3,12,48,128]{3,2,1,0:T(8,128)(2,1)S(1)}, f16[3,12,48,128]{3,2,1,0:T(8,128)(2,1)}, u32[]{:S(2)}, u32[]{:S(2)}) collective-permute-start(f16[3,12,48,128]{3,2,1,0:T(8,128)(2,1)S(1)} %maximum_bitcast_fusion), channel_id=1, source_target_pairs={{0,8},{8,16},{16,24},{24,0},{1,9},{9,17},{17,25},{25,1},{2,10},{10... | collective-permute-start | bytes 1327112 | tf_op jit(solution)/shard_map/ppermute | solution.py:584
  26.3 8.4 %copy-start.12 = (f32[3]{0:T(128)S(1)}, f32[3]{0:T(128)}, u32[]{:S(2)}) copy-start(f32[3]{0:T(128)} %constant.153.clone) | copy-start | bytes 40
  34.6 4.9 %copy-start.1 = (f32[1,1,32768]{2,1,0:T(1,128)S(1)}, f32[1,1,32768]{2,1,0:T(1,128)}, u32[]{:S(2)}) copy-start(f32[1,1,32768]{2,1,0:T(1,128)} %param.27) | copy-start | bytes 393220
  34.6 4.9 %copy-start.3 = (f32[4,8,128]{2,1,0:T(8,128)S(1)}, f32[4,8,128]{2,1,0:T(8,128)}, u32[]{:S(2)}) copy-start(f32[4,8,128]{2,1,0:T(8,128)} %constant.152.clone.table) | copy-start | bytes 49156
  34.9 17.1 %collective-permute-start.2 = (f16[3,5,88,128]{3,2,1,0:T(8,128)(2,1)S(1)}, f16[3,5,88,128]{3,2,1,0:T(8,128)(2,1)S(1)}, u32[]{:S(2)}, u32[]{:S(2)}) collective-permute-start(f16[3,5,88,128]{3,2,1,0:T(8,128)(2,1)S(1)} %get-tuple-element.27), channel_id=1, source_target_pairs={{0,1},{1,2},{2,3},{3,4},{4,5},{5,6},{6,7},{7,0},{8,9},{9,10},{10,1... | collective-permute-start | bytes 1013768 | tf_op jit(solution)/shard_map/ppermute | solution.py:635
  36.2 16.6 %collective-permute-start.3 = (f16[3,5,88,128]{3,2,1,0:T(8,128)(2,1)S(1)}, f16[3,5,88,128]{3,2,1,0:T(8,128)(2,1)S(1)}, u32[]{:S(2)}, u32[]{:S(2)}) collective-permute-start(f16[3,5,88,128]{3,2,1,0:T(8,128)(2,1)S(1)} %get-tuple-element.61), channel_id=1, source_target_pairs={{1,0},{2,1},{3,2},{4,3},{5,4},{6,5},{7,6},{0,7},{9,8},{10,9},{11,1... | collective-permute-start | bytes 1013768 | tf_op jit(solution)/shard_map/ppermute | solution.py:636
  83.3 21.6 %copy-start.9 = (f32[3,32]{1,0:T(4,128)S(1)}, f32[3,32]{1,0:T(4,128)}, u32[]{:S(2)}) copy-start(f32[3,32]{1,0:T(4,128)} %param.21) | copy-start | bytes 1156
  83.3 21.6 %copy-start.10 = (f32[3,32]{1,0:T(4,128)S(1)}, f32[3,32]{1,0:T(4,128)}, u32[]{:S(2)}) copy-start(f32[3,32]{1,0:T(4,128)} %param.22) | copy-start | bytes 1156
  91.2 4.3 %collective-permute-start.4 = (f32[3,27,32]{2,1,0:T(8,128)S(1)}, f32[3,27,32]{2,1,0:T(8,128)S(1)}, u32[]{:S(2)}, u32[]{:S(2)}) collective-permute-start(f32[3,27,32]{2,1,0:T(8,128)S(1)} %get-tuple-element.45), channel_id=1, source_target_pairs={{8,0},{16,8},{24,16},{0,24},{9,1},{17,9},{25,17},{1,25},{10,2},{18... | collective-permute-start | bytes 31112 | tf_op jit(solution)/shard_map/ppermute | solution.py:687
  92.3 3.2 %collective-permute-start.5 = (f32[3,27,32]{2,1,0:T(8,128)S(1)}, f32[3,27,32]{2,1,0:T(8,128)S(1)}, u32[]{:S(2)}, u32[]{:S(2)}) collective-permute-start(f32[3,27,32]{2,1,0:T(8,128)S(1)} %get-tuple-element.46), channel_id=1, source_target_pairs={{0,8},{8,16},{16,24},{24,0},{1,9},{9,17},{17,25},{25,1},{2,10},{10... | collective-permute-start | bytes 31112 | tf_op jit(solution)/shard_map/ppermute | solution.py:687
  95.5 4.9 %collective-permute-start.6 = (f32[27,32]{1,0:T(8,128)S(1)}, f32[27,32]{1,0:T(8,128)S(1)}, u32[]{:S(2)}, u32[]{:S(2)}) collective-permute-start(f32[27,32]{1,0:T(8,128)S(1)} %get-tuple-element.49), channel_id=1, source_target_pairs={{1,0},{2,1},{3,2},{4,3},{5,4},{6,5},{7,6},{0,7},{9,8},{10,9},{11,1... | collective-permute-start | bytes 10376 | tf_op jit(solution)/shard_map/ppermute | solution.py:688
  99.6 5.3 %collective-permute-start.7 = (f32[27,32]{1,0:T(8,128)S(1)}, f32[27,32]{1,0:T(8,128)S(1)}, u32[]{:S(2)}, u32[]{:S(2)}) collective-permute-start(f32[27,32]{1,0:T(8,128)S(1)} %get-tuple-element.50), channel_id=1, source_target_pairs={{0,1},{1,2},{2,3},{3,4},{4,5},{5,6},{6,7},{7,0},{8,9},{9,10},{10,1... | collective-permute-start | bytes 10376 | tf_op jit(solution)/shard_map/ppermute | solution.py:688
  105.1 5.2 %collective-permute-start.8 = (f32[6,32]{1,0:T(8,128)S(1)}, f32[6,32]{1,0:T(8,128)S(1)}, u32[]{:S(2)}, u32[]{:S(2)}) collective-permute-start(f32[6,32]{1,0:T(8,128)S(1)} %get-tuple-element.54), channel_id=1, source_target_pairs={{0,1},{1,2},{2,3},{3,4},{4,5},{5,6},{6,7},{7,0},{8,9},{9,10},{10,1... | collective-permute-start | bytes 2312 | tf_op jit(solution)/shard_map/ppermute | solution.py:706
  105.1 5.1 %collective-permute-start.9 = (f32[6,32]{1,0:T(8,128)S(1)}, f32[6,32]{1,0:T(8,128)S(1)}, u32[]{:S(2)}, u32[]{:S(2)}) collective-permute-start(f32[6,32]{1,0:T(8,128)S(1)} %get-tuple-element.54), channel_id=1, source_target_pairs={{1,0},{2,1},{3,2},{4,3},{5,4},{6,5},{7,6},{0,7},{9,8},{10,9},{11,1... | collective-permute-start | bytes 2312 | tf_op jit(solution)/shard_map/ppermute | solution.py:706
  110.3 4.6 %collective-permute-start.10 = (f32[6,3,32]{2,0,1:T(8,128)S(1)}, f32[6,3,32]{2,0,1:T(8,128)S(1)}, u32[]{:S(2)}, u32[]{:S(2)}) collective-permute-start(f32[6,3,32]{2,0,1:T(8,128)S(1)} %get-tuple-element.52), channel_id=1, source_target_pairs={{0,8},{8,16},{16,24},{24,0},{1,9},{9,17},{17,25},{25,1},{2,10},{10... | collective-permute-start | bytes 6920 | tf_op jit(solution)/shard_map/ppermute | solution.py:709
  114.1 3.1 %collective-permute-start.11 = (f32[6,3,32]{2,0,1:T(8,128)S(1)}, f32[6,3,32]{2,0,1:T(8,128)S(1)}, u32[]{:S(2)}, u32[]{:S(2)}) collective-permute-start(f32[6,3,32]{2,0,1:T(8,128)S(1)} %get-tuple-element.52), channel_id=1, source_target_pairs={{8,0},{16,8},{24,16},{0,24},{9,1},{17,9},{25,17},{1,25},{10,2},{18... | collective-permute-start | bytes 6920 | tf_op jit(solution)/shard_map/ppermute | solution.py:709
  (1 other events, 1.7 us)

commit v6 on v5

--- a/solution.py
+++ b/solution.py
@@ -515,9 +515,37 @@
 
 
 TOGETHER = 4
-
-
-def reflect_kernel(slots, reach, pops, motion, out):
+AROUND = [(ox, oy) for ox in range(-2, 3) for oy in range(-2, 3)]
+
+
+def reflect_kernel(
+    home, partial_sums, slots, reach, pops, motion, report, out, *, per_tile, counts
+):
+    lanes = motion.shape[1]
+    slot_of_lane = lax.broadcasted_iota(jnp.int32, (8, lanes), 1) // per_tile
+    tile_x = slot_of_lane // 3 - 1
+    tile_y = slot_of_lane % 3 - 1
+    totals = jnp.zeros((8, lanes), F32)
+    for ox, oy in AROUND:
+        near = (abs(tile_x - ox) <= 1) & (abs(tile_y - oy) <= 1) & (slot_of_lane < 9)
+        shift = per_tile * (3 * ox + oy)
+        peer_x = lax.rem(home[0] + ox + 2 * counts[0], counts[0])
+        peer_y = lax.rem(home[1] + oy + 2 * counts[1], counts[1])
+        peer = peer_x * counts[1] + peer_y
+        moved = pltpu.roll(partial_sums[peer], shift % lanes, 1)
+        totals = totals + jnp.where(near, moved, 0.0)
+    mass = 4.0 / 3.0 * math.pi * RADIUS**3
+    inertia = 0.4 * mass * RADIUS**2
+    is_force = lax.broadcasted_iota(jnp.int32, (8, lanes), 0) < 3
+    moved = motion[...] + totals * jnp.where(is_force, 1.0 / mass, 1.0 / inertia)
+    stated = totals * jnp.where(is_force, 1.0, 1.0 / RADIUS)
+    report[...] = stated[0:6, 4 * per_tile:5 * per_tile]
+
+    table = [
+        [jnp.broadcast_to(moved[n:n + 1, 128 * h:128 * h + 128], (8, 128)) for h in range(lanes // 128)]
+        for n in range(6)
+    ]
+
     def batch(b, carry):
         for j in range(TOGETHER):
             rs = pl.ds(pl.multiple_of(8 * (TOGETHER * b + j), 8), 8)
@@ -527,9 +555,8 @@
             along = jnp.zeros((8, 128), F32)
             for n in range(6):
                 value = jnp.zeros((8, 128), F32)
-                for h in range(motion.shape[1]):
-                    line = jnp.broadcast_to(motion[n, h:h + 1, :], (8, 128))
-                    value = jnp.where(part == h, lane_pick(line, lane), value)
+                for h in range(lanes // 128):
+                    value = jnp.where(part == h, lane_pick(table[n][h], lane), value)
                 along += reach[n, rs, :] * value
             out[rs, :] = pops[rs, :] - along
         return carry
@@ -553,6 +580,24 @@
 
 def from_half(strips):
     return strips.astype(F32) * (1.0 / scales())
+
+
+MOTION_SCALE = 2.0**10
+REST_SCALE = 2.0**12
+
+
+def motion_plane(motions, rows):
+    value = motions.reshape(-1, motions.shape[-1]) * MOTION_SCALE
+    head = lax.reduce_precision(value, 8, 10)
+    both = jnp.concatenate([head, (value - head) * REST_SCALE], axis=0).astype(HALF)
+    return jnp.pad(both, ((0, rows - both.shape[0]), (0, 128 - both.shape[1])))[None]
+
+
+def motion_of(plane, shape):
+    count = math.prod(shape[:-1])
+    both = plane[:2 * count, :shape[-1]].astype(F32)
+    value = both[:count] + both[count:] * (1.0 / REST_SCALE)
+    return (value * (1.0 / MOTION_SCALE)).reshape(shape)
 
 
 def vmem(n):
@@ -573,18 +618,20 @@
     fx, bx = ring("gx")
     fy, by = ring("gy")
 
+    per_tile = colloid_vel.shape[1]
+    motion = jnp.concatenate([colloid_vel, colloid_spin], axis=0)
     def edge(part):
         strips = jnp.stack([
             potential_start[:, part] * POT_SCALE,
             charge[:, part] * CHARGE_SCALE,
             eps_field[:, part].astype(F32),
         ])
-        return strips.transpose(0, 2, 1, 3).astype(HALF)
+        strips = strips.transpose(0, 2, 1, 3).astype(HALF).reshape(3 * HALO, depth, 128)
+        return jnp.concatenate([strips, motion_plane(motion, depth)], axis=0)
 
     low = lax.ppermute(edge(slice(wide - HALO, wide)), "gx", fx)
     high = lax.ppermute(edge(slice(0, HALO)), "gx", bx)
 
-    per_tile = colloid_vel.shape[1]
     width = 9 * per_tile
     count = link_pop.shape[-1]
     lines = count // 128
@@ -630,10 +677,24 @@
             pltpu.SemaphoreType.DMA,
         ],
     )(potential_start, charge, eps_field,
-      from_half(low).reshape(-1, 128), from_half(high).reshape(-1, 128))
-    to_right, dirs_late = lax.optimization_barrier((to_half(to_right), dirs))
+      *(from_half(part[:-1].reshape(3, HALO, depth, 128)).reshape(-1, 128) for part in (low, high)))
+    row = jnp.stack([
+        motion_of(low[-1], motion.shape), motion, motion_of(high[-1], motion.shape)
+    ])
+    plane = motion_plane(row, wide + 2 * HALO)
+
+    def strip(part):
+        return jnp.concatenate([to_half(part).reshape(-1, *part.shape[2:]), plane], axis=0)
+
+    to_right, dirs_late = lax.optimization_barrier((strip(to_right), dirs))
     from_left = lax.ppermute(to_right, "gy", fy)
-    from_right = lax.ppermute(to_half(to_left), "gy", by)
+    from_right = lax.ppermute(strip(to_left), "gy", by)
+    shape = (3, GROUPS, wide + 2 * HALO, 128)
+    west, east = [from_half(part[:-1].reshape(shape)) for part in (from_left, from_right)]
+    near_motion = jnp.stack(
+        [motion_of(from_left[-1], row.shape), row, motion_of(from_right[-1], row.shape)], axis=1
+    )
+    near_motion = near_motion.transpose(2, 0, 1, 3).reshape(6, width)
 
     terms = 32
     fixed, reach = pl.pallas_call(
@@ -667,7 +728,7 @@
             pltpu.SemaphoreType.DMA((6,)),
         ],
         compiler_params=grant(48), name="relax",
-    )(split, from_half(from_left), from_half(from_right))
+    )(split, west, east)
 
     smem = pl.BlockSpec(memory_space=pltpu.SMEM)
     pressed = pl.pallas_call(
@@ -681,40 +742,30 @@
         table, press.reshape(-1, 128),
     )
 
-    fixed = fixed.reshape(terms, 9, per_tile).transpose(1, 0, 2)
-    sums = jnp.concatenate([fixed[:, 0:6] + pressed[:, 0:6], fixed[:, 6:27]], axis=1)
-    sums = sums.reshape(3, 3, 27, per_tile)
-    mid = sums[1] + lax.ppermute(sums[0], "gx", bx) + lax.ppermute(sums[2], "gx", fx)
-    mine = mid[1] + lax.ppermute(mid[0], "gy", by) + lax.ppermute(mid[2], "gy", fy)
-    motion = jnp.concatenate([colloid_vel, colloid_spin], axis=0)
     drag = []
     for a in range(6):
-        line = jnp.zeros_like(motion[0])
+        line = jnp.zeros((width,), F32)
         for d in range(6):
             n = PAIRS.index((min(a, d), max(a, d)))
-            line = line + mine[6 + n] * motion[d]
+            line = line + fixed[6 + n] * near_motion[d]
         drag.append(line)
-    totals = mine[0:6] - 6.0 * jnp.stack(drag)
-    mass = 4.0 / 3.0 * math.pi * RADIUS**3
-    inertia = 0.4 * mass * RADIUS**2
-    new_motion = jnp.concatenate(
-        [motion[0:3] + totals[0:3] / mass, motion[3:6] + totals[3:6] / inertia], axis=0
-    )
-    report = jnp.concatenate([totals[0:3], totals[3:6] / RADIUS], axis=0)
-
-    column = jnp.stack(
-        [lax.ppermute(new_motion, "gy", fy), new_motion, lax.ppermute(new_motion, "gy", by)], axis=1
-    )
-    around = jnp.stack(
-        [lax.ppermute(column, "gx", fx), column, lax.ppermute(column, "gx", bx)], axis=1
-    ).reshape(6, width)
-    groups = -(-width // 128)
-    around = jnp.pad(around, ((0, 0), (0, groups * 128 - width))).reshape(6, groups, 128)
-    link_out = pl.pallas_call(
-        reflect_kernel,
-        out_shape=jax.ShapeDtypeStruct((lines, 128), F32),
-        in_specs=vmem(4), out_specs=vmem(1)[0], compiler_params=grant(6), name="reflect",
-    )(slots, reach, pops, around)
+    settled = fixed[0:6] - 6.0 * jnp.stack(drag)
+    lanes = -(-width // 128) * 128
+    partial = settled + pressed.transpose(1, 0, 2)[0:6].reshape(6, width)
+    partial = jnp.pad(partial, ((0, 2), (0, lanes - width)))
+    devices = count_x * count_y
+    partials = lax.all_to_all(
+        jnp.broadcast_to(partial, (devices, 8, lanes)), ("gx", "gy"), 0, 0
+    )
+    home = jnp.stack([lax.axis_index("gx"), lax.axis_index("gy")])
+    report, link_out = pl.pallas_call(
+        functools.partial(reflect_kernel, per_tile=per_tile, counts=(count_x, count_y)),
+        out_shape=(
+            jax.ShapeDtypeStruct((6, per_tile), F32), jax.ShapeDtypeStruct((lines, 128), F32),
+        ),
+        in_specs=[smem] + vmem(5), out_specs=tuple(vmem(2)), compiler_params=grant(6),
+        name="reflect",
+    )(home, partials, slots, reach, pops, jnp.pad(near_motion, ((0, 2), (0, lanes - width))))
     return potential, report, link_out.reshape(link_pop.shape)
 
 

time: 119 us -> 119 us (level); the launches traced: 119 us -> 118 us
  starting transfers between devices: 21.7 us -> 11.9 us
  waiting for transfers between devices: 11.3 us -> 15 us
  local copies, waits for them, and re-layouts: 2.49 us -> 4.62 us
  other arithmetic: 22.3 us -> 23.5 us
    ppermute x9 -> x1, starting transfers between devices: 17.7 us -> 3.1 us  [shards(): from_right = lax.ppermute(strip(to_left), 'gy', by)]
    all_to_all x0 -> x1, waiting for transfers between devices: none -> 12.7 us  [shards(): lax.all_to_all(jnp.broadcast_to(partial, (devices, 8, lanes)), ('gx', 'gy...]
    ppermute x9 -> x1, waiting for transfers between devices: 11.3 us -> 1.87 us  [shards(): from_right = lax.ppermute(strip(to_left), 'gy', by)]
    all_to_all x0 -> x1, starting transfers between devices: none -> 4.78 us  [shards(): lax.all_to_all(jnp.broadcast_to(partial, (devices, 8, lanes)), ('gx', 'gy...]
    another operation x5 -> x7, other arithmetic: 0.1 us -> 1.4 us
    squeeze x1 -> x10, local copies, waits for them, and re-layouts: 0.01 us -> 1.26 us  [the longest x1 0.71 us: shards(): low[-1]]
  transfers between devices with their start and end apart: 12 -> 5, of which waited for: 7 -> 3; matrix products, arithmetic and copies ran while one was open for 16% -> 15% of each run, Pallas kernels for 10% -> 10%
where the time goes in v6:
time: 119 us; the launch traced here: 118 us
  Pallas kernels  61.5 us (52%)
  other arithmetic  23.5 us (20%)
  waiting for transfers between devices  15 us (13%)
  starting transfers between devices  11.9 us (10%)
  local copies, waits for them, and re-layouts  4.62 us (4%)
    pallas_call x1, Pallas kernels, shards(): pl.pallas_call(relax_kernel, out_shape=(jax.ShapeDtypeStruct((depth, wide...  30.3 us
    sort x1, other arithmetic, shards(): lax.sort((key.reshape(-1), *(part.reshape(-1) for part in pack_arms(rb)))...  15.9 us
    all_to_all x1, waiting for transfers between devices, shards(): lax.all_to_all(jnp.broadcast_to(partial, (devices, 8, lanes)), ('gx', 'gy...  12.7 us
    pallas_call x1, Pallas kernels, shards(): pl.pallas_call(functools.partial(fixed_kernel, width=width), out_shape=(j...  11.9 us
    pallas_call x1, Pallas kernels, shards(): pl.pallas_call(pack_kernel, out_shape=(jax.ShapeDtypeStruct((6, layers +...  8.36 us
    pallas_call x1, Pallas kernels, shards(): pl.pallas_call(functools.partial(press_kernel, per_tile=per_tile), out_sh...  8.24 us
    all_to_all x1, starting transfers between devices, shards(): lax.all_to_all(jnp.broadcast_to(partial, (devices, 8, lanes)), ('gx', 'gy...  4.78 us
    ppermute x1, starting transfers between devices, shards(): from_right = lax.ppermute(strip(to_left), 'gy', by)  3.1 us
  transfers between devices with their start and end apart: 5, of which 3 were waited for; matrix products, arithmetic and copies ran while one was open for 15% of the time, Pallas kernels for 10%

profile of v6, /device:TPU:1, one launch (start us, length us, event | category | flops | bytes accessed | tf_op | source)
XLA Modules:
  0.0 117.6 jit_solution(7198799854119855702)
XLA Ops:
  0.6 1.3 %fusion.5 = (f16[1,48,12,128]{3,2,1,0:T(8,128)(2,1)S(1)}, f16[1,48,12,128]{3,2,1,0:T(8,128)(2,1)S(1)}) fusion(bf16[48,64,128]{2,1,0:T(8,128)(2,1)} %eps.1), kind=kLoop, calls=%fused_computation.24 | loop fusion | flops 294912 | bytes 589824 | tf_op jit(solution)/shard_map/convert.10
  1.9 1.2 %fusion.3 = (f16[1,48,12,128]{3,2,1,0:T(8,128)(2,1)S(1)}, f16[1,48,12,128]{3,2,1,0:T(8,128)(2,1)S(1)}) fusion(f32[48,64,128]{2,1,0:T(8,128)} %charge.1), kind=kLoop, calls=%fused_computation.22 | loop fusion | flops 294912 | bytes 884736 | tf_op jit(solution)/shard_map/stack | solution.py:624
  3.3 0.4 maximum_bitcast_fusion
  4.0 0.3 copy-done.9
  4.7 2.7 %collective-permute-start = (f16[37,48,128]{2,1,0:T(8,128)(2,1)S(1)}, f16[37,48,128]{2,1,0:T(8,128)(2,1)}, u32[]{:S(2)}, u32[]{:S(2)}) collective-permute-start(f16[37,48,128]{2,1,0:T(8,128)(2,1)S(1)} %get-tuple-element.70), channel_id=1, source_target_pairs={{0,8},{8,16},{16,24},{24,0},{1,9},{9,17},{17,25},{25,1},{2,10},{10... | collective-permute-start | bytes 1363976 | tf_op jit(solution)/shard_map/ppermute | solution.py:632
  7.4 0.6 shift-right-arithmetic_or_fusion
  8.2 0.4 fusion.17
  8.8 15.9 %sort.21 = (s32[32768]{0:T(1024)S(1)}, s32[32768]{0:T(1024)S(1)}, s32[32768]{0:T(1024)S(1)}) sort(s32[32768]{0:T(1024)S(1)} %fusion.17, s32[32768]{0:T(1024)S(1)} %bitcast.90, s32[32768]{0:T(1024)S(1)} %bitcast.89), dimensions={0}, to_apply=%region_0.1 | sort | flops 491520 | bytes 786432 | tf_op jit(solution)/shard_map/sort | solution.py:652
  24.7 0.4 fusion.28.slots
  25.1 0.7 slice_bitcast_fusion.3
  25.8 1.1 slice.240
  27.4 1.6 %convert_multiply_fusion = (f32[1728,128]{1,0:T(8,128)}, f32[1728,128]{1,0:T(8,128)}) fusion(f16[36,48,128]{2,1,0:T(8,128)(2,1)S(1)} %slice.241, f32[1728]{0:T(1024)S(1)} %mul.333, f16[36,48,128]{2,1,0:T(8,128)(2,1)S(1)} %slice.240), kind=kLoop, calls=%fused_computation | loop fusion | flops 884736 | bytes 2661120 | tf_op jit(solution)/shard_map/mul | solution.py:582
  29.0 8.4 %pack.1 = (f32[6,25,96,128]{3,2,1,0:T(8,128)}, f32[3,5,88,128]{3,2,1,0:T(8,128)S(1)}, f32[3,5,88,128]{3,2,1,0:T(8,128)S(1)}) custom-call(f32[48,64,128]{2,1,0:T(8,128)} %pot.1, f32[48,64,128]{2,1,0:T(8,128)} %charge.1, bf16[48,64,128]{2,1,0:T(8,128)(2,1)} %eps.1, f32[1728,128]{1,0:T(8,128)} %get-tuple-element.72.low, f32[1728,128]{1,0:T(8,128)} %get-tuple-element.71.high), custom_call_target="tpu_custom_call" | custom-call | tf_op jit(solution)/shard_map/pack/pallas_call | solution.py:665
  37.8 1.3 %collective-permute-start.2 = (f16[16,88,128]{2,1,0:T(8,128)(2,1)S(1)}, f16[16,88,128]{2,1,0:T(8,128)(2,1)S(1)}, u32[]{:S(2)}, u32[]{:S(2)}) collective-permute-start(f16[16,88,128]{2,1,0:T(8,128)(2,1)S(1)} %get-tuple-element.29), channel_id=1, source_target_pairs={{0,1},{1,2},{2,3},{3,4},{4,5},{5,6},{6,7},{7,0},{8,9},{9,10},{10,1... | collective-permute-start | bytes 1081352 | tf_op jit(solution)/shard_map/ppermute | solution.py:690
  39.1 3.1 %collective-permute-start.3 = (f16[16,88,128]{2,1,0:T(8,128)(2,1)S(1)}, f16[16,88,128]{2,1,0:T(8,128)(2,1)S(1)}, u32[]{:S(2)}, u32[]{:S(2)}) collective-permute-start(f16[16,88,128]{2,1,0:T(8,128)(2,1)S(1)} %get-tuple-element.63), channel_id=1, source_target_pairs={{1,0},{2,1},{3,2},{4,3},{5,4},{6,5},{7,6},{0,7},{9,8},{10,9},{11,1... | collective-permute-start | bytes 1081352 | tf_op jit(solution)/shard_map/ppermute | solution.py:691
  42.2 11.9 %fixed.1 = (f32[32,288]{1,0:T(8,128)S(1)}, f32[6,256,128]{2,1,0:T(8,128)S(1)}) custom-call(s32[256,128]{1,0:T(8,128)S(1)} %fusion.28.slots, s32[256,128]{1,0:T(8,128)S(1)} %bitcast.80, f32[256,128]{1,0:T(8,128)S(1)} %bitcast.81, f32[3,256,128]{2,1,0:T(8,128)S(1)} %bitcast.75, f32[4,8,128]{2,1,0:T(8,128)S(1)} %copy-done.3), custom_call_target="tpu_custom_call" | custom-call | flops 1000000000 | bytes 20000000 | tf_op jit(solution)/shard_map/fixed/pallas_call | solution.py:700
  54.4 0.4 collective-permute-done.2
  54.8 1.9 %collective-permute-done.3 = f16[16,88,128]{2,1,0:T(8,128)(2,1)S(1)} collective-permute-done((f16[16,88,128]{2,1,0:T(8,128)(2,1)S(1)}, f16[16,88,128]{2,1,0:T(8,128)(2,1)S(1)}, u32[]{:S(2)}, u32[]{:S(2)}) %collective-permute-start.3) | collective-permute-done | bytes 360480 | tf_op jit(solution)/shard_map/ppermute | solution.py:691
  57.8 30.3 %relax.1 = (f32[48,64,128]{2,1,0:T(8,128)}, f32[49,64,128]{2,1,0:T(8,128)S(1)}) custom-call(f32[6,25,96,128]{3,2,1,0:T(8,128)} %get-tuple-element.27.kept, f32[3,5,88,128]{3,2,1,0:T(8,128)S(1)} %get-tuple-element.77.from_left, f32[3,5,88,128]{3,2,1,0:T(8,128)S(1)} %get-tuple-element.76.from_right), custom_call_target="tpu_custom_call" | custom-call | tf_op jit(solution)/shard_map/relax/pallas_call | solution.py:712
  88.1 8.2 %press.1 = f32[9,8,32]{2,1,0:T(8,128)S(1)} custom-call(s32[256]{0:T(256)S(1)} %fusion.33.low, s32[4]{0:T(128)S(1)} %and_select_fusion.passes, s32[256,128]{1,0:T(8,128)S(1)} %bitcast.74, s32[256,128]{1,0:T(8,128)S(1)} %bitcast.77, s32[256,128]{1,0:T(8,128)S(1)} %bitcast.78, f32[4,8,128]{2,1,0:T(8,128)S(1)} %copy-done.3, f32[3136,128]{1,0:T(8,128)S(1)} %bitcast.73), custom_call_target="tpu_custom_call" | custom-call | tf_op jit(solution)/shard_map/press/pallas_call | solution.py:734
  96.5 0.8 broadcast_in_dim.20
  97.3 4.8 %all-to-all-start = ((f32[32,8,384]{2,1,0:T(8,128)}), f32[32,8,384]{2,1,0:T(8,128)S(1)}, u32[]{:S(2)}, u32[]{:S(2)}) async-start(f32[32,8,384]{2,1,0:T(8,128)} %broadcast_in_dim.20), calls=%async_computation | async-start | bytes 786432 | tf_op jit(solution)/shard_map/all_to_all | solution.py:757
  102.2 12.7 %all-to-all-done.partial_sums = f32[32,8,384]{2,1,0:T(8,128)S(1)} async-done(((f32[32,8,384]{2,1,0:T(8,128)}), f32[32,8,384]{2,1,0:T(8,128)S(1)}, u32[]{:S(2)}, u32[]{:S(2)}) %all-to-all-start) | async-done | bytes 393248 | tf_op jit(solution)/shard_map/all_to_all | solution.py:757
  115.0 2.6 %reflect.1 = (f32[6,32]{1,0:T(8,128)}, f32[256,128]{1,0:T(8,128)}) custom-call(s32[2]{0:T(128)S(1)} %pad_add_fusion.home, f32[32,8,384]{2,1,0:T(8,128)S(1)} %all-to-all-done.partial_sums, s32[256,128]{1,0:T(8,128)S(1)} %fusion.28.slots, f32[6,256,128]{2,1,0:T(8,128)S(1)} %get-tuple-element.38.reach, f32[256,128]{1,0:T(8,128)S(1)} %bitcast.82, ...), custom_call_target="tpu_custom_call" | custom-call | tf_op jit(solution)/shard_map/reflect/pallas_call | solution.py:761
  (90 shorter events, 3.6 us)
Async XLA Ops:
  0.6 2.5 %copy-start.4 = (f32[48,64,128]{2,1,0:T(8,128)S(1)}, f32[48,64,128]{2,1,0:T(8,128)}, u32[]{:S(2)}) copy-start(f32[48,64,128]{2,1,0:T(8,128)} %pot.1) | copy-start | bytes 4718596
  3.7 0.7 copy-start.9
  3.7 0.7 copy-start.10
  3.9 3.6 %copy-start = (f32[3,1,1,32768]{3,2,1,0:T(1,128)S(1)}, f32[3,1,1,32768]{3,2,1,0:T(1,128)}, u32[]{:S(2)}) copy-start(f32[3,1,1,32768]{3,2,1,0:T(1,128)} %param.28) | copy-start | bytes 1179652
  3.9 4.1 %copy-start.6 = (s32[1,1,32768]{2,1,0:T(1,128)S(1)}, s32[1,1,32768]{2,1,0:T(1,128)}, u32[]{:S(2)}) copy-start(s32[1,1,32768]{2,1,0:T(1,128)} %param.25) | copy-start | bytes 393220
  3.9 4.1 %copy-start.7 = (s32[1,1,32768]{2,1,0:T(1,128)S(1)}, s32[1,1,32768]{2,1,0:T(1,128)}, u32[]{:S(2)}) copy-start(s32[1,1,32768]{2,1,0:T(1,128)} %param.26) | copy-start | bytes 393220
  4.4 3.8 %copy-start.1 = (s32[1,1,32768]{2,1,0:T(1,128)S(1)}, s32[1,1,32768]{2,1,0:T(1,128)}, u32[]{:S(2)}) copy-start(s32[1,1,32768]{2,1,0:T(1,128)} %param.23) | copy-start | bytes 393220
  4.4 3.9 %copy-start.5 = (s32[1,1,32768]{2,1,0:T(1,128)S(1)}, s32[1,1,32768]{2,1,0:T(1,128)}, u32[]{:S(2)}) copy-start(s32[1,1,32768]{2,1,0:T(1,128)} %param.24) | copy-start | bytes 393220
  4.4 4.2 %copy-start.8 = (f32[3]{0:T(128)S(1)}, f32[3]{0:T(128)}, u32[]{:S(2)}) copy-start(f32[3]{0:T(128)} %constant.173) | copy-start | bytes 40
  4.7 20.4 %collective-permute-start.1 = (f16[37,48,128]{2,1,0:T(8,128)(2,1)S(1)}, f16[37,48,128]{2,1,0:T(8,128)(2,1)S(1)}, u32[]{:S(2)}, u32[]{:S(2)}) collective-permute-start(f16[37,48,128]{2,1,0:T(8,128)(2,1)S(1)} %get-tuple-element.69), channel_id=1, source_target_pairs={{8,0},{16,8},{24,16},{0,24},{9,1},{17,9},{25,17},{1,25},{10,2},{18... | collective-permute-start | bytes 1363976 | tf_op jit(solution)/shard_map/ppermute | solution.py:633
  4.7 20.3 %collective-permute-start = (f16[37,48,128]{2,1,0:T(8,128)(2,1)S(1)}, f16[37,48,128]{2,1,0:T(8,128)(2,1)}, u32[]{:S(2)}, u32[]{:S(2)}) collective-permute-start(f16[37,48,128]{2,1,0:T(8,128)(2,1)S(1)} %get-tuple-element.70), channel_id=1, source_target_pairs={{0,8},{8,16},{16,24},{24,0},{1,9},{9,17},{17,25},{25,1},{2,10},{10... | collective-permute-start | bytes 1363976 | tf_op jit(solution)/shard_map/ppermute | solution.py:632
  28.9 8.4 %copy-start.11 = (f32[3]{0:T(128)S(1)}, f32[3]{0:T(128)}, u32[]{:S(2)}) copy-start(f32[3]{0:T(128)} %constant.158.clone) | copy-start | bytes 40
  37.3 4.8 %copy-start.2 = (f32[1,1,32768]{2,1,0:T(1,128)S(1)}, f32[1,1,32768]{2,1,0:T(1,128)}, u32[]{:S(2)}) copy-start(f32[1,1,32768]{2,1,0:T(1,128)} %param.27) | copy-start | bytes 393220
  37.3 4.8 %copy-start.3 = (f32[4,8,128]{2,1,0:T(8,128)S(1)}, f32[4,8,128]{2,1,0:T(8,128)}, u32[]{:S(2)}) copy-start(f32[4,8,128]{2,1,0:T(8,128)} %constant.157.clone.table) | copy-start | bytes 49156
  37.8 17.0 %collective-permute-start.2 = (f16[16,88,128]{2,1,0:T(8,128)(2,1)S(1)}, f16[16,88,128]{2,1,0:T(8,128)(2,1)S(1)}, u32[]{:S(2)}, u32[]{:S(2)}) collective-permute-start(f16[16,88,128]{2,1,0:T(8,128)(2,1)S(1)} %get-tuple-element.29), channel_id=1, source_target_pairs={{0,1},{1,2},{2,3},{3,4},{4,5},{5,6},{6,7},{7,0},{8,9},{9,10},{10,1... | collective-permute-start | bytes 1081352 | tf_op jit(solution)/shard_map/ppermute | solution.py:690
  39.1 17.6 %collective-permute-start.3 = (f16[16,88,128]{2,1,0:T(8,128)(2,1)S(1)}, f16[16,88,128]{2,1,0:T(8,128)(2,1)S(1)}, u32[]{:S(2)}, u32[]{:S(2)}) collective-permute-start(f16[16,88,128]{2,1,0:T(8,128)(2,1)S(1)} %get-tuple-element.63), channel_id=1, source_target_pairs={{1,0},{2,1},{3,2},{4,3},{5,4},{6,5},{7,6},{0,7},{9,8},{10,9},{11,1... | collective-permute-start | bytes 1081352 | tf_op jit(solution)/shard_map/ppermute | solution.py:691
  97.3 17.7 %all-to-all-start = ((f32[32,8,384]{2,1,0:T(8,128)}), f32[32,8,384]{2,1,0:T(8,128)S(1)}, u32[]{:S(2)}, u32[]{:S(2)}) async-start(f32[32,8,384]{2,1,0:T(8,128)} %broadcast_in_dim.20), calls=%async_computation | async-start | bytes 786432 | tf_op jit(solution)/shard_map/all_to_all | solution.py:757

commit v7 on v6

--- a/solution.py
+++ b/solution.py
@@ -192,8 +192,8 @@
 
     for f, target in enumerate((pb, cb, eb)):
         for i in range(GROUPS):
-            west = from_left[f, i]
-            east = from_right[f, i]
+            west = from_left[GROUPS * f + i]
+            east = from_right[GROUPS * f + i]
             red = jnp.where(wide_first, east, roll(west, HALO))
             black = jnp.where(wide_first, roll(east, -HALO), west)
             fill = 1.0 if f == 2 else 0.0
@@ -427,13 +427,6 @@
     )
 
 
-def write_sums(acc, out):
-    total = out.shape[1]
-    for t in range(9):
-        base = 2 * total * t
-        out[t] = acc[base:base + total, :] + acc[base + total:base + 2 * total, :]
-
-
 def fixed_kernel(slots, dirs, pops, rb, table, out, reach, stage, acc, *, width):
     acc[...] = jnp.zeros_like(acc)
     total = stage.shape[0] // 8
@@ -462,7 +455,9 @@
 AHEAD = 4
 
 
-def press_kernel(low, passes, keys, arm0, arm1, table, press, out, stage, acc, *, per_tile):
+def press_kernel(
+    low, passes, keys, arm0, arm1, table, press, settled, out, stage, acc, sums, *, per_tile
+):
     acc[...] = jnp.zeros_like(acc)
     for n in range(6, stage.shape[0] // 8):
         store_term(stage, n, jnp.zeros((8, 128), F32))
@@ -511,7 +506,26 @@
         return carry
 
     lax.fori_loop(0, keys.shape[0] // (8 * BATCH), batch, 0)
-    write_sums(acc, out)
+
+    sums[...] = jnp.zeros_like(sums)
+    for t in range(9):
+        value = acc[16 * t:16 * t + 8, :] + acc[16 * t + 8:16 * t + 16, :]
+        sums[:, per_tile * t:per_tile * (t + 1)] = value
+    sums[...] += settled[...]
+    head, last = sums[:, 0:128], sums[:, 256:384]
+    lane = lanes_of((8, 128))
+    for n in range(6):
+        part = jnp.broadcast_to(last[n:n + 1, :], (8, 128))
+        here = (line == 6 + n // 4) & (lane // per_tile == n % 4)
+        head = jnp.where(here, roll(part, per_tile * (n % 4)), head)
+    tail = sums[:, 128:256]
+
+    def replicate(p, carry):
+        out[p, 0:8, :] = head
+        out[p, 8:16, :] = tail
+        return carry
+
+    lax.fori_loop(0, out.shape[0], replicate, 0)
 
 
 TOGETHER = 4
@@ -519,20 +533,32 @@
 
 
 def reflect_kernel(
-    home, partial_sums, slots, reach, pops, motion, report, out, *, per_tile, counts
+    home, partial_sums, slots, reach, pops, motion, report, out, spread, *, per_tile, counts
 ):
     lanes = motion.shape[1]
     slot_of_lane = lax.broadcasted_iota(jnp.int32, (8, lanes), 1) // per_tile
     tile_x = slot_of_lane // 3 - 1
     tile_y = slot_of_lane % 3 - 1
     totals = jnp.zeros((8, lanes), F32)
-    for ox, oy in AROUND:
+    lane_of = lanes_of((8, 128))
+    line = lax.broadcasted_iota(jnp.int32, (8, 128), 0)
+    place = lane_of % per_tile + per_tile * (line % 4)
+
+    def unpack(n, carry):
+        peer_x = lax.rem(home[0] + n // 5 - 2 + 2 * counts[0], counts[0])
+        peer_y = lax.rem(home[1] + n % 5 - 2 + 2 * counts[1], counts[1])
+        block = partial_sums[peer_x * counts[1] + peer_y]
+        parts = [lane_pick(jnp.broadcast_to(block[r:r + 1, :], (8, 128)), place) for r in (6, 7)]
+        spread[n, :, 0:128] = block[0:8, :]
+        spread[n, :, 128:256] = block[8:16, :]
+        spread[n, :, 256:384] = jnp.where(line < 4, parts[0], parts[1])
+        return carry
+
+    lax.fori_loop(0, len(AROUND), unpack, 0)
+    for n, (ox, oy) in enumerate(AROUND):
         near = (abs(tile_x - ox) <= 1) & (abs(tile_y - oy) <= 1) & (slot_of_lane < 9)
         shift = per_tile * (3 * ox + oy)
-        peer_x = lax.rem(home[0] + ox + 2 * counts[0], counts[0])
-        peer_y = lax.rem(home[1] + oy + 2 * counts[1], counts[1])
-        peer = peer_x * counts[1] + peer_y
-        moved = pltpu.roll(partial_sums[peer], shift % lanes, 1)
+        moved = pltpu.roll(spread[n], shift % lanes, 1)
         totals = totals + jnp.where(near, moved, 0.0)
     mass = 4.0 / 3.0 * math.pi * RADIUS**3
     inertia = 0.4 * mass * RADIUS**2
@@ -578,8 +604,10 @@
     return (strips * scales()).astype(HALF)
 
 
-def from_half(strips):
-    return strips.astype(F32) * (1.0 / scales())
+def from_half(planes):
+    each = (planes.shape[0] - 1) // 3
+    back = [1.0 / POT_SCALE] * each + [1.0 / CHARGE_SCALE] * each + [1.0] * (each + 1)
+    return planes.astype(F32) * jnp.array(back, F32)[:, None, None]
 
 
 MOTION_SCALE = 2.0**10
@@ -662,6 +690,7 @@
     span = jnp.max((row_high - row_low + 1).reshape(-1, 8 * BATCH), axis=1)
     passes = (jnp.maximum(span, 0) + AHEAD - 1) // AHEAD
 
+    low, high = from_half(low), from_half(high)
     split, to_right, to_left = pl.pallas_call(
         pack_kernel,
         out_shape=(
@@ -677,7 +706,7 @@
             pltpu.SemaphoreType.DMA,
         ],
     )(potential_start, charge, eps_field,
-      *(from_half(part[:-1].reshape(3, HALO, depth, 128)).reshape(-1, 128) for part in (low, high)))
+      low.reshape(-1, 128), high.reshape(-1, 128))
     row = jnp.stack([
         motion_of(low[-1], motion.shape), motion, motion_of(high[-1], motion.shape)
     ])
@@ -689,8 +718,7 @@
     to_right, dirs_late = lax.optimization_barrier((strip(to_right), dirs))
     from_left = lax.ppermute(to_right, "gy", fy)
     from_right = lax.ppermute(strip(to_left), "gy", by)
-    shape = (3, GROUPS, wide + 2 * HALO, 128)
-    west, east = [from_half(part[:-1].reshape(shape)) for part in (from_left, from_right)]
+    from_left, from_right = from_half(from_left), from_half(from_right)
     near_motion = jnp.stack(
         [motion_of(from_left[-1], row.shape), row, motion_of(from_right[-1], row.shape)], axis=1
     )
@@ -728,35 +756,36 @@
             pltpu.SemaphoreType.DMA((6,)),
         ],
         compiler_params=grant(48), name="relax",
-    )(split, west, east)
-
+    )(split, from_left, from_right)
+
+    drag = []
+    for a in range(6):
+        drag.append(sum(
+            fixed[6 + PAIRS.index((min(a, d), max(a, d)))] * near_motion[d] for d in range(6)
+        ))
+    settled = fixed[0:6] - 6.0 * jnp.stack(drag)
+    lanes = -(-width // 128) * 128
+    settled, near_motion = [
+        jnp.pad(part, ((0, 2), (0, lanes - width))) for part in (settled, near_motion)
+    ]
+    devices = count_x * count_y
     smem = pl.BlockSpec(memory_space=pltpu.SMEM)
     pressed = pl.pallas_call(
         functools.partial(press_kernel, per_tile=per_tile),
-        out_shape=jax.ShapeDtypeStruct((9, 8, per_tile), F32),
-        in_specs=[smem, smem] + vmem(5), out_specs=vmem(1)[0],
-        scratch_shapes=[pltpu.VMEM((64, 128), F32), pltpu.VMEM((9 * 16, per_tile), F32)],
+        out_shape=jax.ShapeDtypeStruct((devices, 16, 128), F32),
+        in_specs=[smem, smem] + vmem(6), out_specs=vmem(1)[0],
+        scratch_shapes=[
+            pltpu.VMEM((64, 128), F32), pltpu.VMEM((9 * 16, per_tile), F32),
+            pltpu.VMEM((8, lanes), F32),
+        ],
         compiler_params=grant(8), name="press",
     )(
         row_low, passes, keys, arm0.reshape(lines, 128), arm1.reshape(lines, 128),
-        table, press.reshape(-1, 128),
+        table, press.reshape(-1, 128), settled,
     )
 
-    drag = []
-    for a in range(6):
-        line = jnp.zeros((width,), F32)
-        for d in range(6):
-            n = PAIRS.index((min(a, d), max(a, d)))
-            line = line + fixed[6 + n] * near_motion[d]
-        drag.append(line)
-    settled = fixed[0:6] - 6.0 * jnp.stack(drag)
-    lanes = -(-width // 128) * 128
-    partial = settled + pressed.transpose(1, 0, 2)[0:6].reshape(6, width)
-    partial = jnp.pad(partial, ((0, 2), (0, lanes - width)))
-    devices = count_x * count_y
-    partials = lax.all_to_all(
-        jnp.broadcast_to(partial, (devices, 8, lanes)), ("gx", "gy"), 0, 0
-    )
+    partials = lax.all_to_all(pressed, ("gx", "gy"), 0, 0)
+
     home = jnp.stack([lax.axis_index("gx"), lax.axis_index("gy")])
     report, link_out = pl.pallas_call(
         functools.partial(reflect_kernel, per_tile=per_tile, counts=(count_x, count_y)),
@@ -764,8 +793,8 @@
             jax.ShapeDtypeStruct((6, per_tile), F32), jax.ShapeDtypeStruct((lines, 128), F32),
         ),
         in_specs=[smem] + vmem(5), out_specs=tuple(vmem(2)), compiler_params=grant(6),
-        name="reflect",
-    )(home, partials, slots, reach, pops, jnp.pad(near_motion, ((0, 2), (0, lanes - width))))
+        scratch_shapes=[pltpu.VMEM((len(AROUND), 8, lanes), F32)], name="reflect",
+    )(home, partials, slots, reach, pops, near_motion)
     return potential, report, link_out.reshape(link_pop.shape)
 
 

time: 119 us -> 121 us (1.017)
  waiting for transfers between devices: 15 us -> 10.2 us
  Pallas kernels: 61.5 us -> 64.7 us
  other arithmetic: 23.5 us -> 25.5 us
  local copies, waits for them, and re-layouts: 4.62 us -> 6.19 us
    unnamed x24 -> x38, local copies, waits for them, and re-layouts: 0.39 us -> 4.26 us
    all_to_all x1, waiting for transfers between devices: 12.7 us -> 9.93 us  [shards(): partials = lax.all_to_all(pressed, ('gx', 'gy'), 0, 0)]
    pallas_call x1, Pallas kernels: 2.63 us -> 4.5 us  [shards(): pl.pallas_call(functools.partial(reflect_kernel, per_tile=per_tile, count...]
    ppermute x1, waiting for transfers between devices: 1.87 us -> 0.01 us  [shards(): from_right = lax.ppermute(strip(to_left), 'gy', by)]
    add x4 -> x3, other arithmetic: 0.09 us -> 1.81 us  [shards(): sum((fixed[6 + PAIRS.index((min(a, d), max(a, d)))] * near_motion[d] for...]
    slice x12 -> x7, local copies, waits for them, and re-layouts: 1.38 us -> 0.04 us  [shards(): near_motion[d]]
    pallas_call x1, Pallas kernels: 8.24 us -> 9.53 us  [shards(): pl.pallas_call(functools.partial(press_kernel, per_tile=per_tile), out_sh...]
    ppermute x1, starting transfers between devices: 1.26 us -> 0.01 us  [shards(): from_left = lax.ppermute(to_right, 'gy', fy)]
  transfers between devices with their start and end apart: 5 -> 5, of which waited for: 3 -> 2; matrix products, arithmetic and copies ran while one was open for 15% -> 16% of each run, Pallas kernels for 10% -> 10%
where the time goes in v7:
time: 121 us; the launch traced here: 120 us
  Pallas kernels  64.7 us (53%)
  other arithmetic  25.5 us (21%)
  starting transfers between devices  12.3 us (10%)
  waiting for transfers between devices  10.2 us (8%)
  local copies, waits for them, and re-layouts  6.19 us (5%)
    pallas_call x1, Pallas kernels, shards(): pl.pallas_call(relax_kernel, out_shape=(jax.ShapeDtypeStruct((depth, wide...  30.3 us
    sort x1, other arithmetic, shards(): lax.sort((key.reshape(-1), *(part.reshape(-1) for part in pack_arms(rb)))...  16.6 us
    pallas_call x1, Pallas kernels, shards(): pl.pallas_call(functools.partial(fixed_kernel, width=width), out_shape=(j...  11.9 us
    all_to_all x1, waiting for transfers between devices, shards(): partials = lax.all_to_all(pressed, ('gx', 'gy'), 0, 0)  9.93 us
    pallas_call x1, Pallas kernels, shards(): pl.pallas_call(functools.partial(press_kernel, per_tile=per_tile), out_sh...  9.53 us
    pallas_call x1, Pallas kernels, shards(): pl.pallas_call(pack_kernel, out_shape=(jax.ShapeDtypeStruct((6, layers +...  8.37 us
    all_to_all x1, starting transfers between devices, shards(): partials = lax.all_to_all(pressed, ('gx', 'gy'), 0, 0)  5.3 us
    pallas_call x1, Pallas kernels, shards(): pl.pallas_call(functools.partial(reflect_kernel, per_tile=per_tile, count...  4.5 us
  transfers between devices with their start and end apart: 5, of which 2 were waited for; matrix products, arithmetic and copies ran while one was open for 16% of the time, Pallas kernels for 10%

profile of v7, /device:TPU:1, one launch (start us, length us, event | category | flops | bytes accessed | tf_op | source)
XLA Modules:
  0.0 120.0 jit_solution(12557538910001264956)
XLA Ops:
  0.6 1.3 %fusion.5 = (f16[1,48,12,128]{3,2,1,0:T(8,128)(2,1)S(1)}, f16[1,48,12,128]{3,2,1,0:T(8,128)(2,1)S(1)}) fusion(bf16[48,64,128]{2,1,0:T(8,128)(2,1)} %eps.1), kind=kLoop, calls=%fused_computation.24 | loop fusion | flops 294912 | bytes 589824 | tf_op jit(solution)/shard_map/convert.6
  1.9 1.2 %fusion.3 = (f16[1,48,12,128]{3,2,1,0:T(8,128)(2,1)S(1)}, f16[1,48,12,128]{3,2,1,0:T(8,128)(2,1)S(1)}) fusion(f32[48,64,128]{2,1,0:T(8,128)} %charge.1), kind=kLoop, calls=%fused_computation.22 | loop fusion | flops 294912 | bytes 884736 | tf_op jit(solution)/shard_map/stack | solution.py:652
  3.3 0.4 maximum_bitcast_fusion
  4.7 2.7 %collective-permute-start = (f16[37,48,128]{2,1,0:T(8,128)(2,1)S(1)}, f16[37,48,128]{2,1,0:T(8,128)(2,1)S(1)}, u32[]{:S(2)}, u32[]{:S(2)}) collective-permute-start(f16[37,48,128]{2,1,0:T(8,128)(2,1)S(1)} %get-tuple-element.70), channel_id=1, source_target_pairs={{0,8},{8,16},{16,24},{24,0},{1,9},{9,17},{17,25},{25,1},{2,10},{10... | collective-permute-start | bytes 1363976 | tf_op jit(solution)/shard_map/ppermute | solution.py:660
  7.4 0.6 shift-right-arithmetic_or_fusion
  8.2 0.4 fusion.17
  8.6 16.6 %sort.21 = (s32[32768]{0:T(1024)S(1)}, s32[32768]{0:T(1024)}, s32[32768]{0:T(1024)}) sort(s32[32768]{0:T(1024)S(1)} %fusion.17, s32[32768]{0:T(1024)S(1)} %bitcast.79, s32[32768]{0:T(1024)S(1)} %bitcast.78), dimensions={0}, to_apply=%region_0.1 | sort | flops 491520 | bytes 786432 | tf_op jit(solution)/shard_map/sort | solution.py:680
  25.5 1.2 %convert_multiply_fusion = (f32[37,48,128]{2,1,0:T(8,128)S(1)}, f32[37,48,128]{2,1,0:T(8,128)S(1)}) fusion(f16[37,48,128]{2,1,0:T(8,128)(2,1)} %collective-permute-done.1, f32[37]{0:T(128)S(1)} %copy-done.18, f16[37,48,128]{2,1,0:T(8,128)(2,1)S(1)} %collective-permute-done), kind=kLoop, calls=%fused_computation | loop fusion | flops 909312 | bytes 2728084 | tf_op jit(solution)/shard_map/mul | solution.py:610
  26.9 0.9 copy-done.8
  28.0 8.4 %pack.1 = (f32[6,25,96,128]{3,2,1,0:T(8,128)}, f32[3,5,88,128]{3,2,1,0:T(8,128)S(1)}, f32[3,5,88,128]{3,2,1,0:T(8,128)S(1)}) custom-call(f32[48,64,128]{2,1,0:T(8,128)} %pot.1, f32[48,64,128]{2,1,0:T(8,128)} %charge.1, bf16[48,64,128]{2,1,0:T(8,128)(2,1)} %eps.1, f32[1776,128]{1,0:T(8,128)} %bitcast.73, f32[1776,128]{1,0:T(8,128)} %bitcast.72), custom_call_target="tpu_custom_call" | custom-call | tf_op jit(solution)/shard_map/pack/pallas_call | solution.py:694
  36.9 4.3 %collective-permute-start.3 = (f16[16,88,128]{2,1,0:T(8,128)(2,1)S(1)}, f16[16,88,128]{2,1,0:T(8,128)(2,1)S(1)}, u32[]{:S(2)}, u32[]{:S(2)}) collective-permute-start(f16[16,88,128]{2,1,0:T(8,128)(2,1)S(1)} %get-tuple-element.63), channel_id=1, source_target_pairs={{1,0},{2,1},{3,2},{4,3},{5,4},{6,5},{7,6},{0,7},{9,8},{10,9},{11,1... | collective-permute-start | bytes 1081352 | tf_op jit(solution)/shard_map/ppermute | solution.py:720
  41.4 11.9 %fixed.1 = (f32[32,288]{1,0:T(8,128)S(1)}, f32[6,256,128]{2,1,0:T(8,128)S(1)}) custom-call(s32[256,128]{1,0:T(8,128)S(1)} %fusion.28.slots, s32[256,128]{1,0:T(8,128)S(1)} %bitcast.71, f32[256,128]{1,0:T(8,128)S(1)} %bitcast.66, f32[3,256,128]{2,1,0:T(8,128)S(1)} %bitcast.65, f32[4,8,128]{2,1,0:T(8,128)S(1)} %copy-done.7), custom_call_target="tpu_custom_call" | custom-call | flops 1000000000 | bytes 20000000 | tf_op jit(solution)/shard_map/fixed/pallas_call | solution.py:728
  53.4 0.9 copy-done
  55.8 0.6 multiply_add_fusion.4
  56.3 0.6 multiply_add_fusion.2
  56.9 0.6 multiply_add_fusion
  57.6 30.3 %relax.1 = (f32[48,64,128]{2,1,0:T(8,128)}, f32[49,64,128]{2,1,0:T(8,128)S(1)}) custom-call(f32[6,25,96,128]{3,2,1,0:T(8,128)} %get-tuple-element.27.kept, f32[16,88,128]{2,1,0:T(8,128)S(1)} %get-tuple-element.75.from_left, f32[16,88,128]{2,1,0:T(8,128)S(1)} %get-tuple-element.74.from_right), custom_call_target="tpu_custom_call" | custom-call | tf_op jit(solution)/shard_map/relax/pallas_call | solution.py:740
  87.9 0.8 stack.91
  88.8 0.9 copy-done.4
  89.7 0.9 copy-done.5
  90.6 9.5 %press.1 = f32[32,16,128]{2,1,0:T(8,128)} custom-call(s32[256]{0:T(256)S(1)} %fusion.33.low, s32[4]{0:T(128)S(1)} %and_select_fusion.passes, s32[256,128]{1,0:T(8,128)S(1)} %bitcast.64, s32[256,128]{1,0:T(8,128)S(1)} %bitcast.68, s32[256,128]{1,0:T(8,128)S(1)} %bitcast.69, f32[4,8,128]{2,1,0:T(8,128)S(1)} %copy-done.7, f32[3136,128]{1,0:T(8,128)S(1)} %bitcast.63, ...), custom_call_target="tpu_custom_call" | custom-call | tf_op jit(solution)/shard_map/press/pallas_call | solution.py:773
  100.1 5.3 %all-to-all-start = ((f32[32,16,128]{2,1,0:T(8,128)}), f32[32,16,128]{2,1,0:T(8,128)S(1)}, u32[]{:S(2)}, u32[]{:S(2)}) async-start(f32[32,16,128]{2,1,0:T(8,128)} %press.1), calls=%async_computation | async-start | bytes 524288 | tf_op jit(solution)/shard_map/all_to_all | solution.py:787
  105.6 9.9 %all-to-all-done.partial_sums = f32[32,16,128]{2,1,0:T(8,128)S(1)} async-done(((f32[32,16,128]{2,1,0:T(8,128)}), f32[32,16,128]{2,1,0:T(8,128)S(1)}, u32[]{:S(2)}, u32[]{:S(2)}) %all-to-all-start) | async-done | bytes 262176 | tf_op jit(solution)/shard_map/all_to_all | solution.py:787
  115.5 4.5 %reflect.1 = (f32[6,32]{1,0:T(8,128)}, f32[256,128]{1,0:T(8,128)}) custom-call(s32[2]{0:T(128)S(1)} %pad_add_fusion.home, f32[32,16,128]{2,1,0:T(8,128)S(1)} %all-to-all-done.partial_sums, s32[256,128]{1,0:T(8,128)S(1)} %fusion.28.slots, f32[6,256,128]{2,1,0:T(8,128)S(1)} %copy-done.1, f32[256,128]{1,0:T(8,128)S(1)} %bitcast.67, f32[8,384]{1,0:T(8,128)S(1)} %pad.19.motion), custom_call_target="tpu_custom_call" | custom-call | tf_op jit(solution)/shard_map/reflect/pallas_call | solution.py:790
  (91 shorter events, 4.1 us)
Async XLA Ops:
  0.6 2.5 %copy-start.10 = (f32[48,64,128]{2,1,0:T(8,128)S(1)}, f32[48,64,128]{2,1,0:T(8,128)}, u32[]{:S(2)}) copy-start(f32[48,64,128]{2,1,0:T(8,128)} %pot.1) | copy-start | bytes 4718596
  3.7 0.7 copy-start.14
  3.7 0.7 copy-start.15
  3.9 3.5 %copy-start.2 = (f32[3,1,1,32768]{3,2,1,0:T(1,128)S(1)}, f32[3,1,1,32768]{3,2,1,0:T(1,128)}, u32[]{:S(2)}) copy-start(f32[3,1,1,32768]{3,2,1,0:T(1,128)} %param.28) | copy-start | bytes 1179652
  3.9 4.0 %copy-start.12 = (s32[1,1,32768]{2,1,0:T(1,128)S(1)}, s32[1,1,32768]{2,1,0:T(1,128)}, u32[]{:S(2)}) copy-start(s32[1,1,32768]{2,1,0:T(1,128)} %param.25) | copy-start | bytes 393220
  3.9 4.0 %copy-start.13 = (s32[1,1,32768]{2,1,0:T(1,128)S(1)}, s32[1,1,32768]{2,1,0:T(1,128)}, u32[]{:S(2)}) copy-start(s32[1,1,32768]{2,1,0:T(1,128)} %param.26) | copy-start | bytes 393220
  4.4 3.8 %copy-start.6 = (s32[1,1,32768]{2,1,0:T(1,128)S(1)}, s32[1,1,32768]{2,1,0:T(1,128)}, u32[]{:S(2)}) copy-start(s32[1,1,32768]{2,1,0:T(1,128)} %param.23) | copy-start | bytes 393220
  4.4 3.8 %copy-start.11 = (s32[1,1,32768]{2,1,0:T(1,128)S(1)}, s32[1,1,32768]{2,1,0:T(1,128)}, u32[]{:S(2)}) copy-start(s32[1,1,32768]{2,1,0:T(1,128)} %param.24) | copy-start | bytes 393220
  4.7 20.9 %copy-start.18 = (f32[37]{0:T(128)S(1)}, f32[37]{0:T(128)}, u32[]{:S(2)}) copy-start(f32[37]{0:T(128)} %constant.160.clone) | copy-start | bytes 448
  4.7 20.8 %collective-permute-start = (f16[37,48,128]{2,1,0:T(8,128)(2,1)S(1)}, f16[37,48,128]{2,1,0:T(8,128)(2,1)S(1)}, u32[]{:S(2)}, u32[]{:S(2)}) collective-permute-start(f16[37,48,128]{2,1,0:T(8,128)(2,1)S(1)} %get-tuple-element.70), channel_id=1, source_target_pairs={{0,8},{8,16},{16,24},{24,0},{1,9},{9,17},{17,25},{25,1},{2,10},{10... | collective-permute-start | bytes 1363976 | tf_op jit(solution)/shard_map/ppermute | solution.py:660
  7.3 18.2 %collective-permute-start.1 = (f16[37,48,128]{2,1,0:T(8,128)(2,1)S(1)}, f16[37,48,128]{2,1,0:T(8,128)(2,1)}, u32[]{:S(2)}, u32[]{:S(2)}) collective-permute-start(f16[37,48,128]{2,1,0:T(8,128)(2,1)S(1)} %get-tuple-element.69), channel_id=1, source_target_pairs={{8,0},{16,8},{24,16},{0,24},{9,1},{17,9},{25,17},{1,25},{10,2},{18... | collective-permute-start | bytes 1363976 | tf_op jit(solution)/shard_map/ppermute | solution.py:661
  26.8 1.0 copy-start.8
  26.8 1.2 %copy-start.9 = (f32[37,48,128]{2,1,0:T(8,128)}, f32[37,48,128]{2,1,0:T(8,128)S(1)}, u32[]{:S(2)}) copy-start(f32[37,48,128]{2,1,0:T(8,128)S(1)} %get-tuple-element.79) | copy-start | bytes 2727940
  28.0 8.4 %copy-start.17 = (f32[3]{0:T(128)S(1)}, f32[3]{0:T(128)}, u32[]{:S(2)}) copy-start(f32[3]{0:T(128)} %constant.161.clone) | copy-start | bytes 40
  36.4 5.0 %copy-start.3 = (f32[1,1,32768]{2,1,0:T(1,128)S(1)}, f32[1,1,32768]{2,1,0:T(1,128)}, u32[]{:S(2)}) copy-start(f32[1,1,32768]{2,1,0:T(1,128)} %param.27) | copy-start | bytes 393220
  36.4 5.0 %copy-start.7 = (f32[4,8,128]{2,1,0:T(8,128)S(1)}, f32[4,8,128]{2,1,0:T(8,128)}, u32[]{:S(2)}) copy-start(f32[4,8,128]{2,1,0:T(8,128)} %constant.159.clone.table) | copy-start | bytes 49156
  36.9 17.8 %collective-permute-start.3 = (f16[16,88,128]{2,1,0:T(8,128)(2,1)S(1)}, f16[16,88,128]{2,1,0:T(8,128)(2,1)S(1)}, u32[]{:S(2)}, u32[]{:S(2)}) collective-permute-start(f16[16,88,128]{2,1,0:T(8,128)(2,1)S(1)} %get-tuple-element.63), channel_id=1, source_target_pairs={{1,0},{2,1},{3,2},{4,3},{5,4},{6,5},{7,6},{0,7},{9,8},{10,9},{11,1... | collective-permute-start | bytes 1081352 | tf_op jit(solution)/shard_map/ppermute | solution.py:720
  41.2 13.7 %collective-permute-start.2 = (f16[16,88,128]{2,1,0:T(8,128)(2,1)S(1)}, f16[16,88,128]{2,1,0:T(8,128)(2,1)S(1)}, u32[]{:S(2)}, u32[]{:S(2)}) collective-permute-start(f16[16,88,128]{2,1,0:T(8,128)(2,1)S(1)} %get-tuple-element.29), channel_id=1, source_target_pairs={{0,1},{1,2},{2,3},{3,4},{4,5},{5,6},{6,7},{7,0},{8,9},{9,10},{10,1... | collective-permute-start | bytes 1081352 | tf_op jit(solution)/shard_map/ppermute | solution.py:719
  41.4 13.5 %copy-start.16 = (f32[16]{0:T(128)S(1)}, f32[16]{0:T(128)}, u32[]{:S(2)}) copy-start(f32[16]{0:T(128)} %constant.162.clone) | copy-start | bytes 196
  53.4 0.9 copy-start
  87.9 27.6 %copy-start.1 = (f32[6,256,128]{2,1,0:T(8,128)S(1)}, f32[6,256,128]{2,1,0:T(8,128)}, u32[]{:S(2)}) copy-start(f32[6,256,128]{2,1,0:T(8,128)} %copy-done) | copy-start | bytes 2359300
  88.7 0.9 copy-start.4
  89.7 0.9 copy-start.5
  100.1 15.4 %all-to-all-start = ((f32[32,16,128]{2,1,0:T(8,128)}), f32[32,16,128]{2,1,0:T(8,128)S(1)}, u32[]{:S(2)}, u32[]{:S(2)}) async-start(f32[32,16,128]{2,1,0:T(8,128)} %press.1), calls=%async_computation | async-start | bytes 524288 | tf_op jit(solution)/shard_map/all_to_all | solution.py:787

commit v8 on v7

--- a/solution.py
+++ b/solution.py
@@ -456,7 +456,8 @@
 
 
 def press_kernel(
-    low, passes, keys, arm0, arm1, table, press, settled, out, stage, acc, sums, *, per_tile
+    low, passes, keys, arm0, arm1, table, press, fixed, motion, out, stage, acc, sums,
+    *, per_tile
 ):
     acc[...] = jnp.zeros_like(acc)
     for n in range(6, stage.shape[0] // 8):
@@ -511,7 +512,12 @@
     for t in range(9):
         value = acc[16 * t:16 * t + 8, :] + acc[16 * t + 8:16 * t + 16, :]
         sums[:, per_tile * t:per_tile * (t + 1)] = value
-    sums[...] += settled[...]
+    for a in range(6):
+        drag = jnp.zeros_like(motion[0:1, :])
+        for d in range(6):
+            n = 6 + PAIRS.index((min(a, d), max(a, d)))
+            drag += fixed[n:n + 1, :] * motion[d:d + 1, :]
+        sums[a:a + 1, :] += fixed[a:a + 1, :] - 6.0 * drag
     head, last = sums[:, 0:128], sums[:, 256:384]
     lane = lanes_of((8, 128))
     for n in range(6):
@@ -533,7 +539,7 @@
 
 
 def reflect_kernel(
-    home, partial_sums, slots, reach, pops, motion, report, out, spread, *, per_tile, counts
+    control, partial_sums, slots, reach, pops, motion, report, out, spread, *, per_tile, counts
 ):
     lanes = motion.shape[1]
     slot_of_lane = lax.broadcasted_iota(jnp.int32, (8, lanes), 1) // per_tile
@@ -544,17 +550,22 @@
     line = lax.broadcasted_iota(jnp.int32, (8, 128), 0)
     place = lane_of % per_tile + per_tile * (line % 4)
 
+    at = control.shape[0] - 2
+
     def unpack(n, carry):
-        peer_x = lax.rem(home[0] + n // 5 - 2 + 2 * counts[0], counts[0])
-        peer_y = lax.rem(home[1] + n % 5 - 2 + 2 * counts[1], counts[1])
-        block = partial_sums[peer_x * counts[1] + peer_y]
-        parts = [lane_pick(jnp.broadcast_to(block[r:r + 1, :], (8, 128)), place) for r in (6, 7)]
-        spread[n, :, 0:128] = block[0:8, :]
-        spread[n, :, 128:256] = block[8:16, :]
-        spread[n, :, 256:384] = jnp.where(line < 4, parts[0], parts[1])
-        return carry
-
-    lax.fori_loop(0, len(AROUND), unpack, 0)
+        peer_x = lax.rem(control[at] + n - 2 + 2 * counts[0], counts[0])
+        for m in range(5):
+            peer_y = lax.rem(control[at + 1] + m - 2 + 2 * counts[1], counts[1])
+            block = partial_sums[peer_x * counts[1] + peer_y]
+            parts = [
+                lane_pick(jnp.broadcast_to(block[r:r + 1, :], (8, 128)), place) for r in (6, 7)
+            ]
+            spread[5 * n + m, :, 0:128] = block[0:8, :]
+            spread[5 * n + m, :, 128:256] = block[8:16, :]
+            spread[5 * n + m, :, 256:384] = jnp.where(line < 4, parts[0], parts[1])
+        return carry
+
+    lax.fori_loop(0, 5, unpack, 0)
     for n, (ox, oy) in enumerate(AROUND):
         near = (abs(tile_x - ox) <= 1) & (abs(tile_y - oy) <= 1) & (slot_of_lane < 9)
         shift = per_tile * (3 * ox + oy)
@@ -689,6 +700,8 @@
     row_high = jnp.max(jnp.where(table_rows < depth * wide, table_rows, 0), axis=1)
     span = jnp.max((row_high - row_low + 1).reshape(-1, 8 * BATCH), axis=1)
     passes = (jnp.maximum(span, 0) + AHEAD - 1) // AHEAD
+    home = jnp.stack([lax.axis_index("gx"), lax.axis_index("gy")])
+    control = jnp.concatenate([passes, home])
 
     low, high = from_half(low), from_half(high)
     split, to_right, to_left = pl.pallas_call(
@@ -758,35 +771,28 @@
         compiler_params=grant(48), name="relax",
     )(split, from_left, from_right)
 
-    drag = []
-    for a in range(6):
-        drag.append(sum(
-            fixed[6 + PAIRS.index((min(a, d), max(a, d)))] * near_motion[d] for d in range(6)
-        ))
-    settled = fixed[0:6] - 6.0 * jnp.stack(drag)
     lanes = -(-width // 128) * 128
-    settled, near_motion = [
-        jnp.pad(part, ((0, 2), (0, lanes - width))) for part in (settled, near_motion)
+    fixed, near_motion = [
+        jnp.pad(part, ((0, -part.shape[0] % 8), (0, lanes - width))) for part in (fixed, near_motion)
     ]
     devices = count_x * count_y
     smem = pl.BlockSpec(memory_space=pltpu.SMEM)
     pressed = pl.pallas_call(
         functools.partial(press_kernel, per_tile=per_tile),
         out_shape=jax.ShapeDtypeStruct((devices, 16, 128), F32),
-        in_specs=[smem, smem] + vmem(6), out_specs=vmem(1)[0],
+        in_specs=[smem, smem] + vmem(7), out_specs=vmem(1)[0],
         scratch_shapes=[
             pltpu.VMEM((64, 128), F32), pltpu.VMEM((9 * 16, per_tile), F32),
             pltpu.VMEM((8, lanes), F32),
         ],
         compiler_params=grant(8), name="press",
     )(
-        row_low, passes, keys, arm0.reshape(lines, 128), arm1.reshape(lines, 128),
-        table, press.reshape(-1, 128), settled,
+        row_low, control, keys, arm0.reshape(lines, 128), arm1.reshape(lines, 128),
+        table, press.reshape(-1, 128), fixed, near_motion,
     )
 
     partials = lax.all_to_all(pressed, ("gx", "gy"), 0, 0)
 
-    home = jnp.stack([lax.axis_index("gx"), lax.axis_index("gy")])
     report, link_out = pl.pallas_call(
         functools.partial(reflect_kernel, per_tile=per_tile, counts=(count_x, count_y)),
         out_shape=(
@@ -794,7 +800,7 @@
         ),
         in_specs=[smem] + vmem(5), out_specs=tuple(vmem(2)), compiler_params=grant(6),
         scratch_shapes=[pltpu.VMEM((len(AROUND), 8, lanes), F32)], name="reflect",
-    )(home, partials, slots, reach, pops, near_motion)
+    )(control, partials, slots, reach, pops, near_motion)
     return potential, report, link_out.reshape(link_pop.shape)
 
 

time: 121 us -> 115 us (0.950)
  blocking collectives: 0 us -> 15.7 us
  waiting for transfers between devices: 10.2 us -> 1.47 us
  starting transfers between devices: 12.3 us -> 6.92 us
  local copies, waits for them, and re-layouts: 6.19 us -> 2.19 us
  Pallas kernels: 64.7 us -> 61.8 us
    all_to_all x0 -> x1, blocking collectives: none -> 15.7 us  [shards(): partials = lax.all_to_all(pressed, ('gx', 'gy'), 0, 0)]
    all_to_all x1 -> x0, waiting for transfers between devices: 9.93 us -> none  [shards(): partials = lax.all_to_all(pressed, ('gx', 'gy'), 0, 0)]
    all_to_all x1 -> x0, starting transfers between devices: 5.3 us -> none  [shards(): partials = lax.all_to_all(pressed, ('gx', 'gy'), 0, 0)]
    unnamed x38 -> x30, local copies, waits for them, and re-layouts: 4.26 us -> 1.59 us
    add x3 -> x0, other arithmetic: 1.81 us -> none  [shards(): sum((fixed[6 + PAIRS.index((min(a, d), max(a, d)))] * near_motion[d] for...]
    ppermute x1, waiting for transfers between devices: 0.01 us -> 1.46 us  [shards(): from_right = lax.ppermute(strip(to_left), 'gy', by)]
    pallas_call x1, Pallas kernels: 4.5 us -> 3.06 us  [shards(): pl.pallas_call(functools.partial(reflect_kernel, per_tile=per_tile, count...]
    pallas_call x1, Pallas kernels: 9.53 us -> 8.09 us  [shards(): pl.pallas_call(functools.partial(press_kernel, per_tile=per_tile), out_sh...]
  transfers between devices with their start and end apart: 5 -> 4, of which waited for: 2 -> 1; matrix products, arithmetic and copies ran while one was open for 16% -> 16% of each run, Pallas kernels for 10% -> 10%
where the time goes in v8:
time: 115 us; the launch traced here: 114 us
  Pallas kernels  61.8 us (54%)
  other arithmetic  24.9 us (22%)
  blocking collectives  15.7 us (14%)
  starting transfers between devices  6.92 us (6%)
  local copies, waits for them, and re-layouts  2.19 us (2%)
  waiting for transfers between devices  1.47 us (1%)
    pallas_call x1, Pallas kernels, shards(): pl.pallas_call(relax_kernel, out_shape=(jax.ShapeDtypeStruct((depth, wide...  30.4 us
    sort x1, other arithmetic, shards(): lax.sort((key.reshape(-1), *(part.reshape(-1) for part in pack_arms(rb)))...  15.9 us
    all_to_all x1, blocking collectives, shards(): partials = lax.all_to_all(pressed, ('gx', 'gy'), 0, 0)  15.7 us
    pallas_call x1, Pallas kernels, shards(): pl.pallas_call(functools.partial(fixed_kernel, width=width), out_shape=(j...  11.9 us
    pallas_call x1, Pallas kernels, shards(): pl.pallas_call(pack_kernel, out_shape=(jax.ShapeDtypeStruct((6, layers +...  8.37 us
    pallas_call x1, Pallas kernels, shards(): pl.pallas_call(functools.partial(press_kernel, per_tile=per_tile), out_sh...  8.09 us
    pallas_call x1, Pallas kernels, shards(): pl.pallas_call(functools.partial(reflect_kernel, per_tile=per_tile, count...  3.06 us
    ppermute x1, starting transfers between devices, shards(): from_right = lax.ppermute(strip(to_left), 'gy', by)  3.04 us
  transfers between devices with their start and end apart: 4, of which 1 were waited for; matrix products, arithmetic and copies ran while one was open for 16% of the time, Pallas kernels for 10%

profile of v8, /device:TPU:1, one launch (start us, length us, event | category | flops | bytes accessed | tf_op | source)
XLA Modules:
  0.0 114.1 jit_solution(4168367244700865282)
XLA Ops:
  0.6 1.3 %fusion.2 = (f16[1,48,12,128]{3,2,1,0:T(8,128)(2,1)S(1)}, f16[1,48,12,128]{3,2,1,0:T(8,128)(2,1)S(1)}) fusion(f32[48,64,128]{2,1,0:T(8,128)} %pot.1), kind=kLoop, calls=%fused_computation.21 | loop fusion | flops 294912 | bytes 884736 | tf_op jit(solution)/shard_map/stack | solution.py:663
  1.9 1.2 %fusion.3 = (f16[1,48,12,128]{3,2,1,0:T(8,128)(2,1)S(1)}, f16[1,48,12,128]{3,2,1,0:T(8,128)(2,1)S(1)}) fusion(f32[48,64,128]{2,1,0:T(8,128)} %charge.1), kind=kLoop, calls=%fused_computation.22 | loop fusion | flops 294912 | bytes 884736 | tf_op jit(solution)/shard_map/stack | solution.py:663
  3.3 0.4 maximum_bitcast_fusion
  4.1 0.3 copy-done.10
  4.7 2.7 %collective-permute-start = (f16[37,48,128]{2,1,0:T(8,128)(2,1)S(1)}, f16[37,48,128]{2,1,0:T(8,128)(2,1)S(1)}, u32[]{:S(2)}, u32[]{:S(2)}) collective-permute-start(f16[37,48,128]{2,1,0:T(8,128)(2,1)S(1)} %get-tuple-element.58), channel_id=1, source_target_pairs={{0,8},{8,16},{16,24},{24,0},{1,9},{9,17},{17,25},{25,1},{2,10},{10... | collective-permute-start | bytes 1363976 | tf_op jit(solution)/shard_map/ppermute | solution.py:671
  7.4 0.6 shift-right-arithmetic_or_fusion
  8.2 0.4 fusion.17
  8.6 15.9 %sort.21 = (s32[32768]{0:T(1024)S(1)}, s32[32768]{0:T(1024)S(1)}, s32[32768]{0:T(1024)S(1)}) sort(s32[32768]{0:T(1024)S(1)} %fusion.17, s32[32768]{0:T(1024)S(1)} %bitcast.79, s32[32768]{0:T(1024)S(1)} %bitcast.78), dimensions={0}, to_apply=%region_0.1 | sort | flops 491520 | bytes 786432 | tf_op jit(solution)/shard_map/sort | solution.py:691
  24.5 0.4 fusion.28.slots
  24.9 1.2 %convert_multiply_fusion = (f32[37,48,128]{2,1,0:T(8,128)S(1)}, f32[37,48,128]{2,1,0:T(8,128)S(1)}) fusion(f16[37,48,128]{2,1,0:T(8,128)(2,1)} %collective-permute-done.1, f32[37]{0:T(128)S(1)} %copy-done.14, f16[37,48,128]{2,1,0:T(8,128)(2,1)S(1)} %collective-permute-done), kind=kLoop, calls=%fused_computation | loop fusion | flops 909312 | bytes 2728084 | tf_op jit(solution)/shard_map/mul | solution.py:621
  26.2 0.9 copy-done.5
  27.1 0.3 copy-done.4
  27.4 8.4 %pack.1 = (f32[6,25,96,128]{3,2,1,0:T(8,128)}, f32[3,5,88,128]{3,2,1,0:T(8,128)S(1)}, f32[3,5,88,128]{3,2,1,0:T(8,128)S(1)}) custom-call(f32[48,64,128]{2,1,0:T(8,128)} %pot.1, f32[48,64,128]{2,1,0:T(8,128)} %charge.1, bf16[48,64,128]{2,1,0:T(8,128)(2,1)} %eps.1, f32[1776,128]{1,0:T(8,128)} %bitcast.73, f32[1776,128]{1,0:T(8,128)} %bitcast.72), custom_call_target="tpu_custom_call" | custom-call | tf_op jit(solution)/shard_map/pack/pallas_call | solution.py:707
  35.9 0.2 multiply_convert_fusion
  36.1 1.0 pad_maximum_fusion.2
  37.2 1.2 %collective-permute-start.2 = (f16[16,88,128]{2,1,0:T(8,128)(2,1)}, f16[16,88,128]{2,1,0:T(8,128)(2,1)S(1)}, u32[]{:S(2)}, u32[]{:S(2)}) collective-permute-start(f16[16,88,128]{2,1,0:T(8,128)(2,1)} %get-tuple-element.29), channel_id=1, source_target_pairs={{0,1},{1,2},{2,3},{3,4},{4,5},{5,6},{6,7},{7,0},{8,9},{9,10},{10,1... | collective-permute-start | bytes 1081352 | tf_op jit(solution)/shard_map/ppermute | solution.py:732
  38.4 3.0 %collective-permute-start.3 = (f16[16,88,128]{2,1,0:T(8,128)(2,1)}, f16[16,88,128]{2,1,0:T(8,128)(2,1)}, u32[]{:S(2)}, u32[]{:S(2)}) collective-permute-start(f16[16,88,128]{2,1,0:T(8,128)(2,1)} %get-tuple-element.51), channel_id=1, source_target_pairs={{1,0},{2,1},{3,2},{4,3},{5,4},{6,5},{7,6},{0,7},{9,8},{10,9},{11,1... | collective-permute-start | bytes 1081352 | tf_op jit(solution)/shard_map/ppermute | solution.py:733
  42.0 11.9 %fixed.1 = (f32[32,288]{1,0:T(8,128)S(1)}, f32[6,256,128]{2,1,0:T(8,128)S(1)}) custom-call(s32[256,128]{1,0:T(8,128)S(1)} %fusion.28.slots, s32[256,128]{1,0:T(8,128)S(1)} %bitcast.71, f32[256,128]{1,0:T(8,128)S(1)} %bitcast.66, f32[3,256,128]{2,1,0:T(8,128)S(1)} %bitcast.65, f32[4,8,128]{2,1,0:T(8,128)S(1)} %copy-done.3), custom_call_target="tpu_custom_call" | custom-call | flops 1000000000 | bytes 20000000 | tf_op jit(solution)/shard_map/fixed/pallas_call | solution.py:741
  54.0 1.5 %collective-permute-done.3 = f16[16,88,128]{2,1,0:T(8,128)(2,1)} collective-permute-done((f16[16,88,128]{2,1,0:T(8,128)(2,1)}, f16[16,88,128]{2,1,0:T(8,128)(2,1)}, u32[]{:S(2)}, u32[]{:S(2)}) %collective-permute-start.3) | collective-permute-done | bytes 360480 | tf_op jit(solution)/shard_map/ppermute | solution.py:733
  55.5 1.2 %convert_multiply_fusion.2 = (f32[16,88,128]{2,1,0:T(8,128)S(1)}, f32[16,88,128]{2,1,0:T(8,128)S(1)}) fusion(f16[16,88,128]{2,1,0:T(8,128)(2,1)} %collective-permute-done.3, f32[16]{0:T(128)S(1)} %copy-done.12, f16[16,88,128]{2,1,0:T(8,128)(2,1)S(1)} %collective-permute-done.2), kind=kLoop, calls=%fused_computation.2 | loop fusion | flops 720896 | bytes 2162752 | tf_op jit(solution)/shard_map/mul | solution.py:621
  56.9 30.4 %relax.1 = (f32[48,64,128]{2,1,0:T(8,128)}, f32[49,64,128]{2,1,0:T(8,128)S(1)}) custom-call(f32[6,25,96,128]{3,2,1,0:T(8,128)} %get-tuple-element.27.kept, f32[16,88,128]{2,1,0:T(8,128)S(1)} %get-tuple-element.63.from_left, f32[16,88,128]{2,1,0:T(8,128)S(1)} %get-tuple-element.62.from_right), custom_call_target="tpu_custom_call" | custom-call | tf_op jit(solution)/shard_map/relax/pallas_call | solution.py:753
  87.2 8.1 %press.1 = f32[32,16,128]{2,1,0:T(8,128)S(1)} custom-call(s32[256]{0:T(256)S(1)} %fusion.33.low, s32[6]{0:T(128)S(1)} %pad_add_fusion.passes.control, s32[256,128]{1,0:T(8,128)S(1)} %bitcast.64, s32[256,128]{1,0:T(8,128)S(1)} %bitcast.68, s32[256,128]{1,0:T(8,128)S(1)} %bitcast.69, f32[4,8,128]{2,1,0:T(8,128)S(1)} %copy-done.3, f32[3136,128]{1,0:T(8,128)S(1)} %bitcast.63, ...), custom_call_target="tpu_custom_call" | custom-call | tf_op jit(solution)/shard_map/press/pallas_call | solution.py:780
  95.3 15.7 %all_to_all.5.partial_sums = f32[32,16,128]{2,1,0:T(8,128)S(1)} all-to-all(f32[32,16,128]{2,1,0:T(8,128)S(1)} %press.1), channel_id=1, replica_groups=mesh['gx'=4,'gy'=8] {'gx','gy'}, dimensions={0} | all-to-all | bytes 524288 | tf_op jit(solution)/shard_map/all_to_all | solution.py:794
  111.1 3.1 %reflect.1 = (f32[6,32]{1,0:T(8,128)}, f32[256,128]{1,0:T(8,128)}) custom-call(s32[6]{0:T(128)S(1)} %pad_add_fusion.passes.control, f32[32,16,128]{2,1,0:T(8,128)S(1)} %all_to_all.5.partial_sums, s32[256,128]{1,0:T(8,128)S(1)} %fusion.28.slots, f32[6,256,128]{2,1,0:T(8,128)S(1)} %get-tuple-element.38.reach, f32[256,128]{1,0:T(8,128)S(1)} %bitcast.67, ...), custom_call_target="tpu_custom_call" | custom-call | tf_op jit(solution)/shard_map/reflect/pallas_call | solution.py:796
  (64 shorter events, 1.8 us)
Async XLA Ops:
  0.6 2.6 %copy-start.6 = (bf16[48,64,128]{2,1,0:T(8,128)(2,1)S(1)}, bf16[48,64,128]{2,1,0:T(8,128)(2,1)}, u32[]{:S(2)}) copy-start(bf16[48,64,128]{2,1,0:T(8,128)(2,1)} %eps.1) | copy-start | bytes 2359300
  3.7 0.7 copy-start.10
  3.7 0.7 copy-start.11
  3.9 3.5 %copy-start = (f32[3,1,1,32768]{3,2,1,0:T(1,128)S(1)}, f32[3,1,1,32768]{3,2,1,0:T(1,128)}, u32[]{:S(2)}) copy-start(f32[3,1,1,32768]{3,2,1,0:T(1,128)} %param.28) | copy-start | bytes 1179652
  3.9 4.0 %copy-start.8 = (s32[1,1,32768]{2,1,0:T(1,128)S(1)}, s32[1,1,32768]{2,1,0:T(1,128)}, u32[]{:S(2)}) copy-start(s32[1,1,32768]{2,1,0:T(1,128)} %param.25) | copy-start | bytes 393220
  3.9 4.0 %copy-start.9 = (s32[1,1,32768]{2,1,0:T(1,128)S(1)}, s32[1,1,32768]{2,1,0:T(1,128)}, u32[]{:S(2)}) copy-start(s32[1,1,32768]{2,1,0:T(1,128)} %param.26) | copy-start | bytes 393220
  4.4 3.8 %copy-start.2 = (s32[1,1,32768]{2,1,0:T(1,128)S(1)}, s32[1,1,32768]{2,1,0:T(1,128)}, u32[]{:S(2)}) copy-start(s32[1,1,32768]{2,1,0:T(1,128)} %param.23) | copy-start | bytes 393220
  4.4 3.8 %copy-start.7 = (s32[1,1,32768]{2,1,0:T(1,128)S(1)}, s32[1,1,32768]{2,1,0:T(1,128)}, u32[]{:S(2)}) copy-start(s32[1,1,32768]{2,1,0:T(1,128)} %param.24) | copy-start | bytes 393220
  4.7 20.2 %copy-start.14 = (f32[37]{0:T(128)S(1)}, f32[37]{0:T(128)}, u32[]{:S(2)}) copy-start(f32[37]{0:T(128)} %constant.158.clone) | copy-start | bytes 448
  4.7 20.2 %collective-permute-start = (f16[37,48,128]{2,1,0:T(8,128)(2,1)S(1)}, f16[37,48,128]{2,1,0:T(8,128)(2,1)S(1)}, u32[]{:S(2)}, u32[]{:S(2)}) collective-permute-start(f16[37,48,128]{2,1,0:T(8,128)(2,1)S(1)} %get-tuple-element.58), channel_id=1, source_target_pairs={{0,8},{8,16},{16,24},{24,0},{1,9},{9,17},{17,25},{25,1},{2,10},{10... | collective-permute-start | bytes 1363976 | tf_op jit(solution)/shard_map/ppermute | solution.py:671
  7.4 17.5 %collective-permute-start.1 = (f16[37,48,128]{2,1,0:T(8,128)(2,1)S(1)}, f16[37,48,128]{2,1,0:T(8,128)(2,1)}, u32[]{:S(2)}, u32[]{:S(2)}) collective-permute-start(f16[37,48,128]{2,1,0:T(8,128)(2,1)S(1)} %get-tuple-element.57), channel_id=1, source_target_pairs={{8,0},{16,8},{24,16},{0,24},{9,1},{17,9},{25,17},{1,25},{10,2},{18... | collective-permute-start | bytes 1363976 | tf_op jit(solution)/shard_map/ppermute | solution.py:672
  26.2 0.9 copy-start.5
  26.2 1.3 %copy-start.4 = (f32[37,48,128]{2,1,0:T(8,128)}, f32[37,48,128]{2,1,0:T(8,128)S(1)}, u32[]{:S(2)}) copy-start(f32[37,48,128]{2,1,0:T(8,128)S(1)} %get-tuple-element.66) | copy-start | bytes 2727940
  27.4 8.4 %copy-start.13 = (f32[3]{0:T(128)S(1)}, f32[3]{0:T(128)}, u32[]{:S(2)}) copy-start(f32[3]{0:T(128)} %constant.159.clone) | copy-start | bytes 40
  35.9 6.1 %copy-start.1 = (f32[1,1,32768]{2,1,0:T(1,128)S(1)}, f32[1,1,32768]{2,1,0:T(1,128)}, u32[]{:S(2)}) copy-start(f32[1,1,32768]{2,1,0:T(1,128)} %param.27) | copy-start | bytes 393220
  35.9 6.1 %copy-start.3 = (f32[4,8,128]{2,1,0:T(8,128)S(1)}, f32[4,8,128]{2,1,0:T(8,128)}, u32[]{:S(2)}) copy-start(f32[4,8,128]{2,1,0:T(8,128)} %constant.157.clone.table) | copy-start | bytes 49156
  37.2 16.9 %collective-permute-start.2 = (f16[16,88,128]{2,1,0:T(8,128)(2,1)}, f16[16,88,128]{2,1,0:T(8,128)(2,1)S(1)}, u32[]{:S(2)}, u32[]{:S(2)}) collective-permute-start(f16[16,88,128]{2,1,0:T(8,128)(2,1)} %get-tuple-element.29), channel_id=1, source_target_pairs={{0,1},{1,2},{2,3},{3,4},{4,5},{5,6},{6,7},{7,0},{8,9},{9,10},{10,1... | collective-permute-start | bytes 1081352 | tf_op jit(solution)/shard_map/ppermute | solution.py:732
  38.4 17.1 %collective-permute-start.3 = (f16[16,88,128]{2,1,0:T(8,128)(2,1)}, f16[16,88,128]{2,1,0:T(8,128)(2,1)}, u32[]{:S(2)}, u32[]{:S(2)}) collective-permute-start(f16[16,88,128]{2,1,0:T(8,128)(2,1)} %get-tuple-element.51), channel_id=1, source_target_pairs={{1,0},{2,1},{3,2},{4,3},{5,4},{6,5},{7,6},{0,7},{9,8},{10,9},{11,1... | collective-permute-start | bytes 1081352 | tf_op jit(solution)/shard_map/ppermute | solution.py:733
  42.0 13.5 %copy-start.12 = (f32[16]{0:T(128)S(1)}, f32[16]{0:T(128)}, u32[]{:S(2)}) copy-start(f32[16]{0:T(128)} %constant.160.clone) | copy-start | bytes 196

commit v9 on v8

--- a/solution.py
+++ b/solution.py
@@ -452,7 +452,7 @@
 
 
 BATCH = 8
-AHEAD = 4
+AHEAD = 8
 
 
 def press_kernel(
@@ -534,7 +534,7 @@
     lax.fori_loop(0, out.shape[0], replicate, 0)
 
 
-TOGETHER = 4
+TOGETHER = 8
 AROUND = [(ox, oy) for ox in range(-2, 3) for oy in range(-2, 3)]
 
 

time: 115 us -> 113 us (0.983)
  Pallas kernels: 61.8 us -> 60.2 us
    pallas_call x1, Pallas kernels: 8.09 us -> 6.76 us  [shards(): pl.pallas_call(functools.partial(press_kernel, per_tile=per_tile), out_sh...]
  transfers between devices with their start and end apart: 4 -> 4, of which waited for: 1 -> 1; matrix products, arithmetic and copies ran while one was open for 16% -> 16% of each run, Pallas kernels for 10% -> 11%
where the time goes in v9:
time: 113 us; the launch traced here: 112 us
  Pallas kernels  60.2 us (53%)
  other arithmetic  24.9 us (22%)
  blocking collectives  15.7 us (14%)
  starting transfers between devices  6.92 us (6%)
  local copies, waits for them, and re-layouts  2.19 us (2%)
  waiting for transfers between devices  1.47 us (1%)
    pallas_call x1, Pallas kernels, shards(): pl.pallas_call(relax_kernel, out_shape=(jax.ShapeDtypeStruct((depth, wide...  30.4 us
    sort x1, other arithmetic, shards(): lax.sort((key.reshape(-1), *(part.reshape(-1) for part in pack_arms(rb)))...  15.9 us
    all_to_all x1, blocking collectives, shards(): partials = lax.all_to_all(pressed, ('gx', 'gy'), 0, 0)  15.7 us
    pallas_call x1, Pallas kernels, shards(): pl.pallas_call(functools.partial(fixed_kernel, width=width), out_shape=(j...  11.9 us
    pallas_call x1, Pallas kernels, shards(): pl.pallas_call(pack_kernel, out_shape=(jax.ShapeDtypeStruct((6, layers +...  8.37 us
    pallas_call x1, Pallas kernels, shards(): pl.pallas_call(functools.partial(press_kernel, per_tile=per_tile), out_sh...  6.76 us
    ppermute x1, starting transfers between devices, shards(): from_right = lax.ppermute(strip(to_left), 'gy', by)  3.04 us
    pallas_call x1, Pallas kernels, shards(): pl.pallas_call(functools.partial(reflect_kernel, per_tile=per_tile, count...  2.77 us
  transfers between devices with their start and end apart: 4, of which 1 were waited for; matrix products, arithmetic and copies ran while one was open for 16% of the time, Pallas kernels for 11%

profile of v9, /device:TPU:1, one launch (start us, length us, event | category | flops | bytes accessed | tf_op | source)
XLA Modules:
  0.0 112.5 jit_solution(5608379762394867099)
XLA Ops:
  0.6 1.3 %fusion.2 = (f16[1,48,12,128]{3,2,1,0:T(8,128)(2,1)S(1)}, f16[1,48,12,128]{3,2,1,0:T(8,128)(2,1)S(1)}) fusion(f32[48,64,128]{2,1,0:T(8,128)} %pot.1), kind=kLoop, calls=%fused_computation.21 | loop fusion | flops 294912 | bytes 884736 | tf_op jit(solution)/shard_map/stack | solution.py:663
  1.9 1.2 %fusion.3 = (f16[1,48,12,128]{3,2,1,0:T(8,128)(2,1)S(1)}, f16[1,48,12,128]{3,2,1,0:T(8,128)(2,1)S(1)}) fusion(f32[48,64,128]{2,1,0:T(8,128)} %charge.1), kind=kLoop, calls=%fused_computation.22 | loop fusion | flops 294912 | bytes 884736 | tf_op jit(solution)/shard_map/stack | solution.py:663
  3.3 0.4 maximum_bitcast_fusion
  4.1 0.3 copy-done.10
  4.7 2.7 %collective-permute-start = (f16[37,48,128]{2,1,0:T(8,128)(2,1)S(1)}, f16[37,48,128]{2,1,0:T(8,128)(2,1)S(1)}, u32[]{:S(2)}, u32[]{:S(2)}) collective-permute-start(f16[37,48,128]{2,1,0:T(8,128)(2,1)S(1)} %get-tuple-element.58), channel_id=1, source_target_pairs={{0,8},{8,16},{16,24},{24,0},{1,9},{9,17},{17,25},{25,1},{2,10},{10... | collective-permute-start | bytes 1363976 | tf_op jit(solution)/shard_map/ppermute | solution.py:671
  7.4 0.6 shift-right-arithmetic_or_fusion
  8.2 0.4 fusion.17
  8.6 15.9 %sort.21 = (s32[32768]{0:T(1024)S(1)}, s32[32768]{0:T(1024)S(1)}, s32[32768]{0:T(1024)S(1)}) sort(s32[32768]{0:T(1024)S(1)} %fusion.17, s32[32768]{0:T(1024)S(1)} %bitcast.79, s32[32768]{0:T(1024)S(1)} %bitcast.78), dimensions={0}, to_apply=%region_0.1 | sort | flops 491520 | bytes 786432 | tf_op jit(solution)/shard_map/sort | solution.py:691
  24.5 0.4 fusion.28.slots
  24.9 1.2 %convert_multiply_fusion = (f32[37,48,128]{2,1,0:T(8,128)S(1)}, f32[37,48,128]{2,1,0:T(8,128)S(1)}) fusion(f16[37,48,128]{2,1,0:T(8,128)(2,1)} %collective-permute-done.1, f32[37]{0:T(128)S(1)} %copy-done.14, f16[37,48,128]{2,1,0:T(8,128)(2,1)S(1)} %collective-permute-done), kind=kLoop, calls=%fused_computation | loop fusion | flops 909312 | bytes 2728084 | tf_op jit(solution)/shard_map/mul | solution.py:621
  26.2 0.9 copy-done.5
  27.1 0.3 copy-done.4
  27.4 8.4 %pack.1 = (f32[6,25,96,128]{3,2,1,0:T(8,128)}, f32[3,5,88,128]{3,2,1,0:T(8,128)S(1)}, f32[3,5,88,128]{3,2,1,0:T(8,128)S(1)}) custom-call(f32[48,64,128]{2,1,0:T(8,128)} %pot.1, f32[48,64,128]{2,1,0:T(8,128)} %charge.1, bf16[48,64,128]{2,1,0:T(8,128)(2,1)} %eps.1, f32[1776,128]{1,0:T(8,128)} %bitcast.73, f32[1776,128]{1,0:T(8,128)} %bitcast.72), custom_call_target="tpu_custom_call" | custom-call | tf_op jit(solution)/shard_map/pack/pallas_call | solution.py:707
  35.9 0.2 multiply_convert_fusion
  36.1 1.0 pad_maximum_fusion.2
  37.2 1.2 %collective-permute-start.2 = (f16[16,88,128]{2,1,0:T(8,128)(2,1)}, f16[16,88,128]{2,1,0:T(8,128)(2,1)S(1)}, u32[]{:S(2)}, u32[]{:S(2)}) collective-permute-start(f16[16,88,128]{2,1,0:T(8,128)(2,1)} %get-tuple-element.29), channel_id=1, source_target_pairs={{0,1},{1,2},{2,3},{3,4},{4,5},{5,6},{6,7},{7,0},{8,9},{9,10},{10,1... | collective-permute-start | bytes 1081352 | tf_op jit(solution)/shard_map/ppermute | solution.py:732
  38.4 3.0 %collective-permute-start.3 = (f16[16,88,128]{2,1,0:T(8,128)(2,1)}, f16[16,88,128]{2,1,0:T(8,128)(2,1)}, u32[]{:S(2)}, u32[]{:S(2)}) collective-permute-start(f16[16,88,128]{2,1,0:T(8,128)(2,1)} %get-tuple-element.51), channel_id=1, source_target_pairs={{1,0},{2,1},{3,2},{4,3},{5,4},{6,5},{7,6},{0,7},{9,8},{10,9},{11,1... | collective-permute-start | bytes 1081352 | tf_op jit(solution)/shard_map/ppermute | solution.py:733
  42.0 11.9 %fixed.1 = (f32[32,288]{1,0:T(8,128)S(1)}, f32[6,256,128]{2,1,0:T(8,128)S(1)}) custom-call(s32[256,128]{1,0:T(8,128)S(1)} %fusion.28.slots, s32[256,128]{1,0:T(8,128)S(1)} %bitcast.71, f32[256,128]{1,0:T(8,128)S(1)} %bitcast.66, f32[3,256,128]{2,1,0:T(8,128)S(1)} %bitcast.65, f32[4,8,128]{2,1,0:T(8,128)S(1)} %copy-done.3), custom_call_target="tpu_custom_call" | custom-call | flops 1000000000 | bytes 20000000 | tf_op jit(solution)/shard_map/fixed/pallas_call | solution.py:741
  54.0 1.5 %collective-permute-done.3 = f16[16,88,128]{2,1,0:T(8,128)(2,1)} collective-permute-done((f16[16,88,128]{2,1,0:T(8,128)(2,1)}, f16[16,88,128]{2,1,0:T(8,128)(2,1)}, u32[]{:S(2)}, u32[]{:S(2)}) %collective-permute-start.3) | collective-permute-done | bytes 360480 | tf_op jit(solution)/shard_map/ppermute | solution.py:733
  55.5 1.2 %convert_multiply_fusion.2 = (f32[16,88,128]{2,1,0:T(8,128)S(1)}, f32[16,88,128]{2,1,0:T(8,128)S(1)}) fusion(f16[16,88,128]{2,1,0:T(8,128)(2,1)} %collective-permute-done.3, f32[16]{0:T(128)S(1)} %copy-done.12, f16[16,88,128]{2,1,0:T(8,128)(2,1)S(1)} %collective-permute-done.2), kind=kLoop, calls=%fused_computation.2 | loop fusion | flops 720896 | bytes 2162752 | tf_op jit(solution)/shard_map/mul | solution.py:621
  56.9 30.4 %relax.1 = (f32[48,64,128]{2,1,0:T(8,128)}, f32[49,64,128]{2,1,0:T(8,128)S(1)}) custom-call(f32[6,25,96,128]{3,2,1,0:T(8,128)} %get-tuple-element.27.kept, f32[16,88,128]{2,1,0:T(8,128)S(1)} %get-tuple-element.63.from_left, f32[16,88,128]{2,1,0:T(8,128)S(1)} %get-tuple-element.62.from_right), custom_call_target="tpu_custom_call" | custom-call | tf_op jit(solution)/shard_map/relax/pallas_call | solution.py:753
  87.2 6.8 %press.1 = f32[32,16,128]{2,1,0:T(8,128)S(1)} custom-call(s32[256]{0:T(256)S(1)} %fusion.33.low, s32[6]{0:T(128)S(1)} %pad_add_fusion.passes.control, s32[256,128]{1,0:T(8,128)S(1)} %bitcast.64, s32[256,128]{1,0:T(8,128)S(1)} %bitcast.68, s32[256,128]{1,0:T(8,128)S(1)} %bitcast.69, f32[4,8,128]{2,1,0:T(8,128)S(1)} %copy-done.3, f32[3136,128]{1,0:T(8,128)S(1)} %bitcast.63, ...), custom_call_target="tpu_custom_call" | custom-call | tf_op jit(solution)/shard_map/press/pallas_call | solution.py:780
  94.0 15.7 %all_to_all.5.partial_sums = f32[32,16,128]{2,1,0:T(8,128)S(1)} all-to-all(f32[32,16,128]{2,1,0:T(8,128)S(1)} %press.1), channel_id=1, replica_groups=mesh['gx'=4,'gy'=8] {'gx','gy'}, dimensions={0} | all-to-all | bytes 524288 | tf_op jit(solution)/shard_map/all_to_all | solution.py:794
  109.7 2.8 %reflect.1 = (f32[6,32]{1,0:T(8,128)}, f32[256,128]{1,0:T(8,128)}) custom-call(s32[6]{0:T(128)S(1)} %pad_add_fusion.passes.control, f32[32,16,128]{2,1,0:T(8,128)S(1)} %all_to_all.5.partial_sums, s32[256,128]{1,0:T(8,128)S(1)} %fusion.28.slots, f32[6,256,128]{2,1,0:T(8,128)S(1)} %get-tuple-element.38.reach, f32[256,128]{1,0:T(8,128)S(1)} %bitcast.67, ...), custom_call_target="tpu_custom_call" | custom-call | tf_op jit(solution)/shard_map/reflect/pallas_call | solution.py:796
  (64 shorter events, 1.8 us)
Async XLA Ops:
  0.6 2.6 %copy-start.6 = (bf16[48,64,128]{2,1,0:T(8,128)(2,1)S(1)}, bf16[48,64,128]{2,1,0:T(8,128)(2,1)}, u32[]{:S(2)}) copy-start(bf16[48,64,128]{2,1,0:T(8,128)(2,1)} %eps.1) | copy-start | bytes 2359300
  3.7 0.7 copy-start.10
  3.7 0.7 copy-start.11
  3.9 3.5 %copy-start = (f32[3,1,1,32768]{3,2,1,0:T(1,128)S(1)}, f32[3,1,1,32768]{3,2,1,0:T(1,128)}, u32[]{:S(2)}) copy-start(f32[3,1,1,32768]{3,2,1,0:T(1,128)} %param.28) | copy-start | bytes 1179652
  3.9 4.0 %copy-start.8 = (s32[1,1,32768]{2,1,0:T(1,128)S(1)}, s32[1,1,32768]{2,1,0:T(1,128)}, u32[]{:S(2)}) copy-start(s32[1,1,32768]{2,1,0:T(1,128)} %param.25) | copy-start | bytes 393220
  3.9 4.0 %copy-start.9 = (s32[1,1,32768]{2,1,0:T(1,128)S(1)}, s32[1,1,32768]{2,1,0:T(1,128)}, u32[]{:S(2)}) copy-start(s32[1,1,32768]{2,1,0:T(1,128)} %param.26) | copy-start | bytes 393220
  4.4 3.8 %copy-start.2 = (s32[1,1,32768]{2,1,0:T(1,128)S(1)}, s32[1,1,32768]{2,1,0:T(1,128)}, u32[]{:S(2)}) copy-start(s32[1,1,32768]{2,1,0:T(1,128)} %param.23) | copy-start | bytes 393220
  4.4 3.8 %copy-start.7 = (s32[1,1,32768]{2,1,0:T(1,128)S(1)}, s32[1,1,32768]{2,1,0:T(1,128)}, u32[]{:S(2)}) copy-start(s32[1,1,32768]{2,1,0:T(1,128)} %param.24) | copy-start | bytes 393220
  4.7 20.2 %copy-start.14 = (f32[37]{0:T(128)S(1)}, f32[37]{0:T(128)}, u32[]{:S(2)}) copy-start(f32[37]{0:T(128)} %constant.156.clone) | copy-start | bytes 448
  4.7 20.2 %collective-permute-start = (f16[37,48,128]{2,1,0:T(8,128)(2,1)S(1)}, f16[37,48,128]{2,1,0:T(8,128)(2,1)S(1)}, u32[]{:S(2)}, u32[]{:S(2)}) collective-permute-start(f16[37,48,128]{2,1,0:T(8,128)(2,1)S(1)} %get-tuple-element.58), channel_id=1, source_target_pairs={{0,8},{8,16},{16,24},{24,0},{1,9},{9,17},{17,25},{25,1},{2,10},{10... | collective-permute-start | bytes 1363976 | tf_op jit(solution)/shard_map/ppermute | solution.py:671
  7.4 17.5 %collective-permute-start.1 = (f16[37,48,128]{2,1,0:T(8,128)(2,1)S(1)}, f16[37,48,128]{2,1,0:T(8,128)(2,1)}, u32[]{:S(2)}, u32[]{:S(2)}) collective-permute-start(f16[37,48,128]{2,1,0:T(8,128)(2,1)S(1)} %get-tuple-element.57), channel_id=1, source_target_pairs={{8,0},{16,8},{24,16},{0,24},{9,1},{17,9},{25,17},{1,25},{10,2},{18... | collective-permute-start | bytes 1363976 | tf_op jit(solution)/shard_map/ppermute | solution.py:672
  26.2 0.9 copy-start.5
  26.2 1.3 %copy-start.4 = (f32[37,48,128]{2,1,0:T(8,128)}, f32[37,48,128]{2,1,0:T(8,128)S(1)}, u32[]{:S(2)}) copy-start(f32[37,48,128]{2,1,0:T(8,128)S(1)} %get-tuple-element.66) | copy-start | bytes 2727940
  27.4 8.4 %copy-start.13 = (f32[3]{0:T(128)S(1)}, f32[3]{0:T(128)}, u32[]{:S(2)}) copy-start(f32[3]{0:T(128)} %constant.157.clone) | copy-start | bytes 40
  35.9 6.1 %copy-start.1 = (f32[1,1,32768]{2,1,0:T(1,128)S(1)}, f32[1,1,32768]{2,1,0:T(1,128)}, u32[]{:S(2)}) copy-start(f32[1,1,32768]{2,1,0:T(1,128)} %param.27) | copy-start | bytes 393220
  35.9 6.1 %copy-start.3 = (f32[4,8,128]{2,1,0:T(8,128)S(1)}, f32[4,8,128]{2,1,0:T(8,128)}, u32[]{:S(2)}) copy-start(f32[4,8,128]{2,1,0:T(8,128)} %constant.155.clone.table) | copy-start | bytes 49156
  37.2 16.9 %collective-permute-start.2 = (f16[16,88,128]{2,1,0:T(8,128)(2,1)}, f16[16,88,128]{2,1,0:T(8,128)(2,1)S(1)}, u32[]{:S(2)}, u32[]{:S(2)}) collective-permute-start(f16[16,88,128]{2,1,0:T(8,128)(2,1)} %get-tuple-element.29), channel_id=1, source_target_pairs={{0,1},{1,2},{2,3},{3,4},{4,5},{5,6},{6,7},{7,0},{8,9},{9,10},{10,1... | collective-permute-start | bytes 1081352 | tf_op jit(solution)/shard_map/ppermute | solution.py:732
  38.4 17.1 %collective-permute-start.3 = (f16[16,88,128]{2,1,0:T(8,128)(2,1)}, f16[16,88,128]{2,1,0:T(8,128)(2,1)}, u32[]{:S(2)}, u32[]{:S(2)}) collective-permute-start(f16[16,88,128]{2,1,0:T(8,128)(2,1)} %get-tuple-element.51), channel_id=1, source_target_pairs={{1,0},{2,1},{3,2},{4,3},{5,4},{6,5},{7,6},{0,7},{9,8},{10,9},{11,1... | collective-permute-start | bytes 1081352 | tf_op jit(solution)/shard_map/ppermute | solution.py:733
  42.0 13.5 %copy-start.12 = (f32[16]{0:T(128)S(1)}, f32[16]{0:T(128)}, u32[]{:S(2)}) copy-start(f32[16]{0:T(128)} %constant.158.clone) | copy-start | bytes 196
